TPU v7x, 32 devices: a whole 2x2x4 slice. The times are simulated.
32 devices in a mesh: group: 2 (over x), replica: 16 (over z, y, core).
Axes of the slice: x: 2, y: 2, z: 4, core: 2. Of those that a mesh axis runs over, the one named last changes fastest.
Arguments:
- block_in: bfloat16 [16, 1024, 1024], P('replica', 'group'), may hold values from -6 to 6
- attn_gain: bfloat16 [1024], P('group'), may hold values from 0.5 to 1.5
- query_weight: bfloat16 [1024, 1024], P('group'), may hold values from -0.25 to 0.25
- key_weight: bfloat16 [1024, 512], P('group'), may hold values from -0.25 to 0.25
- value_weight: bfloat16 [1024, 512], P('group'), may hold values from -0.1875 to 0.1875
- out_weight: bfloat16 [1024, 1024], P('group'), may hold values from -1.5 to 1.5
- ffn_gain: bfloat16 [1024], P('group'), may hold values from 0.5 to 1.5
- router_weight: bfloat16 [1024, 16], P('group'), may hold values from -0.09375 to 0.09375
- expert_in: bfloat16 [16, 1024, 1024], P('group'), may hold values from -0.1875 to 0.1875
- expert_out: bfloat16 [16, 1024, 512], P('group'), may hold values from -1.5 to 1.5
- routes: int32 [16, 1024, 8], P('replica', 'group'), may hold values from 0 to 15, all different within a row; in each aligned block of 512 rows (0 to 511, 512 to 1023, ..., all dimensions but the last counted through in order) at most 384 rows name the same one
- prefix: int32 [16], P('replica'), may hold values from 102 to 512, as said below
- cotangent: bfloat16 [16, 1024, 1024], P('replica', 'group'), may hold values from -6 to 6
Outputs:
- block_out: bfloat16 [16, 1024, 1024], P('replica', 'group')
- input_grad: float32 [16, 1024, 1024], P('replica', 'group')
- attn_gain_grad: float32 [1024], P(('group', 'replica'))
- query_grad: float32 [1024, 1024], P(('group', 'replica'))
- key_grad: float32 [1024, 512], P(('group', 'replica'))
- value_grad: float32 [1024, 512], P(('group', 'replica'))
- out_grad: float32 [1024, 1024], P(None, ('group', 'replica'))
- ffn_gain_grad: float32 [1024], P(('group', 'replica'))
- router_grad: float32 [1024, 16], P(('group', 'replica'))
- expert_in_grad: float32 [16, 1024, 1024], P(None, ('group', 'replica'))
- expert_out_grad: float32 [16, 1024, 512], P(None, ('group', 'replica'))
Inputs may be any that keep to these rules, and one draw needn't show every extreme that they name: `routes`: each token names 8 different experts. Among the 512 tokens of one sequence block no expert is named more than 384 times, and in every draw some expert is named exactly 384 times by some block. Some sequence has a prefix of exactly 512.
All inputs are finite; a program needn't handle non-finite values.
Results may differ from a plain program's by a relative error of at most 0.017.
The roundings to bfloat16 on the way count: a program that leaves them out, or rounds other values in their place, can miss the bound.
Values may be sent and summed in bfloat16 or wider, within the bound.
No kernel may reach another device: no remote copies, remote signals or barrier semaphores. Data moves between devices by JAX's collectives and lax.ppermute only.
A program may use at most 448 MiB of HBM per device.

v0:
```python
import math

import jax
import jax.numpy as jnp
from jax import lax
from jax.sharding import PartitionSpec as P

HEADS = 16
KV_HEADS = 8
HEAD = 64
FF = 512
TOP = 8
EXPERTS = 16
CAP = 384


EPSILON = 1e-06
THETA_BASE = 10000.0
MASKED = -1e30
HIGHEST = lax.Precision.HIGHEST


def from_behind(value, axis, steps):
    count = lax.axis_size(axis)
    first, last = (max(0, -steps), min(count, count - steps))
    return lax.ppermute(value, axis, [(source, source + steps) for source in range(first, last)])


def normalize(values, gain):
    return values * lax.rsqrt(jnp.mean(values * values, -1, keepdims=True) + EPSILON) * gain


def rope_tables(positions, head_size):
    half_head = head_size // 2
    frequency = THETA_BASE ** (-jnp.arange(half_head, dtype=jnp.float32) * 2.0 / head_size)
    angles = positions.astype(jnp.float32)[:, None] * frequency[None, :]
    return (jnp.cos(angles)[:, None, :], jnp.sin(angles)[:, None, :])


def rotate(values, cosine, sine_table):
    half_head = values.shape[-1] // 2
    first_half = values[..., :half_head]
    second_half = values[..., half_head:]
    return jnp.concatenate(
        [
            first_half * cosine - second_half * sine_table,
            second_half * cosine + first_half * sine_table,
        ],
        -1,
    )


def rotate_back(gradient, cosine, sine_table):
    half_head = gradient.shape[-1] // 2
    first_half = gradient[..., :half_head]
    second_half = gradient[..., half_head:]
    return jnp.concatenate(
        [
            first_half * cosine + second_half * sine_table,
            second_half * cosine - first_half * sine_table,
        ],
        -1,
    )


def contract_rows(left, right):
    return lax.dot_general(
        left, right, (((0,), (0,)), ((), ())), preferred_element_type=jnp.float32
    )


def contract_cols(left, right):
    return lax.dot_general(
        left, right, (((1,), (1,)), ((), ())), preferred_element_type=jnp.float32
    )


def expert_forward(rows, weight_in, weight_out):
    gate_up = jnp.einsum("ecd,edf->ecf", rows, weight_in, preferred_element_type=jnp.float32)
    hidden = (jax.nn.silu(gate_up[..., :FF]) * gate_up[..., FF:]).astype(jnp.bfloat16)
    outputs = jnp.einsum("ecf,edf->ecd", hidden, weight_out, preferred_element_type=jnp.float32)
    return (gate_up, hidden, outputs)


def expert_backward(rows, gate_up, hidden, grad_rows, weight_in, weight_out):
    grad_hidden = jnp.einsum(
        "ecd,edf->ecf", grad_rows, weight_out, preferred_element_type=jnp.float32
    )
    grad_out_weight = jnp.einsum(
        "ecd,ecf->edf", grad_rows, hidden, preferred_element_type=jnp.float32
    )
    gate_part = gate_up[..., :FF]
    up_part = gate_up[..., FF:]
    sigmoid = jax.nn.sigmoid(gate_part)
    grad_gate = grad_hidden * up_part * sigmoid * (1.0 + gate_part * (1.0 - sigmoid))
    grad_up = grad_hidden * (gate_part * sigmoid)
    grad_gate_up = jnp.concatenate([grad_gate, grad_up], -1).astype(jnp.bfloat16)
    grad_in_weight = jnp.einsum(
        "ecd,ecf->edf", rows, grad_gate_up, preferred_element_type=jnp.float32
    )
    grad_rows_in = jnp.einsum(
        "ecf,edf->ecd", grad_gate_up, weight_in, preferred_element_type=jnp.float32
    )
    return (grad_rows_in, grad_in_weight, grad_out_weight)


def on_device(
    block_in,
    attn_gain,
    query_weight,
    key_weight,
    value_weight,
    out_weight,
    ffn_gain,
    router_weight,
    expert_in,
    expert_out,
    routes,
    prefix,
    cotangent,
):
    tokens = block_in.shape[1]
    width = block_in.shape[2]
    half_index = lax.axis_index("group")
    inputs = block_in[0].astype(jnp.float32)
    token_routes = routes[0]
    prefix_len = prefix[0]
    grad_out = cotangent[0].astype(jnp.float32)
    groups = HEADS // KV_HEADS
    score_scale = 1.0 / math.sqrt(HEAD)
    rows_block = min(tokens, 512)
    block_count = tokens // rows_block
    positions = half_index * tokens + jnp.arange(tokens, dtype=jnp.int32)
    key_positions = jnp.concatenate([positions - tokens, positions])
    cosine, sine_table = rope_tables(positions, HEAD)
    gain_attn, weight_q, weight_k, weight_v, weight_o = (
        lax.all_gather(attn_gain, "group", axis=0, tiled=True),
        lax.all_gather(query_weight, "group", axis=0, tiled=True),
        lax.all_gather(key_weight, "group", axis=0, tiled=True),
        lax.all_gather(value_weight, "group", axis=0, tiled=True),
        lax.all_gather(out_weight, "group", axis=0, tiled=True),
    )
    normed_attn_f, attn_norm_pull = jax.vjp(normalize, inputs, gain_attn.astype(jnp.float32))
    normed_attn = normed_attn_f.astype(jnp.bfloat16)
    query_pre = jnp.dot(normed_attn, weight_q, preferred_element_type=jnp.float32).reshape(
        tokens, HEADS, HEAD
    )
    key_pre = jnp.dot(normed_attn, weight_k, preferred_element_type=jnp.float32).reshape(
        tokens, KV_HEADS, HEAD
    )
    queries = rotate(query_pre, cosine, sine_table).astype(jnp.bfloat16)
    own_keys = rotate(key_pre, cosine, sine_table).astype(jnp.bfloat16)
    own_values = (
        jnp.dot(normed_attn, weight_v, preferred_element_type=jnp.float32)
        .astype(jnp.bfloat16)
        .reshape(tokens, KV_HEADS, HEAD)
    )
    prev_keys, prev_values = from_behind((own_keys, own_values), "group", 1)
    all_keys = jnp.concatenate([prev_keys, own_keys], 0)
    all_values = jnp.concatenate([prev_values, own_values], 0)
    query_blocks = queries.reshape(block_count, rows_block, KV_HEADS, groups, HEAD)
    position_blocks = positions.reshape(block_count, rows_block)

    def masked_scores(query_block, query_pos):
        scores = (
            jnp.einsum("qkgd,jkd->kgqj", query_block, all_keys, preferred_element_type=jnp.float32)
            * score_scale
        )
        visible = (key_positions[None, :] >= 0) & (
            (key_positions[None, :] <= query_pos[:, None]) | (key_positions[None, :] < prefix_len)
        )
        return jnp.where(visible, scores, MASKED)

    def forward_block(operands):
        query_block, query_pos = operands
        scores = masked_scores(query_block, query_pos)
        row_peak = jnp.max(scores, -1, keepdims=True)
        exponent = jnp.exp(scores - row_peak)
        row_total = jnp.sum(exponent, -1, keepdims=True)
        weights_low = (exponent / row_total).astype(jnp.bfloat16)
        attended_block = jnp.einsum(
            "kgqj,jkd->qkgd", weights_low, all_values, preferred_element_type=jnp.float32
        )
        return (attended_block.astype(jnp.bfloat16), row_peak + jnp.log(row_total))

    attended_blocks, log_totals = lax.map(forward_block, (query_blocks, position_blocks))
    attended = attended_blocks.reshape(tokens, HEADS * HEAD)
    residual = inputs + jnp.dot(attended, weight_o, preferred_element_type=jnp.float32)
    gain_ffn, router_full, expert_in_full, expert_out_full = (
        lax.all_gather(ffn_gain, "group", axis=0, tiled=True),
        lax.all_gather(router_weight, "group", axis=0, tiled=True),
        lax.all_gather(expert_in, "group", axis=0, tiled=True),
        lax.all_gather(expert_out, "group", axis=0, tiled=True),
    )
    normed_ffn_f, ffn_norm_pull = jax.vjp(normalize, residual, gain_ffn.astype(jnp.float32))
    normed_ffn = normed_ffn_f.astype(jnp.bfloat16)
    logits = jnp.dot(normed_ffn, router_full, preferred_element_type=jnp.float32)
    gate_probs = jax.nn.softmax(jnp.take_along_axis(logits, token_routes, 1), -1)
    expert_ids = jnp.arange(EXPERTS, dtype=jnp.int32)
    member = (token_routes[:, :, None] == expert_ids[None, None, :]).astype(jnp.int32)
    per_token = jnp.sum(member, 1)
    before = jnp.cumsum(per_token, 0) - per_token
    slot_index = jnp.sum(member * before[:, None, :], 2)
    flat_slot = (token_routes * CAP + slot_index).reshape(-1)
    token_ids = jnp.repeat(jnp.arange(tokens, dtype=jnp.int32), TOP)
    source = jnp.zeros((EXPERTS * CAP,), jnp.int32).at[flat_slot].set(token_ids)
    filled = jnp.zeros((EXPERTS * CAP,), jnp.bfloat16).at[flat_slot].set(1.0)
    gate_rows = jnp.zeros((EXPERTS * CAP,), jnp.float32).at[flat_slot].set(gate_probs.reshape(-1))
    buffer = (normed_ffn[source] * filled[:, None]).reshape(EXPERTS, CAP, width)
    gate_up, hidden, expert_rows = expert_forward(buffer, expert_in_full, expert_out_full)
    picked = expert_rows.reshape(EXPERTS * CAP, width)[flat_slot].reshape(tokens, TOP, width)
    block_out = (residual + jnp.sum(gate_probs[:, :, None] * picked, 1)).astype(jnp.bfloat16)
    grad_gates = jnp.sum(picked * grad_out[:, None, :], 2)
    grad_expert_rows = (
        (grad_out[source] * gate_rows[:, None]).astype(jnp.bfloat16).reshape(EXPERTS, CAP, width)
    )
    back_in, back_out = (
        lax.all_gather(expert_in, "group", axis=0, tiled=True),
        lax.all_gather(expert_out, "group", axis=0, tiled=True),
    )
    grad_buffer, grad_in_weight, grad_out_weight = expert_backward(
        buffer, gate_up, hidden, grad_expert_rows, back_in, back_out
    )
    expert_in_grad, expert_out_grad = (
        lax.psum_scatter(grad_in_weight, ("group", "replica"), scatter_dimension=1, tiled=True),
        lax.psum_scatter(grad_out_weight, ("group", "replica"), scatter_dimension=1, tiled=True),
    )
    grad_from_experts = jnp.sum(
        grad_buffer.reshape(EXPERTS * CAP, width)[flat_slot].reshape(tokens, TOP, width), 1
    )
    mean_term = jnp.sum(gate_probs * grad_gates, 1, keepdims=True)
    grad_chosen = gate_probs * (grad_gates - mean_term)
    grad_logits = jnp.sum(
        grad_chosen[:, :, None]
        * (token_routes[:, :, None] == expert_ids[None, None, :]).astype(jnp.float32),
        1,
    )
    router_f = router_full.astype(jnp.float32)
    router_full_grad = lax.dot_general(
        normed_ffn.astype(jnp.float32), grad_logits, (((0,), (0,)), ((), ())), precision=HIGHEST
    )
    grad_normed_ffn = grad_from_experts + lax.dot_general(
        grad_logits, router_f, (((1,), (1,)), ((), ())), precision=HIGHEST
    )
    grad_res_norm, ffn_gain_full_grad = ffn_norm_pull(grad_normed_ffn)
    grad_residual = grad_out + grad_res_norm
    grad_res_low = grad_residual.astype(jnp.bfloat16)
    out_full_grad = contract_rows(attended, grad_res_low)
    grad_attended = contract_cols(grad_res_low, weight_o).astype(jnp.bfloat16)
    grad_blocks = grad_attended.reshape(block_count, rows_block, KV_HEADS, groups, HEAD)

    def backward_block(running, operands):
        grad_key_sum, grad_value_sum = running
        query_block, query_pos, grad_block, log_total = operands
        scores = masked_scores(query_block, query_pos)
        probability = jnp.exp(scores - log_total)
        grad_probs = jnp.einsum(
            "qkgd,jkd->kgqj", grad_block, all_values, preferred_element_type=jnp.float32
        )
        row_delta = jnp.sum(probability * grad_probs, -1, keepdims=True)
        grad_scores = (probability * (grad_probs - row_delta)).astype(jnp.bfloat16)
        grad_query = (
            jnp.einsum("kgqj,jkd->qkgd", grad_scores, all_keys, preferred_element_type=jnp.float32)
            * score_scale
        )
        grad_key_sum = (
            grad_key_sum
            + jnp.einsum(
                "kgqj,qkgd->jkd", grad_scores, query_block, preferred_element_type=jnp.float32
            )
            * score_scale
        )
        grad_value_sum = grad_value_sum + jnp.einsum(
            "kgqj,qkgd->jkd",
            probability.astype(jnp.bfloat16),
            grad_block,
            preferred_element_type=jnp.float32,
        )
        return ((grad_key_sum, grad_value_sum), grad_query)

    empty_keys = jnp.zeros((2 * tokens, KV_HEADS, HEAD), jnp.float32)
    (grad_keys_all, grad_values_all), grad_query_blocks = lax.scan(
        backward_block,
        (empty_keys, empty_keys),
        (query_blocks, position_blocks, grad_blocks, log_totals),
    )
    back_keys, back_values = (
        from_behind(grad_keys_all[:tokens].astype(jnp.bfloat16), "group", -1).astype(jnp.float32),
        from_behind(grad_values_all[:tokens].astype(jnp.bfloat16), "group", -1).astype(jnp.float32),
    )
    grad_keys = grad_keys_all[tokens:] + back_keys
    grad_values = grad_values_all[tokens:] + back_values
    grad_query_pre = (
        rotate_back(grad_query_blocks.reshape(tokens, HEADS, HEAD), cosine, sine_table)
        .astype(jnp.bfloat16)
        .reshape(tokens, HEADS * HEAD)
    )
    grad_key_pre = (
        rotate_back(grad_keys, cosine, sine_table)
        .astype(jnp.bfloat16)
        .reshape(tokens, KV_HEADS * HEAD)
    )
    grad_value_pre = grad_values.astype(jnp.bfloat16).reshape(tokens, KV_HEADS * HEAD)
    query_full_grad = contract_rows(normed_attn, grad_query_pre)
    key_full_grad = contract_rows(normed_attn, grad_key_pre)
    value_full_grad = contract_rows(normed_attn, grad_value_pre)
    grad_normed_attn = (
        contract_cols(grad_query_pre, weight_q)
        + contract_cols(grad_key_pre, weight_k)
        + contract_cols(grad_value_pre, weight_v)
    )
    grad_in_norm, attn_gain_full_grad = attn_norm_pull(grad_normed_attn)
    input_grad = grad_residual + grad_in_norm
    attn_gain_grad, query_grad, key_grad, value_grad, out_grad, ffn_gain_grad, router_grad = (
        lax.psum_scatter(
            attn_gain_full_grad, ("group", "replica"), scatter_dimension=0, tiled=True
        ),
        lax.psum_scatter(query_full_grad, ("group", "replica"), scatter_dimension=0, tiled=True),
        lax.psum_scatter(key_full_grad, ("group", "replica"), scatter_dimension=0, tiled=True),
        lax.psum_scatter(value_full_grad, ("group", "replica"), scatter_dimension=0, tiled=True),
        lax.psum_scatter(out_full_grad, ("group", "replica"), scatter_dimension=1, tiled=True),
        lax.psum_scatter(ffn_gain_full_grad, ("group", "replica"), scatter_dimension=0, tiled=True),
        lax.psum_scatter(router_full_grad, ("group", "replica"), scatter_dimension=0, tiled=True),
    )
    return (
        block_out[None],
        input_grad[None],
        attn_gain_grad,
        query_grad,
        key_grad,
        value_grad,
        out_grad,
        ffn_gain_grad,
        router_grad,
        expert_in_grad,
        expert_out_grad,
    )


def solution(mesh):
    placed = (
        P("replica", "group", None),
        P("group"),
        P("group", None),
        P("group", None),
        P("group", None),
        P("group", None),
        P("group"),
        P("group", None),
        P("group", None, None),
        P("group", None, None),
        P("replica", "group", None),
        P("replica"),
        P("replica", "group", None),
    )
    return jax.shard_map(
        on_device,
        mesh=mesh,
        in_specs=placed,
        out_specs=(
            P("replica", "group", None),
            P("replica", "group", None),
            P(("group", "replica")),
            P(("group", "replica"), None),
            P(("group", "replica"), None),
            P(("group", "replica"), None),
            P(None, ("group", "replica")),
            P(("group", "replica")),
            P(("group", "replica"), None),
            P(None, ("group", "replica"), None),
            P(None, ("group", "replica"), None),
        ),
        check_vma=False,
    )
```

profile of v0, /device:TPU:28, one launch (start us, length us, event | category | flops | bytes accessed | tf_op | source)
XLA Modules:
  0.0 2652.3 jit_solution(8985328769214327289)
XLA Ops:
  12.5 4.3 all-gather
  16.8 4.4 all-gather.1
  21.8 4.7 all_gather.35
  29.4 28.6 %scatter_custom_fusion.1 = bf16[6144]{0:T(1024)(128)(2,1)S(1)} fusion(s32[4096]{0:T(1024)S(1)} %bitcast.237, bf16[4096]{0:T(1024)(128)(2,1)S(1)} %broadcast.399, bf16[]{:T(256)} %constant.114.clone.1), kind=kCustom, calls=%fused_computation.149 | custom fusion | bytes 12290 | tf_op jit(solution)/shard_map/scatter | solution.py:207
  60.4 15.5 scatter_custom_fusion
  77.4 27.4 %gather_fusion.2 = f32[6144,1024]{1,0:T(8,128)} fusion(f32[512,1024]{1,0:T(8,128)S(1)} %bitcast_convert_fusion, s32[6144]{0:T(1024)S(1)} %fusion.64), kind=kCustom, calls=%fused_computation.2 | custom fusion | bytes 50356224 | tf_op jit(solution)/shard_map/gather | solution.py:215
  104.8 24.7 copy.88
  134.6 4.4 collective-permute-start
  145.2 4.3 copy.76
  153.3 13.4 collective-permute-done.1
  166.7 15.8 fusion.91
  182.5 13.1 fusion.3
  195.7 13.8 fusion.41
  209.6 3.3 multiply_reduce_fusion.2
  214.5 26.8 %gather_fusion = bf16[6144,1024]{1,0:T(8,128)(2,1)} fusion(bf16[512,1024]{1,0:T(8,128)(2,1)S(1)} %multiply_convert_fusion.6, s32[6144]{0:T(1024)S(1)} %fusion.64), kind=kCustom, calls=%fused_computation | custom fusion | bytes 25190400 | tf_op jit(solution)/shard_map/gather | solution.py:209
  242.0 33.0 %gather_fusion.4 = f32[4096]{0:T(1024)S(1)} fusion(f32[512,16]{0,1:T(8,128)S(1)} %fusion.92, s32[4096]{0:T(1024)S(1)} %copy-done.4), kind=kCustom, calls=%fused_computation.4 | custom fusion | bytes 65536 | tf_op jit(solution)/shard_map/jit(take_along_axis)/gather | solution.py:198
  276.3 16.1 scatter_custom_fusion.2
  292.4 15.5 copy.85
  309.4 207.6 %all-gather.17.cloned.1.call-done = bf16[16,1024,1024]{2,1,0:T(8,128)(2,1)} async-done(((bf16[8,1024,1024]{2,1,0:T(8,128)(2,1)}), bf16[16,1024,1024]{2,1,0:T(8,128)(2,1)}) %all-gather.17.cloned.1.call-update) | async-done | bytes 33554448 | tf_op jit(solution)/shard_map/all_gather | solution.py:192
  517.0 30.6 %fusion.14 = f32[16,384,1024]{2,1,0:T(8,128)} fusion(bf16[16,1024,1024]{2,1,0:T(8,128)(2,1)} %all-gather.17.cloned.1.call-done, bf16[16,384,1024]{1,2,0:T(8,128)(2,1)} %copy.85, bf16[16,384]{1,0:T(8,128)(2,1)S(1)} %copy-done.38), kind=kOutput, calls=%fused_computation.36 | convolution fusion | flops 12891193344 | bytes 71315456 | tf_op jit(solution)/shard_map/ecd,edf->ecf/dot_general | solution.py:79
  547.7 171.8 %all-gather.19.cloned.1.call-done = bf16[16,1024,512]{2,1,0:T(8,128)(2,1)} async-done(((bf16[8,1024,512]{2,1,0:T(8,128)(2,1)}), bf16[16,1024,512]{2,1,0:T(8,128)(2,1)}) %all-gather.19.cloned.1.call-update) | async-done | bytes 16777232 | tf_op jit(solution)/shard_map/all_gather | solution.py:193
  719.4 30.4 %multiply_convert_fusion.2 = (bf16[16,384,512]{2,1,0:T(8,128)(2,1)}, bf16[16,384,512]{2,1,0:T(8,128)(2,1)}, bf16[16,384,512]{2,1,0:T(8,128)(2,1)}) fusion(f32[16,384,1024]{2,1,0:T(8,128)} %fusion.14, bf16[16,1024,512]{2,1,0:T(8,128)(2,1)} %all-gather.19.cloned.1.call-done, f32[16,384,1024]{1,2,0:T(8,128)} %copy.88, f32[16,384]{1,0:T(8,128)S(1)} %mul.437), kind=kOutput, calls=%fused_computation.30 | convolution fusion | flops 6502219776 | bytes 86007808 | tf_op jit(solution)/shard_map/ecd,edf->ecf/dot_general | solution.py:86
  749.8 26.2 fusion.16
  776.0 30.5 %gather_fusion.3 = f32[4096,1024]{1,0:T(8,128)} fusion(f32[6144,1024]{1,0:T(8,128)} %bitcast.198, s32[4096]{0:T(1024)S(1)} %copy-done.44), kind=kCustom, calls=%fused_computation.3 | custom fusion | bytes 33570816 | tf_op jit(solution)/shard_map/gather | solution.py:229
  806.5 9.7 bitcast_reduce_fusion
  816.1 22.7 fusion.93
  838.8 30.6 %gather_fusion.1 = f32[4096,1024]{1,0:T(8,128)} fusion(f32[6144,1024]{1,0:T(8,128)} %bitcast.197, s32[4096]{0:T(1024)S(1)} %copy-done.44), kind=kCustom, calls=%fused_computation.1 | custom fusion | bytes 33570816 | tf_op jit(solution)/shard_map/gather | solution.py:211
  869.4 10.8 fusion.8
  884.5 3.9 multiply_reduce_fusion
  893.5 13.3 fusion.38
  908.1 23.0 fusion
  934.9 27.6 %fusion.2 = bf16[8,2,512,1024]{2,3,1,0:T(8,128)(2,1)} fusion(f32[8,1024,512,2]{2,1,3,0:T(8,128)} %get-tuple-element.105, f32[8,2,512,1024]{2,3,1,0:T(8,128)} %get-tuple-element.100, f32[8,2,512]{2,1,0:T(2,128)S(1)} %get-tuple-element.104, f32[8,2,512]{2,1,0:T(2,128)S(1)} %bitcast.222), kind=kLoop, calls=%fused_computation.12 | loop fusion | flops 33554432 | bytes 83951616 | tf_op jit(solution)/shard_map/while/body/eval_jaxpr/convert_element_type | solution.py:261
  962.5 11.3 fusion.37
  975.2 14.1 collective-permute-done.2
  992.9 4.5 fusion.58
  998.3 9.0 convolution_multiply_fusion
  1008.7 3.4 fusion.49
  1012.9 24.6 fusion.19
  1038.2 33.7 %fusion.12 = f32[16,1024,1024]{2,1,0:T(8,128)} fusion(bf16[16,384,1024]{1,2,0:T(8,128)(2,1)} %copy.85, bf16[16,384,512]{2,1,0:T(8,128)(2,1)} %get-tuple-element.71, bf16[16,384,512]{2,1,0:T(8,128)(2,1)} %get-tuple-element.70, bf16[16,384]{1,0:T(8,128)(2,1)S(1)} %copy-done.39), kind=kOutput, calls=%fused_computation.34 | convolution fusion | flops 12916359168 | bytes 92286976 | tf_op jit(solution)/shard_map/ecd,ecf->edf/dot_general | solution.py:98
  1071.9 4.5 fusion.94
  1082.9 39.2 %all-reduce.2 = (f32[1024]{0:T(1024)S(1)}, f32[1024]{0:T(1024)S(1)}) all-reduce(f32[1024]{0:T(1024)S(1)} %get-tuple-element.66, f32[1024]{0:T(1024)S(1)} %copy-done.60), channel_id=2, replica_groups=mesh['group'=2,'replica'=16] {'group','replica'}, use_global_device_ids=true, to_apply=%region_22.23.clone | all-reduce | flops 2048 | bytes 16384
  1123.3 3.4 fusion.36
  1126.8 31.7 %reduce-scatter.14.cloned.1.call-done = f32[32,512]{1,0:T(8,128)} async-done(((f32[1024,512]{1,0:T(8,128)}), f32[32,512]{1,0:T(8,128)}) %reduce-scatter.14.cloned.1.call-update) | async-done | bytes 65552 | tf_op jit(solution)/shard_map/reduce_scatter | solution.py:320
  1158.5 135.9 %reduce-scatter.12.cloned.1.call-done = f32[32,512]{1,0:T(8,128)} async-done(((f32[1024,512]{1,0:T(8,128)}), f32[32,512]{1,0:T(8,128)}) %reduce-scatter.12.cloned.1.call-update) | async-done | bytes 65552 | tf_op jit(solution)/shard_map/reduce_scatter | solution.py:319
  1294.4 140.0 %reduce-scatter.16.cloned.1.call-done = f32[1024,32]{0,1:T(8,128)} async-done(((f32[1024,1024]{0,1:T(8,128)}), f32[1024,32]{0,1:T(8,128)}) %reduce-scatter.16.cloned.1.call-update) | async-done | bytes 131088 | tf_op jit(solution)/shard_map/reduce_scatter | solution.py:321
  1434.4 140.5 %reduce-scatter.10.cloned.1.call-done = f32[32,1024]{1,0:T(8,128)} async-done(((f32[1024,1024]{1,0:T(8,128)}), f32[32,1024]{1,0:T(8,128)}) %reduce-scatter.10.cloned.1.call-update) | async-done | bytes 131088 | tf_op jit(solution)/shard_map/reduce_scatter | solution.py:318
  1574.9 361.5 %reduce-scatter.20.cloned.1.call-done = f32[16,32,512]{2,1,0:T(8,128)} async-done(((f32[16,1024,512]{2,1,0:T(8,128)}), f32[16,32,512]{2,1,0:T(8,128)}) %reduce-scatter.20.cloned.1.call-update) | async-done | bytes 1048592 | tf_op jit(solution)/shard_map/reduce_scatter | solution.py:226
  1936.3 709.0 %reduce-scatter.18.cloned.1.call-done = f32[16,32,1024]{2,1,0:T(8,128)} async-done(((f32[16,1024,1024]{2,1,0:T(8,128)}), f32[16,32,1024]{2,1,0:T(8,128)}) %reduce-scatter.18.cloned.1.call-update) | async-done | bytes 2097168 | tf_op jit(solution)/shard_map/reduce_scatter | solution.py:225
  (247 shorter events, 62.1 us)
Async XLA Ops:
  7.2 124.3 %all-gather.9.cloned.1.call-start = ((), (), s32[]{:S(2)}) async-start(), calls=%async_computation.7 | async-start | bytes 1572864 | tf_op jit(solution)/shard_map/all_gather | solution.py:140
  7.9 131.1 %all-gather.11.cloned.1.call-start = ((), (), s32[]{:S(2)}) async-start(), calls=%async_computation.8 | async-start | bytes 1572864 | tf_op jit(solution)/shard_map/all_gather | solution.py:139
  8.7 136.5 %all-gather.13.cloned.1.call-start = ((), (), s32[]{:S(2)}) async-start(), calls=%async_computation.9 | async-start | bytes 3145728 | tf_op jit(solution)/shard_map/all_gather | solution.py:138
  9.4 200.1 %all-gather.15.cloned.1.call-start = ((), (), s32[]{:S(2)}) async-start(), calls=%async_computation.10 | async-start | bytes 3145728 | tf_op jit(solution)/shard_map/all_gather | solution.py:141
  10.0 507.0 %all-gather.17.cloned.1.call-start = ((), (), s32[]{:S(2)}) async-start(), calls=%async_computation.11 | async-start | bytes 50331648 | tf_op jit(solution)/shard_map/all_gather | solution.py:192
  10.6 6.2 copy-start.62
  10.6 11.2 copy-start.59
  10.6 708.8 %all-gather.19.cloned.1.call-start = ((), (), s32[]{:S(2)}) async-start(), calls=%async_computation.12 | async-start | bytes 25165824 | tf_op jit(solution)/shard_map/all_gather | solution.py:193
  11.2 1065.3 %reduce-scatter.22.cloned.1.call-start = ((), (), s32[]{:S(2)}) async-start(), calls=%async_computation.19 | async-start | bytes 540672
  11.5 64.5 %copy-start.14 = (s32[1,512,8]{2,1,0:T(8,128)}, s32[1,512,8]{2,1,0:T(8,128)S(1)}, u32[]{:S(2)}) copy-start(s32[1,512,8]{2,1,0:T(8,128)S(1)} %copy.78) | copy-start | bytes 49156
  12.4 15.6 copy-start.55
  12.4 137.1 %copy-start.51 = (f32[512]{0:T(512)}, f32[512]{0:T(512)S(1)}, u32[]{:S(2)}) copy-start(f32[512]{0:T(512)S(1)} %fusion.74) | copy-start | bytes 6148
  16.8 132.7 %copy-start.45 = (f32[2,1,512]{2,1,0:T(1,128)}, f32[2,1,512]{2,1,0:T(1,128)S(1)}, u32[]{:S(2)}) copy-start(f32[2,1,512]{2,1,0:T(1,128)S(1)} %convert_element_type.171) | copy-start | bytes 12292
  28.8 47.2 %copy-start.48 = (s32[4096,1]{0,1:T(1,128)}, s32[4096,1]{0,1:T(1,128)S(1)}, u32[]{:S(2)}) copy-start(s32[4096,1]{0,1:T(1,128)S(1)} %compare_select_fusion.1) | copy-start | bytes 49156
  77.4 27.4 %copy-start = (f32[512,1024]{1,0:T(8,128)}, f32[512,1024]{1,0:T(8,128)S(1)}, u32[]{:S(2)}) copy-start(f32[512,1024]{1,0:T(8,128)S(1)} %bitcast_convert_fusion) | copy-start | bytes 6291460
  129.8 23.0 copy-start.28
  129.8 23.0 copy-start.30
  134.6 61.1 %collective-permute-start = (bf16[512,8,64]{0,2,1:T(8,128)(2,1)}, bf16[512,8,64]{0,2,1:T(8,128)(2,1)}, u32[]{:S(2)}, u32[]{:S(2)}) collective-permute-start(bf16[512,8,64]{0,2,1:T(8,128)(2,1)} %bitcast.2), channel_id=1, source_target_pairs={{0,16},{1,17},{2,18},{3,19},{4,20},{5,21},{6,22},{7,23},{8,24},{9,... | collective-permute-start | bytes 1572872 | tf_op jit(solution)/shard_map/ppermute | solution.py:26
  141.9 24.8 copy-start.21
  141.9 24.8 copy-start.23
  142.8 23.8 collective-permute-start.1
  152.9 13.8 copy-start.37
  153.3 29.2 %copy-start.25 = (bf16[512,16,32]{0,2,1:T(8,128)(2,1)}, bf16[512,16,32]{0,2,1:T(8,128)(2,1)S(1)}, u32[]{:S(2)}) copy-start(bf16[512,16,32]{0,2,1:T(8,128)(2,1)S(1)} %get-tuple-element.87) | copy-start | bytes 1572868
  153.3 29.2 %copy-start.26 = (bf16[512,16,32]{0,2,1:T(8,128)(2,1)}, bf16[512,16,32]{0,2,1:T(8,128)(2,1)S(1)}, u32[]{:S(2)}) copy-start(bf16[512,16,32]{0,2,1:T(8,128)(2,1)S(1)} %get-tuple-element.88) | copy-start | bytes 1572868
  209.5 4.7 copy-start.49
  214.5 26.8 %copy-start.2 = (bf16[512,1024]{1,0:T(8,128)(2,1)}, bf16[512,1024]{1,0:T(8,128)(2,1)S(1)}, u32[]{:S(2)}) copy-start(bf16[512,1024]{1,0:T(8,128)(2,1)S(1)} %multiply_convert_fusion.6) | copy-start | bytes 3145732
  214.5 26.8 %copy-start.40 = (bf16[1024,16]{0,1:T(8,128)(2,1)S(1)}, bf16[1024,16]{0,1:T(8,128)(2,1)}, u32[]{:S(2)}) copy-start(bf16[1024,16]{0,1:T(8,128)(2,1)} %all_gather.35) | copy-start | bytes 98308
  242.0 33.2 %copy-start.15 = (s32[1,512,8]{2,1,0:T(8,128)S(1)}, s32[1,512,8]{2,1,0:T(8,128)}, u32[]{:S(2)}) copy-start(s32[1,512,8]{2,1,0:T(8,128)} %copy-done.14) | copy-start | bytes 49156
  292.4 427.0 %copy-start.42 = (f32[16,384]{1,0:T(8,128)}, f32[16,384]{1,0:T(8,128)S(1)}, u32[]{:S(2)}) copy-start(f32[16,384]{1,0:T(8,128)S(1)} %mul.437) | copy-start | bytes 73732
  292.4 224.6 %copy-start.38 = (bf16[16,384]{1,0:T(8,128)(2,1)S(1)}, bf16[16,384]{1,0:T(8,128)(2,1)}, u32[]{:S(2)}) copy-start(bf16[16,384]{1,0:T(8,128)(2,1)} %mul.431) | copy-start | bytes 36868
  749.8 26.2 copy-start.44
  806.5 9.7 copy-start.7
  838.8 30.6 %copy-start.1 = (f32[512,1024]{1,0:T(8,128)S(1)}, f32[512,1024]{1,0:T(8,128)}, u32[]{:S(2)}) copy-start(f32[512,1024]{1,0:T(8,128)} %copy-done) | copy-start | bytes 6291460
  838.8 30.6 %copy-start.19 = (f32[512,8]{1,0:T(8,128)S(1)}, f32[512,8]{1,0:T(8,128)}, u32[]{:S(2)}) copy-start(f32[512,8]{1,0:T(8,128)} %fusion.61) | copy-start | bytes 49156
  869.4 12.9 copy-start.36
  880.3 4.2 copy-start.50
  880.3 4.2 copy-start.54
  893.3 265.2 %reduce-scatter.14.cloned.1.call-start = ((), (), s32[]{:S(2)}) async-start(), calls=%async_computation.15 | async-start | bytes 2162688 | tf_op jit(solution)/shard_map/reduce_scatter | solution.py:320
  906.8 24.3 collective-permute-start.3
  934.8 359.5 %reduce-scatter.12.cloned.1.call-start = ((), (), s32[]{:S(2)}) async-start(), calls=%async_computation.14 | async-start | bytes 2162688 | tf_op jit(solution)/shard_map/reduce_scatter | solution.py:319
  973.8 15.7 copy-start.29
  973.8 15.7 copy-start.31
  973.9 15.4 collective-permute-start.2
  992.8 441.6 %reduce-scatter.16.cloned.1.call-start = ((), (), s32[]{:S(2)}) async-start(), calls=%async_computation.16 | async-start | bytes 4325376 | tf_op jit(solution)/shard_map/reduce_scatter | solution.py:321
  997.4 577.5 %reduce-scatter.10.cloned.1.call-start = ((), (), s32[]{:S(2)}) async-start(), calls=%async_computation.13 | async-start | bytes 4325376 | tf_op jit(solution)/shard_map/reduce_scatter | solution.py:318
  1012.1 924.2 %reduce-scatter.20.cloned.1.call-start = ((), (), s32[]{:S(2)}) async-start(), calls=%async_computation.18 | async-start | bytes 34603008 | tf_op jit(solution)/shard_map/reduce_scatter | solution.py:226
  1037.5 1607.8 %reduce-scatter.18.cloned.1.call-start = ((), (), s32[]{:S(2)}) async-start(), calls=%async_computation.17 | async-start | bytes 69206016 | tf_op jit(solution)/shard_map/reduce_scatter | solution.py:225
  1080.4 43.0 %copy-start.56 = (f32[512]{0:T(512)S(1)}, f32[512]{0:T(512)}, u32[]{:S(2)}) copy-start(f32[512]{0:T(512)} %copy-done.55) | copy-start | bytes 6148
  (32 other events, 62.5 us)
Sparse Core Ops, SparseCore 0:
  9.6 22.5 all-gather.8
  33.7 21.2 all-gather.10
  56.6 33.1 all-gather.12
  91.2 33.1 all-gather.14
  125.7 391.2 all-gather.16
  518.4 200.9 all-gather.18
  893.4 128.8 reduce-scatter.21
  1025.3 133.1 reduce-scatter.13
  1161.3 133.0 reduce-scatter.11
  1297.1 137.1 reduce-scatter.15
  1437.3 137.5 reduce-scatter.9
  1577.7 358.5 reduce-scatter.19
  1939.4 705.8 reduce-scatter.17
where the time goes:
time: 2660 us; the launch traced here: 2650 us
  waiting for transfers between devices  1930 us (73%)
  matrix products  294 us (11%)
  local copies, waits for them, and re-layouts  271 us (10%)
  other arithmetic  78.3 us (3%)
  blocking collectives  52.6 us (2%)
    reduce_scatter x1, waiting for transfers between devices, on_device(): lax.psum_scatter(grad_in_weight, ('group', 'replica'), scatter_dimension=...  709 us
    reduce_scatter x1, waiting for transfers between devices, on_device(): lax.psum_scatter(grad_out_weight, ('group', 'replica'), scatter_dimension...  361 us
    all_gather x1, waiting for transfers between devices, on_device(): lax.all_gather(expert_in, 'group', axis=0, tiled=True)  208 us
    all_gather x1, waiting for transfers between devices, on_device(): lax.all_gather(expert_out, 'group', axis=0, tiled=True)  172 us
    reduce_scatter x1, waiting for transfers between devices, on_device(): lax.psum_scatter(query_full_grad, ('group', 'replica'), scatter_dimension...  141 us
    reduce_scatter x1, waiting for transfers between devices, on_device(): lax.psum_scatter(out_full_grad, ('group', 'replica'), scatter_dimension=1...  140 us
    reduce_scatter x1, waiting for transfers between devices, on_device(): lax.psum_scatter(key_full_grad, ('group', 'replica'), scatter_dimension=0...  136 us
  transfers between devices with their start and end apart: 17, of which 10 were waited for; matrix products, arithmetic and copies ran while one was open for 17% of the time, Pallas kernels for 0%

commit v1 on v0

v1 whole, which is shorter than its diff:
```python
import functools
import math

import jax
import jax.numpy as jnp
import numpy as np
from jax import lax
from jax.experimental import pallas as pl
from jax.experimental.pallas import tpu as pltpu
from jax.sharding import PartitionSpec as P

HEADS = 16
KV_HEADS = 8
HEAD = 64
FF = 512
TOP = 8
EXPERTS = 16

EPSILON = 1e-06
THETA_BASE = 10000.0
MASKED = -1e30
HIGHEST = lax.Precision.HIGHEST
F32 = jnp.float32
BF16 = jnp.bfloat16
MIB = 1 << 20


def nn(left, right):
    return lax.dot_general(left, right, (((1,), (0,)), ((), ())), preferred_element_type=F32)


def nt(left, right):
    return lax.dot_general(left, right, (((1,), (1,)), ((), ())), preferred_element_type=F32)


def params(limit=48, **more):
    return pltpu.CompilerParams(vmem_limit_bytes=limit * MIB, **more)


def whole(shape):
    return pl.BlockSpec(shape, lambda *_: (0,) * len(shape), pipeline_mode=pl.Buffered(1))


SCALAR = pl.BlockSpec(memory_space=pltpu.SMEM)


def half_lanes(ref, which, half):
    return ref[:, pl.ds(pl.multiple_of(which * half, half), half)]


def swap_halves(tile):
    lane = lax.broadcasted_iota(jnp.int32, tile.shape, 1) % HEAD
    return jnp.where(
        lane < HEAD // 2, pltpu.roll(tile, 128 - HEAD // 2, 1), pltpu.roll(tile, HEAD // 2, 1)
    )


def rotated(values, cosine, sine, sign):
    tiles = []
    for start in range(0, values.shape[1], 128):
        tile = values[:, start : start + 128]
        tiles.append(tile * cosine + swap_halves(tile) * (sine * sign))
    return tiles[0] if len(tiles) == 1 else jnp.concatenate(tiles, 1)


def project_kernel(g_ref, x_ref, gain_ref, wq0, wq1, wk0, wk1, wv0, wv1, cos_ref, sin_ref,
                   n_ref, q_ref, k_ref, v_ref):
    half = x_ref.shape[1] // 2
    g = g_ref[0]

    @pl.when(pl.program_id(0) == 0)
    def _():
        x = x_ref[...].astype(F32)
        scale = lax.rsqrt(jnp.mean(x * x, -1, keepdims=True) + EPSILON)
        n_ref[...] = (x * scale * gain_ref[...]).astype(BF16)

    own = half_lanes(n_ref, g, half)
    other = half_lanes(n_ref, 1 - g, half)
    cosine, sine = cos_ref[...], sin_ref[...]
    q = rotated(nn(own, wq0[...]) + nn(other, wq1[...]), cosine, sine, 1.0)
    q_ref[...] = q.astype(BF16) * jnp.asarray(1.0 / math.sqrt(HEAD), BF16)
    k = rotated(nn(own, wk0[...]) + nn(other, wk1[...]), cosine, sine, 1.0)
    k_ref[...] = k.astype(BF16)
    v_ref[...] = (nn(own, wv0[...]) + nn(other, wv1[...])).astype(BF16)


def project(g, x, gain, wq, wk, wv, cosine, sine):
    tokens, width = x.shape
    steps = 4
    qb, kb = wq[0].shape[1] // steps, wk[0].shape[1] // steps
    half = width // 2
    w_spec = lambda n: pl.BlockSpec((half, n), lambda i: (0, i))
    o_spec = lambda n: pl.BlockSpec((tokens, n), lambda i: (0, i))
    return pl.pallas_call(
        project_kernel,
        grid=(steps,),
        in_specs=[SCALAR, whole((tokens, width)), whole((1, width)),
                  w_spec(qb), w_spec(qb), w_spec(kb), w_spec(kb), w_spec(kb), w_spec(kb),
                  whole((tokens, 128)), whole((tokens, 128))],
        out_specs=[pl.BlockSpec((tokens, width), lambda i: (0, 0)), o_spec(qb), o_spec(kb), o_spec(kb)],
        out_shape=[jax.ShapeDtypeStruct((tokens, width), BF16),
                   jax.ShapeDtypeStruct((tokens, wq[0].shape[1]), BF16),
                   jax.ShapeDtypeStruct((tokens, wk[0].shape[1]), BF16),
                   jax.ShapeDtypeStruct((tokens, wv[0].shape[1]), BF16)],
        compiler_params=params(),
        cost_estimate=pl.CostEstimate(flops=2 * tokens * width * 2048, bytes_accessed=8 * MIB, transcendentals=0),
        name="project",
    )(g, x, gain, *wq, *wk, *wv, cosine, sine)


def lane_half(shape, which):
    lane = lax.broadcasted_iota(jnp.int32, shape, 1)
    return ((lane // HEAD) % 2 == which).astype(F32)


def doubled(tile, which):
    kept = tile.astype(F32) * lane_half(tile.shape, which)
    return kept + pltpu.roll(kept, HEAD, 1)


def fill_bias(bias, prefix_ref, g):
    shape = bias.shape
    key = lax.broadcasted_iota(jnp.int32, shape, 0)
    query = lax.broadcasted_iota(jnp.int32, shape, 1)
    seen = (key <= query) | (key + g * shape[0] < prefix_ref[0])
    bias[...] = jnp.where(seen, 0.0, MASKED)


def attend_kernel(g_ref, prefix_ref, q_ref, k0_ref, v0_ref, k1_ref, v1_ref, o_ref, lse_ref, bias):
    g = g_ref[0]
    which = pl.program_id(0) % 2

    @pl.when(pl.program_id(0) == 0)
    def _():
        fill_bias(bias, prefix_ref, g)

    def run(blocks):
        q = q_ref[...].astype(F32)
        keys = [doubled(k[...], which).astype(BF16) for k, _ in blocks]
        values = [doubled(v[...], which).T[:HEAD].astype(BF16) for _, v in blocks]
        outs = []
        for a in range(2):
            qa = (q * lane_half(q.shape, a)).astype(BF16)
            scores = [nt(k, qa) for k in keys]
            scores[0] = scores[0] + bias[...]
            peak = functools.reduce(jnp.maximum, [jnp.max(s, 0, keepdims=True) for s in scores])
            weights = [jnp.exp(s - peak) for s in scores]
            total = sum(jnp.sum(w, 0, keepdims=True) for w in weights)
            out = sum(nn(v, w.astype(BF16)) for v, w in zip(values, weights))
            outs.append(out * (1.0 / total))
            lse_ref[0, a : a + 1, :] = peak + jnp.log(total)
        o_ref[...] = jnp.concatenate(outs, 0).T.astype(BF16)

    @pl.when(g == 0)
    def _():
        run([(k0_ref, v0_ref)])

    @pl.when(g != 0)
    def _():
        run([(k0_ref, v0_ref), (k1_ref, v1_ref)])


def attend(g, prefix, q, k0, v0, k1, v1):
    tokens = q.shape[0]
    kv = pl.BlockSpec((tokens, 128), lambda i: (0, i // 2))
    qs = pl.BlockSpec((tokens, 128), lambda i: (0, i))
    return pl.pallas_call(
        attend_kernel,
        grid=(KV_HEADS,),
        in_specs=[SCALAR, SCALAR, qs, kv, kv, kv, kv],
        out_specs=[qs, pl.BlockSpec((1, 8, tokens), lambda i: (i, 0, 0))],
        out_shape=[jax.ShapeDtypeStruct(q.shape, BF16), jax.ShapeDtypeStruct((KV_HEADS, 8, tokens), F32)],
        scratch_shapes=[pltpu.VMEM((tokens, tokens), F32)],
        compiler_params=params(),
        cost_estimate=pl.CostEstimate(flops=16 * tokens * tokens * 2 * 256 * 4, bytes_accessed=5 * MIB,
                                      transcendentals=16 * tokens * tokens * 2),
        name="attend",
    )(g, prefix, q, k0, v0, k1, v1)


def attend_back_kernel(g_ref, prefix_ref, q_ref, k0_ref, v0_ref, k1_ref, v1_ref, do_ref, lse_ref,
                       cos_ref, sin_ref, dq_ref, dk0_ref, dv0_ref, dk1_ref, dv1_ref, bias):
    g = g_ref[0]
    which = pl.program_id(0) % 2

    @pl.when(pl.program_id(0) == 0)
    def _():
        fill_bias(bias, prefix_ref, g)

    def run(blocks):
        q = q_ref[...].astype(F32)
        do = do_ref[...].astype(F32)
        keys = [doubled(b[0][...], which) for b in blocks]
        keys_t = [k.T[:HEAD].astype(BF16) for k in keys]
        keys = [k.astype(BF16) for k in keys]
        values = [doubled(b[1][...], which).astype(BF16) for b in blocks]
        dks = [0.0 for _ in blocks]
        dvs = [0.0 for _ in blocks]
        dqs = []
        for a in range(2):
            half = lane_half(q.shape, a)
            qa = (q * half).astype(BF16)
            doa = (do * half).astype(BF16)
            lse = lse_ref[0, a : a + 1, :]
            scores = [nt(k, qa) for k in keys]
            scores[0] = scores[0] + bias[...]
            probs = [jnp.exp(s - lse) for s in scores]
            dps = [nt(v, doa) for v in values]
            delta = sum(jnp.sum(p * dp, 0, keepdims=True) for p, dp in zip(probs, dps))
            dq = 0.0
            for n in range(len(blocks)):
                ds = (probs[n] * (dps[n] - delta)).astype(BF16)
                dvs[n] = dvs[n] + nn(probs[n].astype(BF16), doa)
                dks[n] = dks[n] + nn(ds, qa)
                dq = dq + nn(keys_t[n], ds)
            dqs.append(dq)
        dq = jnp.concatenate(dqs, 0).T * (1.0 / math.sqrt(HEAD))
        dq_ref[...] = rotated(dq, cos_ref[...], sin_ref[...], -1.0).astype(BF16)
        for n, (_, _, dk_ref, dv_ref) in enumerate(blocks):
            for grad, ref in ((dks[n], dk_ref), (dvs[n], dv_ref)):
                both = grad + pltpu.roll(grad, HEAD, 1)
                part = both * lane_half(both.shape, which)

                @pl.when(which == 0)
                def _():
                    ref[...] = part.astype(ref.dtype)

                @pl.when(which != 0)
                def _():
                    ref[...] = (ref[...].astype(F32) + part).astype(ref.dtype)

    own = (k0_ref, v0_ref, dk0_ref, dv0_ref)
    earlier = (k1_ref, v1_ref, dk1_ref, dv1_ref)

    @pl.when(g == 0)
    def _():
        run([own])
        dk1_ref[...] = jnp.zeros_like(dk1_ref)
        dv1_ref[...] = jnp.zeros_like(dv1_ref)

    @pl.when(g != 0)
    def _():
        run([own, earlier])


def attend_back(g, prefix, q, k0, v0, k1, v1, do, lse, cosine, sine):
    tokens = q.shape[0]
    kv = pl.BlockSpec((tokens, 128), lambda i: (0, i // 2))
    qs = pl.BlockSpec((tokens, 128), lambda i: (0, i))
    return pl.pallas_call(
        attend_back_kernel,
        grid=(KV_HEADS,),
        in_specs=[SCALAR, SCALAR, qs, kv, kv, kv, kv, qs,
                  pl.BlockSpec((1, 8, tokens), lambda i: (i, 0, 0)),
                  whole((tokens, 128)), whole((tokens, 128))],
        out_specs=[qs, kv, kv, kv, kv],
        out_shape=[jax.ShapeDtypeStruct(q.shape, BF16),
                   jax.ShapeDtypeStruct(k0.shape, F32), jax.ShapeDtypeStruct(k0.shape, F32),
                   jax.ShapeDtypeStruct(k0.shape, BF16), jax.ShapeDtypeStruct(k0.shape, BF16)],
        scratch_shapes=[pltpu.VMEM((tokens, tokens), F32)],
        compiler_params=params(),
        cost_estimate=pl.CostEstimate(flops=16 * tokens * tokens * 2 * 256 * 10, bytes_accessed=8 * MIB,
                                      transcendentals=16 * tokens * tokens * 2),
        name="attend_back",
    )(g, prefix, q, k0, v0, k1, v1, do, lse, cosine, sine)


def output_kernel(g_ref, a_ref, wo0, wo1, x_ref, gain_ref, res_ref, n_ref):
    half = a_ref.shape[1] // 2
    g = g_ref[0]
    res = x_ref[...].astype(F32) + (
        nn(half_lanes(a_ref, g, half), wo0[...]) + nn(half_lanes(a_ref, 1 - g, half), wo1[...]))
    res_ref[...] = res
    scale = lax.rsqrt(jnp.mean(res * res, -1, keepdims=True) + EPSILON)
    n_ref[...] = (res * scale * gain_ref[...]).astype(BF16)


def output(g, attended, wo, x, gain):
    tokens, width = x.shape
    rows = 256
    row = pl.BlockSpec((rows, width), lambda i: (i, 0))
    return pl.pallas_call(
        output_kernel,
        grid=(tokens // rows,),
        in_specs=[SCALAR, row, whole(wo[0].shape), whole(wo[1].shape), row, whole((1, width))],
        out_specs=[row, row],
        out_shape=[jax.ShapeDtypeStruct((tokens, width), F32), jax.ShapeDtypeStruct((tokens, width), BF16)],
        compiler_params=params(),
        cost_estimate=pl.CostEstimate(flops=2 * tokens * width * width, bytes_accessed=7 * MIB, transcendentals=0),
        name="output",
    )(g, attended, *wo, x, gain)


def gates_of(rows, router_t, member):
    logits = jnp.where(member > 0.0, nt(rows, router_t), MASKED)
    peak = jnp.max(logits, -1, keepdims=True)
    weights = jnp.where(member > 0.0, jnp.exp(logits - peak), 0.0)
    return weights / jnp.sum(weights, -1, keepdims=True)


def experts_kernel(g_ref, x0, x1, xt0, xt1, c0, c1, ct0, ct1, m0, m1, router_ref, win, wout,
                   keep_ref, send_ref, grad0_ref, back_ref, sum0_ref, sum1_ref, p0_ref, gg0_ref,
                   p_scr, gg_scr, hid_scr, dgu_scr, grad1, sum1):
    e = pl.program_id(0)
    last = pl.num_programs(0) - 1
    tokens, width = x0.shape
    column = g_ref[0] * pl.num_programs(0) + e

    @pl.when(e == 0)
    def _():
        router = router_ref[...]
        p_scr[0:tokens] = gates_of(x0[...], router, m0[...])
        p_scr[tokens:] = gates_of(x1[...], router, m1[...])
        p0_ref[...] = p_scr[0:tokens]
        gg_scr[...] = jnp.zeros_like(gg_scr)

    def tile(x_ref, c_ref, grad_ref, sum_ref, base, start, rows):
        at = pl.ds(start, rows)
        to = pl.ds(base + start, rows)
        probs = p_scr[to]
        mine = lax.broadcasted_iota(jnp.int32, probs.shape, 1) == column
        p = jnp.sum(jnp.where(mine, probs, 0.0), 1, keepdims=True)
        gate_up = nn(x_ref[at], win[0])
        back = nn(c_ref[at], wout[0])
        gate, up = gate_up[:, :FF], gate_up[:, FF:]
        sig = 1.0 / (1.0 + jnp.exp(-gate))
        act = gate * sig
        hid = act * up
        gg = jnp.sum(hid * back, 1, keepdims=True)
        gg_scr[to] = jnp.where(mine, gg, gg_scr[to])
        back = back * p
        dgate = back * up * (sig * (1.0 + gate * (1.0 - sig)))
        dup = back * act
        hid_low = (hid * p).astype(BF16)
        dgu = jnp.concatenate([dgate, dup], 1).astype(BF16)
        hid_scr[to] = hid_low
        dgu_scr[to] = dgu
        add = nt(hid_low, wout[0])
        grad = nt(dgu, win[0])

        @pl.when(e == 0)
        def _():
            sum_ref[at] = add
            grad_ref[at] = grad

        @pl.when(e != 0)
        def _():
            sum_ref[at] += add
            grad_ref[at] += grad

    rows = 256

    @pl.loop(0, tokens // rows)
    def _(i):
        tile(x0, c0, grad0_ref, sum0_ref, 0, pl.multiple_of(i * rows, rows), rows)

    @pl.loop(0, tokens // rows)
    def _(i):
        tile(x1, c1, grad1, sum1, tokens, pl.multiple_of(i * rows, rows), rows)

    block = 256
    for out, base in ((keep_ref, 0), (send_ref, width // 2)):

        @pl.loop(0, width // 2 // block)
        def _(i, out=out, base=base):
            at = pl.ds(pl.multiple_of(base + i * block, block), block)
            to = pl.ds(pl.multiple_of(i * block, block), block)
            win_grad = nn(xt0[at], dgu_scr[0:tokens]) + nn(xt1[at], dgu_scr[tokens:])
            out[0, to, 0 : 2 * FF] = win_grad.astype(BF16)
            wout_grad = nn(ct0[at], hid_scr[0:tokens]) + nn(ct1[at], hid_scr[tokens:])
            out[0, to, 2 * FF :] = wout_grad.astype(BF16)

    @pl.when(e == last)
    def _():
        back_ref[:, 0:width] = grad1[...].astype(BF16)
        back_ref[:, width:] = gg_scr[tokens:].astype(BF16)
        sum1_ref[...] = sum1[...].astype(BF16)
        gg0_ref[...] = gg_scr[0:tokens]


def experts(g, x, xt, c, ct, member, router_t, win, wout):
    tokens, width = x[0].shape
    count = win.shape[0]
    cols = 3 * FF
    full = whole((tokens, width))
    full_t = whole((width, tokens))
    small = whole((tokens, EXPERTS))
    shape = jax.ShapeDtypeStruct
    const = lambda s: pl.BlockSpec(s, lambda i: (0, 0))
    half = pl.BlockSpec((1, width // 2, cols), lambda i: (i, 0, 0))
    return pl.pallas_call(
        experts_kernel,
        grid=(count,),
        in_specs=[SCALAR, full, full, full_t, full_t, full, full, full_t, full_t, small, small,
                  whole((EXPERTS, width)),
                  pl.BlockSpec((1, width, 2 * FF), lambda i: (i, 0, 0)),
                  pl.BlockSpec((1, width, FF), lambda i: (i, 0, 0))],
        out_specs=[half, half, const((tokens, width)), const((tokens, width + EXPERTS)),
                   const((tokens, width)), const((tokens, width)), const((tokens, EXPERTS)),
                   const((tokens, EXPERTS))],
        out_shape=[shape((count, width // 2, cols), BF16), shape((count, width // 2, cols), BF16),
                   shape((tokens, width), F32), shape((tokens, width + EXPERTS), BF16),
                   shape((tokens, width), F32), shape((tokens, width), BF16),
                   shape((tokens, EXPERTS), F32), shape((tokens, EXPERTS), F32)],
        scratch_shapes=[pltpu.VMEM((2 * tokens, EXPERTS), F32), pltpu.VMEM((2 * tokens, EXPERTS), F32),
                        pltpu.VMEM((2 * tokens, FF), BF16), pltpu.VMEM((2 * tokens, 2 * FF), BF16),
                        pltpu.VMEM((tokens, width), F32), pltpu.VMEM((tokens, width), F32)],
        compiler_params=params(60),
        cost_estimate=pl.CostEstimate(flops=2 * tokens * count * width * FF * 18, bytes_accessed=70 * MIB,
                                      transcendentals=2 * tokens * count * FF),
        name="experts",
    )(g, *x, *xt, *c, *ct, *member, router_t, win, wout)


def middle_kernel(g_ref, c_ref, grad_ref, back_ref, gg_ref, p_ref, router_ref, res_ref, gain_ref, wo0, wo1,
                  dres_ref, low_ref, da_ref, dl_ref):
    width = c_ref.shape[1]
    half = width // 2
    g = g_ref[0]
    p = p_ref[...]
    gg = gg_ref[...] + back_ref[:, width:].astype(F32)
    dlogits = p * (gg - jnp.sum(p * gg, 1, keepdims=True))
    dl_ref[...] = dlogits
    grad = grad_ref[...] + back_ref[:, :width].astype(F32) + lax.dot_general(
        dlogits, router_ref[...].astype(F32), (((1,), (0,)), ((), ())), precision=HIGHEST,
        preferred_element_type=F32)
    res = res_ref[...]
    scale = lax.rsqrt(jnp.mean(res * res, -1, keepdims=True) + EPSILON)
    w = grad * gain_ref[...]
    dres = c_ref[...].astype(F32) + (scale * w - res * (scale * scale * scale)
                                     * jnp.mean(w * res, -1, keepdims=True))
    dres_ref[...] = dres
    low = dres.astype(BF16)
    low_ref[...] = low
    da_ref[:, pl.ds(pl.multiple_of(g * half, half), half)] = nt(low, wo0[...]).astype(BF16)
    da_ref[:, pl.ds(pl.multiple_of((1 - g) * half, half), half)] = nt(low, wo1[...]).astype(BF16)


def middle(g, c, grad, back, gg, p, router_t, res, gain, wo):
    tokens, width = c.shape
    rows = 256
    row = lambda n: pl.BlockSpec((rows, n), lambda i: (i, 0))
    shape = jax.ShapeDtypeStruct
    return pl.pallas_call(
        middle_kernel,
        grid=(tokens // rows,),
        in_specs=[SCALAR, row(width), row(width), row(width + EXPERTS), row(EXPERTS), row(EXPERTS),
                  whole((EXPERTS, width)), row(width), whole((1, width)), whole(wo[0].shape), whole(wo[1].shape)],
        out_specs=[row(width), row(width), row(width), row(EXPERTS)],
        out_shape=[shape((tokens, width), F32), shape((tokens, width), BF16), shape((tokens, width), BF16),
                   shape((tokens, EXPERTS), F32)],
        compiler_params=params(),
        cost_estimate=pl.CostEstimate(flops=2 * tokens * width * width, bytes_accessed=14 * MIB, transcendentals=0),
        name="middle",
    )(g, c, grad, back, gg, p, router_t, res, gain, *wo)


def weight_kernel(xt_ref, dq_ref, dk0, dk1, dv0, dv1, cos_ref, sin_ref, keep_ref, send_ref, dk_ref, dv_ref):
    half = keep_ref.shape[0]
    dq = dq_ref[...]
    dk = rotated(dk0[...] + dk1[...].astype(F32), cos_ref[...], sin_ref[...], -1.0).astype(BF16)
    dv = (dv0[...] + dv1[...].astype(F32)).astype(BF16)
    dk_ref[...] = dk
    dv_ref[...] = dv
    qb, kb = dq.shape[1], dk.shape[1]
    for ref, base in ((keep_ref, 0), (send_ref, half)):
        rows = xt_ref[base : base + half]
        ref[:, 0:qb] = nn(rows, dq).astype(BF16)
        ref[:, qb : qb + kb] = nn(rows, dk).astype(BF16)
        ref[:, qb + kb :] = nn(rows, dv).astype(BF16)


def weight_grads(xt, dq, dk, dv, cosine, sine):
    width, tokens = xt.shape
    steps = 4
    qb, kb = dq.shape[1] // steps, dk[0].shape[1] // steps
    col = lambda n: pl.BlockSpec((tokens, n), lambda i: (0, i))
    out = pl.BlockSpec((width // 2, qb + 2 * kb), lambda i: (0, i))
    shape = jax.ShapeDtypeStruct
    total = steps * (qb + 2 * kb)
    return pl.pallas_call(
        weight_kernel,
        grid=(steps,),
        in_specs=[whole((width, tokens)), col(qb), col(kb), col(kb), col(kb), col(kb),
                  whole((tokens, 128)), whole((tokens, 128))],
        out_specs=[out, out, col(kb), col(kb)],
        out_shape=[shape((width // 2, total), BF16), shape((width // 2, total), BF16),
                   shape(dk[0].shape, BF16), shape(dv[0].shape, BF16)],
        compiler_params=params(),
        cost_estimate=pl.CostEstimate(flops=2 * tokens * width * total, bytes_accessed=10 * MIB, transcendentals=0),
        name="weight_grads",
    )(xt, dq, *dk, *dv, cosine, sine)


def input_kernel(g_ref, dq_ref, dk_ref, dv_ref, wq0, wq1, wk0, wk1, wv0, wv1, x_ref, gain_ref, dres_ref,
                 out_ref, grad):
    half = x_ref.shape[1] // 2
    g = g_ref[0]
    dq, dk, dv = dq_ref[...], dk_ref[...], dv_ref[...]
    grad[:, pl.ds(pl.multiple_of(g * half, half), half)] = (
        nt(dq, wq0[...]) + nt(dk, wk0[...]) + nt(dv, wv0[...]))
    grad[:, pl.ds(pl.multiple_of((1 - g) * half, half), half)] = (
        nt(dq, wq1[...]) + nt(dk, wk1[...]) + nt(dv, wv1[...]))
    x = x_ref[...].astype(F32)
    scale = lax.rsqrt(jnp.mean(x * x, -1, keepdims=True) + EPSILON)
    w = grad[...] * gain_ref[...]
    out_ref[...] = dres_ref[...] + (scale * w - x * (scale * scale * scale) * jnp.mean(w * x, -1, keepdims=True))


def input_grads(g, dq, dk, dv, wq, wk, wv, x, gain, dres):
    tokens, width = x.shape
    rows = 256
    row = lambda a: pl.BlockSpec((rows, a.shape[1]), lambda i: (i, 0))
    weights = (*wq, *wk, *wv)
    return pl.pallas_call(
        input_kernel,
        grid=(tokens // rows,),
        in_specs=[SCALAR, row(dq), row(dk), row(dv), *(whole(w.shape) for w in weights), row(x),
                  whole((1, width)), row(dres)],
        out_specs=row(dres),
        out_shape=jax.ShapeDtypeStruct((tokens, width), F32),
        scratch_shapes=[pltpu.VMEM((rows, width), F32)],
        compiler_params=params(),
        cost_estimate=pl.CostEstimate(flops=2 * tokens * width * 2048, bytes_accessed=12 * MIB, transcendentals=0),
        name="input_grads",
    )(g, dq, dk, dv, *weights, x, gain, dres)


def exchange(value, bit):
    if bit == "group":
        return lax.ppermute(value, "group", [(0, 1), (1, 0)])
    count = lax.axis_size("replica")
    return lax.ppermute(value, "replica", [(i, i ^ (1 << bit)) for i in range(count)])


def halving(parts, axes, order):
    axes = list(axes)
    for bit, dim in order:
        at = axes.index(dim)
        take = lambda which: sum(lax.index_in_dim(p, which, at, False).astype(F32) for p in parts)
        received = exchange(take(1).astype(BF16), bit)
        parts = [lax.index_in_dim(p, 0, at, False) for p in parts] + [received]
        axes.pop(at)
    return sum(p.astype(F32) for p in parts)


def on_device(
    block_in, attn_gain, query_weight, key_weight, value_weight, out_weight, ffn_gain, router_weight,
    expert_in, expert_out, routes, prefix, cotangent,
):
    replicas = lax.axis_size("replica")
    bits = replicas.bit_length() - 1
    tokens, width = block_in.shape[1:]
    half = width // 2
    chunk = half // replicas
    group, replica = lax.axis_index("group"), lax.axis_index("replica")
    g = group.astype(jnp.int32).reshape(1)
    x, cot = block_in[0], cotangent[0]
    swap = lambda v: exchange(v, "group")

    def ordered(own, other, axis):
        return jnp.where(group == 0, jnp.concatenate([own, other], axis), jnp.concatenate([other, own], axis))

    wq = (query_weight, swap(query_weight))
    wk = (key_weight, swap(key_weight))
    wv = (value_weight, swap(value_weight))
    expert_ids = jnp.arange(EXPERTS, dtype=jnp.int32)
    member = (routes[0][:, None, :] == expert_ids[None, :, None]).any(-1)
    small = jnp.concatenate(
        [attn_gain[None], ffn_gain[None], router_weight.T, member.astype(BF16).T], 0)
    small_other = swap(small)
    vectors = ordered(small[: 2 + EXPERTS], small_other[: 2 + EXPERTS], 1)
    gain_attn, gain_ffn = vectors[0:1].astype(F32), vectors[1:2].astype(F32)
    router_t = vectors[2:]
    member = (member.astype(F32), small_other[2 + EXPERTS :].T.astype(F32))
    wo_send, cot_send, *_ = lax.optimization_barrier((out_weight, cot, wq[1], wk[1], wv[1]))
    wo = (out_weight, swap(wo_send))
    cots = (cot, swap(cot_send))

    positions = group * tokens + jnp.arange(tokens, dtype=jnp.int32)
    frequency = THETA_BASE ** (-jnp.arange(HEAD // 2, dtype=F32) * 2.0 / HEAD)
    angles = positions.astype(F32)[:, None] * frequency[None, :]
    cosine = jnp.tile(jnp.cos(angles), (1, 4))
    sine = jnp.sin(angles)
    sine = jnp.concatenate([-sine, sine, -sine, sine], 1)

    place = np.arange(width)
    blocks, inner = place // chunk, place % chunk
    reverse = np.zeros_like(blocks)
    for b in range(bits):
        reverse |= ((blocks >> 1 >> (bits - 1 - b)) & 1) << b
    feature = ((jnp.asarray(blocks & 1, jnp.int32) ^ group) * half
               + (jnp.asarray(reverse, jnp.int32) ^ replica) * chunk + jnp.asarray(inner, jnp.int32))
    order = (feature[:, None] == jnp.arange(width, dtype=jnp.int32)[None, :]).astype(BF16)
    reorder = lambda a: nt(order, a).astype(BF16)

    normed_attn, q, k, v = project(g, x, gain_attn, wq, wk, wv, cosine, sine)
    to_later = lambda a: lax.ppermute(a, "group", [(0, 1)])
    to_earlier = lambda a: lax.ppermute(a, "group", [(1, 0)])
    k1, v1 = to_later(k), to_later(v)
    attended, lse = attend(g, prefix, q, k, v, k1, v1)
    residual, normed_ffn = output(g, attended, wo, x, gain_ffn)
    normed = (normed_ffn, swap(normed_ffn))
    normed_t = (reorder(normed[0]), reorder(normed[1]))
    cots_t = (reorder(cots[0]), reorder(cots[1]))
    keep, send, grad_own, back, sum_own, sum_other, gates, gg = experts(
        g, normed, normed_t, cots, cots_t, member, router_t, expert_in, expert_out)

    back = swap(back)
    grad_res, grad_low, grad_att, grad_logits = middle(
        g, cot, grad_own, back, gg, gates, router_t, residual, gain_ffn, wo)
    block_out = (residual + sum_own + swap(sum_other).astype(F32)).astype(BF16)
    dq, dk0, dv0, dk1, dv1 = attend_back(g, prefix, q, k, v, k1, v1, grad_att, lse, cosine, sine)
    dk = (dk0, to_earlier(dk1))
    dv = (dv0, to_earlier(dv1))
    attn_keep, attn_send, dk_low, dv_low = weight_grads(reorder(normed_attn), dq, dk, dv, cosine, sine)
    input_grad = input_grads(g, dq, dk_low, dv_low, wq, wk, wv, x, gain_attn, grad_res)

    dims = [*range(1, bits), "group"]
    shape = (2,) * bits + (chunk,)
    received = exchange(send, 0)
    two = max(1, keep.shape[0] // 4)
    summed = []
    for first in range(0, keep.shape[0], two):
        stages = list(range(1, bits))
        if first + two >= keep.shape[0] and bits > 2:
            stages[0], stages[1] = stages[1], stages[0]
        parts = [p[first : first + two].reshape(two, *shape, 3 * FF) for p in (keep, received)]
        summed.append(halving(parts, ["e", *dims], [(b, b) for b in stages]))
    summed = jnp.concatenate(summed, 0)
    rows = lambda owner: lax.dynamic_slice_in_dim(expert_in, owner * half + replica * chunk, chunk, 1).astype(F32)
    gain_parts = [jnp.sum(summed[:, n, :, : 2 * FF] * rows(owner), (0, 2)) for n, owner in ((0, group), (1, 1 - group))]
    other_experts = swap(summed[:, 1].astype(BF16)).astype(F32)
    gain_other = swap(jnp.broadcast_to(gain_parts[1][:, None], (chunk, 128)))[:, 0]
    expert_grads = ordered(summed[:, 0], other_experts, 0)

    def sum_rows(keep, send, orders):
        received = exchange(send, 0)
        total = keep.shape[1]
        cut = total // 128 // len(orders) * 128
        outs = []
        for n, stages in enumerate(orders):
            first, end = n * cut, total if n == len(orders) - 1 else (n + 1) * cut
            parts = [p[:, first:end].reshape(*shape, end - first) for p in (keep, received)]
            outs.append(halving(parts, dims, [(b, b) for b in stages]))
        return jnp.concatenate(outs, 1)

    later = list(range(1, bits))
    turned = later[1:2] + later[0:1] + later[2:]
    orders = [["group", *later], [*later, "group"], [*turned, "group"]]
    out_t = jnp.concatenate(
        [nn(reorder(grad_low), attended).astype(BF16), nn(normed_t[0], grad_logits.astype(BF16)).astype(BF16)], 1)
    out_sum = sum_rows(out_t[:half], out_t[half:], orders)
    attn_sum = sum_rows(attn_keep, attn_send, orders)

    out_grad = out_sum[:, :width].T
    router_grad = out_sum[:, width:]
    qb, kb = HEADS * HEAD // 4, KV_HEADS * HEAD // 4
    attn_sum = attn_sum.reshape(chunk, 4, qb + 2 * kb)
    query_grad = attn_sum[:, :, :qb].reshape(chunk, -1)
    key_grad = attn_sum[:, :, qb : qb + kb].reshape(chunk, -1)
    value_grad = attn_sum[:, :, qb + kb :].reshape(chunk, -1)

    mine = lambda a: lax.dynamic_slice_in_dim(a, replica * chunk, chunk, 0).astype(F32)
    attn_gain_grad = (
        jnp.sum(mine(query_weight) * query_grad, 1) + jnp.sum(mine(key_weight) * key_grad, 1)
        + jnp.sum(mine(value_weight) * value_grad, 1)) / mine(attn_gain)
    ffn_gain_grad = (
        gain_parts[0] + gain_other + jnp.sum(mine(router_weight) * router_grad, 1)) / mine(ffn_gain)
    return (
        block_out[None], input_grad[None], attn_gain_grad, query_grad, key_grad, value_grad, out_grad,
        ffn_gain_grad, router_grad, expert_grads[:, :, : 2 * FF], expert_grads[:, :, 2 * FF :],
    )


def solution(mesh):
    placed = (
        P("replica", "group", None),
        P("group"),
        P("group", None),
        P("group", None),
        P("group", None),
        P("group", None),
        P("group"),
        P("group", None),
        P("group", None, None),
        P("group", None, None),
        P("replica", "group", None),
        P("replica"),
        P("replica", "group", None),
    )
    both = ("group", "replica")
    return jax.shard_map(
        on_device,
        mesh=mesh,
        in_specs=placed,
        out_specs=(
            P("replica", "group", None),
            P("replica", "group", None),
            P(both),
            P(both, None),
            P(both, None),
            P(both, None),
            P(None, both),
            P(both),
            P(both, None),
            P(None, both, None),
            P(None, both, None),
        ),
        check_vma=False,
    )
```

time: 2660 us -> 701 us (0.26)
  waiting for transfers between devices: 1930 us -> 295 us
  matrix products: 294 us -> 20.4 us
  local copies, waits for them, and re-layouts: 271 us -> 77.5 us
  Pallas kernels: 0 us -> 180 us
  starting transfers between devices: 10.3 us -> 74.5 us
  blocking collectives: 52.6 us -> 0 us
  other arithmetic: 78.3 us -> 45.5 us
    reduce_scatter x6 -> x0, waiting for transfers between devices: 1520 us -> none  [the longest x1 709 us: on_device(): lax.psum_scatter(grad_in_weight, ('group', 'replica'), scatter_dimension=...]
    all_gather x6 -> x0, waiting for transfers between devices: 379 us -> none  [the longest x1 208 us: on_device(): lax.all_gather(expert_in, 'group', axis=0, tiled=True)]
    dot_general x26 -> x7, matrix products: 292 us -> 20.4 us  [the longest x5 16.3 us: nt(): lax.dot_general(left, right, (((1,), (1,)), ((), ())), preferred_element_...]
    ppermute x4 -> x54, waiting for transfers between devices: 27.5 us -> 295 us  [the longest x33 160 us: exchange(): lax.ppermute(value, 'replica', [(i, i ^ 1 << bit) for i in range(count)])]
    gather x10 -> x0, local copies, waits for them, and re-layouts: 190 us -> none  [the longest x2 52.1 us: on_device(): grad_out[source] * gate_rows[:, None]]
    pallas_call x0 -> x8, Pallas kernels: none -> 180 us  [the longest x1 114 us: experts(): pl.pallas_call(experts_kernel, grid=(count,), in_specs=[SCALAR, full, ful...]
    ppermute x4 -> x54, starting transfers between devices: 9.29 us -> 74.5 us  [the longest x33 37.8 us: exchange(): lax.ppermute(value, 'replica', [(i, i ^ 1 << bit) for i in range(count)])]
    scatter x3 -> x0, local copies, waits for them, and re-layouts: 60.2 us -> none  [the longest x1 28.6 us: on_device(): filled = jnp.zeros((EXPERTS * CAP,), jnp.bfloat16).at[flat_slot].set(1.0)]
  transfers between devices with their start and end apart: 17 -> 54, of which waited for: 10 -> 34; matrix products, arithmetic and copies ran while one was open for 17% -> 16% of each run, Pallas kernels for 0% -> 8%
where the time goes in v1:
time: 701 us; the launch traced here: 695 us
  waiting for transfers between devices  295 us (42%)
  Pallas kernels  180 us (26%)
  local copies, waits for them, and re-layouts  77.5 us (11%)
  starting transfers between devices  74.5 us (11%)
  other arithmetic  45.5 us (6%)
  matrix products  20.4 us (3%)
    ppermute x33, waiting for transfers between devices, exchange(): lax.ppermute(value, 'replica', [(i, i ^ 1 << bit) for i in range(count)])  160 us
    pallas_call x1, Pallas kernels, experts(): pl.pallas_call(experts_kernel, grid=(count,), in_specs=[SCALAR, full, ful...  114 us
    ppermute x17, waiting for transfers between devices, exchange(): return lax.ppermute(value, 'group', [(0, 1), (1, 0)])  108 us
    ppermute x33, starting transfers between devices, exchange(): lax.ppermute(value, 'replica', [(i, i ^ 1 << bit) for i in range(count)])  37.8 us
    ppermute x17, starting transfers between devices, exchange(): return lax.ppermute(value, 'group', [(0, 1), (1, 0)])  29 us
    unnamed x138, local copies, waits for them, and re-layouts  27.6 us
    pallas_call x1, Pallas kernels, attend_back(): pl.pallas_call(attend_back_kernel, grid=(KV_HEADS,), in_specs=[SCALAR, SC...  23.9 us
    convert_element_type x32, other arithmetic, halving(): received = exchange(take(1).astype(BF16), bit)  21.4 us
  transfers between devices with their start and end apart: 54, of which 34 were waited for; matrix products, arithmetic and copies ran while one was open for 16% of the time, Pallas kernels for 8%

profile of v1, /device:TPU:28, one launch (start us, length us, event | category | flops | bytes accessed | tf_op | source)
XLA Modules:
  0.0 695.4 jit_solution(9066430727131289844)
XLA Ops:
  10.1 17.8 %collective-permute-done = bf16[34,512]{1,0:T(8,128)(2,1)S(1)} collective-permute-done((bf16[34,512]{1,0:T(8,128)(2,1)S(1)}, bf16[34,512]{1,0:T(8,128)(2,1)S(1)}, u32[]{:S(2)}, u32[]{:S(2)}) %collective-permute-start) | collective-permute-done | bytes 34848 | tf_op jit(solution)/shard_map/ppermute | solution.py:531
  27.9 11.2 %collective-permute-done.2.wk1 = bf16[512,512]{1,0:T(8,128)(2,1)S(1)} collective-permute-done((bf16[512,512]{1,0:T(8,128)(2,1)}, bf16[512,512]{1,0:T(8,128)(2,1)S(1)}, u32[]{:S(2)}, u32[]{:S(2)}) %collective-permute-start.2) | collective-permute-done | bytes 524320 | tf_op jit(solution)/shard_map/ppermute | solution.py:531
  39.1 10.1 %collective-permute-done.3.wv1 = bf16[512,512]{1,0:T(8,128)(2,1)S(1)} collective-permute-done((bf16[512,512]{1,0:T(8,128)(2,1)}, bf16[512,512]{1,0:T(8,128)(2,1)S(1)}, u32[]{:S(2)}, u32[]{:S(2)}) %collective-permute-start.3) | collective-permute-done | bytes 524320 | tf_op jit(solution)/shard_map/ppermute | solution.py:531
  50.4 7.2 %project.1 = (bf16[512,1024]{1,0:T(8,128)(2,1)S(1)}, bf16[512,1024]{1,0:T(8,128)(2,1)S(1)}, bf16[512,512]{1,0:T(8,128)(2,1)}, bf16[512,512]{1,0:T(8,128)(2,1)}) custom-call(s32[1]{0:T(128)} %bitcast.g_ref, bf16[512,1024]{1,0:T(8,128)(2,1)} %bitcast.510, f32[1,1024]{1,0:T(1,128)S(1)} %get-tuple-element.176.gain_ref, bf16[512,1024]{1,0:T(8,128)(2,1)} %wq0.3, ...), custom_call_target="tpu_custom_call" | custom-call | flops 2147483648 | bytes 8388608 | tf_op jit(solution)/shard_map/project/pallas_call | solution.py:94
  59.6 3.4 collective-permute-start.4
  68.3 7.3 %collective-permute-done.4.k1_ref = bf16[512,512]{1,0:T(8,128)(2,1)S(1)} collective-permute-done((bf16[512,512]{1,0:T(8,128)(2,1)}, bf16[512,512]{1,0:T(8,128)(2,1)S(1)}, u32[]{:S(2)}, u32[]{:S(2)}) %collective-permute-start.4) | collective-permute-done | bytes 524320 | tf_op jit(solution)/shard_map/ppermute | solution.py:598
  76.4 10.4 %collective-permute-done.5.v1_ref = bf16[512,512]{1,0:T(8,128)(2,1)S(1)} collective-permute-done((bf16[512,512]{1,0:T(8,128)(2,1)}, bf16[512,512]{1,0:T(8,128)(2,1)S(1)}, u32[]{:S(2)}, u32[]{:S(2)}) %collective-permute-start.5) | collective-permute-done | bytes 524320 | tf_op jit(solution)/shard_map/ppermute | solution.py:598
  91.0 12.6 %attend.1 = (bf16[512,1024]{1,0:T(8,128)(2,1)S(1)}, f32[8,8,512]{2,1,0:T(8,128)S(1)}) custom-call(s32[1]{0:T(128)} %bitcast.g_ref, s32[1]{0:T(128)S(6)} %copy.376.prefix_ref, bf16[512,1024]{1,0:T(8,128)(2,1)S(1)} %copy-done.31, bf16[512,512]{1,0:T(8,128)(2,1)} %get-tuple-element.43.k0_ref, bf16[512,512]{1,0:T(8,128)(2,1)} %get-tuple-element.44.v0_ref, ...), custom_call_target="tpu_custom_call" | custom-call | flops 8589934592 | bytes 5242880 | tf_op jit(solution)/shard_map/attend/pallas_call | solution.py:167
  103.6 5.6 collective-permute-done.6.wo1
  112.0 3.2 collective-permute-start.7
  115.2 3.5 fusion.18.ct0
  120.2 3.5 fusion.16.xt0
  123.7 8.1 %collective-permute-done.8.c1 = bf16[512,1024]{1,0:T(8,128)(2,1)} collective-permute-done((bf16[512,1024]{1,0:T(8,128)(2,1)}, bf16[512,1024]{1,0:T(8,128)(2,1)}, u32[]{:S(2)}, u32[]{:S(2)}) %collective-permute-start.8) | collective-permute-done | bytes 1048608 | tf_op jit(solution)/shard_map/ppermute | solution.py:531
  131.8 3.5 fusion.19.ct1
  135.3 16.9 %collective-permute-done.7.x1 = bf16[512,1024]{1,0:T(8,128)(2,1)} collective-permute-done((bf16[512,1024]{1,0:T(8,128)(2,1)}, bf16[512,1024]{1,0:T(8,128)(2,1)}, u32[]{:S(2)}, u32[]{:S(2)}) %collective-permute-start.7) | collective-permute-done | bytes 1048608 | tf_op jit(solution)/shard_map/ppermute | solution.py:531
  152.2 3.5 fusion.17.xt1
  155.8 113.8 %experts.1 = (bf16[8,512,1536]{2,1,0:T(8,128)(2,1)}, bf16[8,512,1536]{2,1,0:T(8,128)(2,1)}, f32[512,1024]{1,0:T(8,128)}, bf16[512,1040]{1,0:T(8,128)(2,1)}, f32[...) custom-call(s32[1]{0:T(128)} %bitcast.g_ref, ...), custom_call_target="tpu_custom_call" | custom-call | flops 77309411328 | bytes 73400320 | tf_op jit(solution)/shard_map/experts/pallas_call | solution.py:391
  278.3 20.9 %collective-permute-done.10 = bf16[512,1040]{0,1:T(8,128)(2,1)} collective-permute-done((bf16[512,1040]{0,1:T(8,128)(2,1)}, bf16[512,1040]{0,1:T(8,128)(2,1)}, u32[]{:S(2)}, u32[]{:S(2)}) %collective-permute-start.10) | collective-permute-done | bytes 1064992 | tf_op jit(solution)/shard_map/ppermute | solution.py:531
  301.6 6.5 middle.1
  310.0 23.9 %attend_back.1 = (bf16[512,1024]{1,0:T(8,128)(2,1)S(1)}, f32[512,512]{1,0:T(8,128)S(1)}, f32[512,512]{1,0:T(8,128)}, bf16[512,512]{1,0:T(8,128)(2,1)}, bf16[512,512]{1,0:T(8,128)(2,1)}) custom-call(s32[1]{0:T(128)} %bitcast.g_ref, s32[1]{0:T(128)S(6)} %copy.376.prefix_ref, bf16[512,1024]{1,0:T(8,128)(2,1)} %copy-done.30, ...), custom_call_target="tpu_custom_call" | custom-call | flops 21474836480 | bytes 8388608 | tf_op jit(solution)/shard_map/attend_back/pallas_call | solution.py:250
  338.9 3.7 convolution_convert_fusion
  345.5 9.3 %fusion.73 = (bf16[2,512,1536]{2,1,0:T(8,128)(2,1)}, bf16[2,512,1536]{2,1,0:T(8,128)(2,1)}, bf16[2,512,1536]{2,1,0:T(8,128)(2,1)}, bf16[2,512,1536]{2,1,0:T(8,128)(2,1)}) fusion(bf16[8,512,1536]{2,1,0:T(8,128)(2,1)} %get-tuple-element.71), kind=kLoop, calls=%fused_computation.275 | loop fusion | bytes 25165824 | tf_op jit(solution)/shard_map/slice | solution.py:628
  354.9 2.9 fusion.23
  359.5 3.6 collective-permute-done.11.dk1
  363.1 5.6 collective-permute-done.12.dv1
  368.7 6.7 weight_grads.1
  379.7 6.1 input_grads.1
  405.9 8.4 %collective-permute-start.27 = (bf16[2,2,2,32,256]{4,3,2,1,0:T(8,128)(2,1)S(1)}, bf16[2,2,2,32,256]{4,3,2,1,0:T(8,128)(2,1)S(1)}, u32[]{:S(2)}, u32[]{:S(2)}) collective-permute-start(bf16[2,2,2,32,256]{4,3,2,1,0:T(8,128)(2,1)S(1)} %fusion.49), channel_id=1, source_target_pairs={{0,16},{16,0},{1,17},{17,1},{2,18},{18,2},{3,19},{19,3},{4,20},{20... | collective-permute-start | bytes 393224 | tf_op jit(solution)/shard_map/ppermute | solution.py:531
  431.6 2.9 collective-permute-done.36
  438.2 2.8 collective-permute-done.37
  460.1 3.3 collective-permute-done.18
  465.9 3.0 collective-permute-done.19
  471.1 4.2 collective-permute-done.20
  477.5 2.8 collective-permute-start.24
  484.4 3.0 collective-permute-done.25
  489.3 5.5 fusion.74
  515.3 13.1 %collective-permute-done.49 = bf16[2,2,2,2,32,1536]{5,4,0,3,2,1:T(8,128)(2,1)S(1)} collective-permute-done((bf16[2,2,2,2,32,1536]{5,4,0,3,2,1:T(8,128)(2,1)}, bf16[2,2,2,2,32,1536]{5,4,0,3,2,1:T(8,128)(2,1)S(1)}, u32[]{:S(2)}, u32[]{:S(2)}) %collective-permute-start.49) | collective-permute-done | bytes 1572896 | tf_op jit(solution)/shard_map/ppermute | solution.py:533
  530.5 10.7 %collective-permute-done.46 = bf16[2,2,2,2,32,1536]{5,4,0,3,2,1:T(8,128)(2,1)S(1)} collective-permute-done((bf16[2,2,2,2,32,1536]{5,4,0,3,2,1:T(8,128)(2,1)}, bf16[2,2,2,2,32,1536]{5,4,0,3,2,1:T(8,128)(2,1)S(1)}, u32[]{:S(2)}, u32[]{:S(2)}) %collective-permute-start.46) | collective-permute-done | bytes 1572896 | tf_op jit(solution)/shard_map/ppermute | solution.py:533
  542.7 32.3 %collective-permute-done.43 = bf16[2,2,2,2,32,1536]{5,4,0,3,2,1:T(8,128)(2,1)} collective-permute-done((bf16[2,2,2,2,32,1536]{5,4,0,3,2,1:T(8,128)(2,1)}, bf16[2,2,2,2,32,1536]{5,4,0,3,2,1:T(8,128)(2,1)}, u32[]{:S(2)}, u32[]{:S(2)}) %collective-permute-start.43) | collective-permute-done | bytes 1572896 | tf_op jit(solution)/shard_map/ppermute | solution.py:533
  577.7 27.1 %collective-permute-done.40 = bf16[2,2,2,2,32,1536]{5,4,0,3,2,1:T(8,128)(2,1)S(1)} collective-permute-done((bf16[2,2,2,2,32,1536]{5,4,0,3,2,1:T(8,128)(2,1)S(1)}, bf16[2,2,2,2,32,1536]{5,4,0,3,2,1:T(8,128)(2,1)S(1)}, u32[]{:S(2)}, u32[]{:S(2)}) %collective-permute-start.40) | collective-permute-done | bytes 1572896 | tf_op jit(solution)/shard_map/ppermute | solution.py:533
  608.2 4.9 collective-permute-done.50
  619.4 5.4 collective-permute-done.41
  625.1 3.3 collective-permute-start.42
  628.4 24.0 %collective-permute-done.51 = bf16[2,2,32,1536]{3,2,0,1:T(8,128)(2,1)S(1)} collective-permute-done((bf16[2,2,32,1536]{3,2,0,1:T(8,128)(2,1)S(1)}, bf16[2,2,32,1536]{3,2,0,1:T(8,128)(2,1)S(1)}, u32[]{:S(2)}, u32[]{:S(2)}) %collective-permute-start.51) | collective-permute-done | bytes 393248 | tf_op jit(solution)/shard_map/ppermute | solution.py:533
  652.6 8.2 %collective-permute-done.48 = bf16[2,2,32,1536]{3,2,0,1:T(8,128)(2,1)S(1)} collective-permute-done((bf16[2,2,32,1536]{3,2,0,1:T(8,128)(2,1)S(1)}, bf16[2,2,32,1536]{3,2,0,1:T(8,128)(2,1)S(1)}, u32[]{:S(2)}, u32[]{:S(2)}) %collective-permute-start.48) | collective-permute-done | bytes 393248 | tf_op jit(solution)/shard_map/ppermute | solution.py:533
  661.0 8.2 %collective-permute-done.45 = bf16[2,2,32,1536]{3,2,0,1:T(8,128)(2,1)S(1)} collective-permute-done((bf16[2,2,32,1536]{3,2,0,1:T(8,128)(2,1)S(1)}, bf16[2,2,32,1536]{3,2,0,1:T(8,128)(2,1)S(1)}, u32[]{:S(2)}, u32[]{:S(2)}) %collective-permute-start.45) | collective-permute-done | bytes 393248 | tf_op jit(solution)/shard_map/ppermute | solution.py:533
  669.5 4.3 collective-permute-done.42
  678.3 13.3 %collective-permute-done.52 = f32[32,128]{0,1:T(8,128)S(1)} collective-permute-done((f32[32,128]{0,1:T(8,128)S(1)}, f32[32,128]{0,1:T(8,128)S(1)}, u32[]{:S(2)}, u32[]{:S(2)}) %collective-permute-start.52) | collective-permute-done | bytes 16416 | tf_op jit(solution)/shard_map/ppermute | solution.py:531
  (339 shorter events, 171.1 us)
Async XLA Ops:
  0.7 48.5 %collective-permute-start.1 = (bf16[512,1024]{1,0:T(8,128)(2,1)}, bf16[512,1024]{1,0:T(8,128)(2,1)}, u32[]{:S(2)}, u32[]{:S(2)}) collective-permute-start(bf16[512,1024]{1,0:T(8,128)(2,1)} %wq0.3), channel_id=1, source_target_pairs={{0,16},{16,0},{1,17},{17,1},{2,18},{18,2},{3,19},{19,3},{4,20},{20... | collective-permute-start | bytes 3145736 | tf_op jit(solution)/shard_map/ppermute | solution.py:531
  5.2 22.7 %collective-permute-start = (bf16[34,512]{1,0:T(8,128)(2,1)S(1)}, bf16[34,512]{1,0:T(8,128)(2,1)S(1)}, u32[]{:S(2)}, u32[]{:S(2)}) collective-permute-start(bf16[34,512]{1,0:T(8,128)(2,1)S(1)} %pad_maximum_fusion.6), channel_id=1, source_target_pairs={{0,16},{16,0},{1,17},{17,1},{2,18},{18,2},{3,19},{19,3},{4,20},{20... | collective-permute-start | bytes 104456 | tf_op jit(solution)/shard_map/ppermute | solution.py:531
  5.8 33.3 %collective-permute-start.2 = (bf16[512,512]{1,0:T(8,128)(2,1)}, bf16[512,512]{1,0:T(8,128)(2,1)S(1)}, u32[]{:S(2)}, u32[]{:S(2)}) collective-permute-start(bf16[512,512]{1,0:T(8,128)(2,1)} %wk0.3), channel_id=1, source_target_pairs={{0,16},{16,0},{1,17},{17,1},{2,18},{18,2},{3,19},{19,3},{4,20},{20... | collective-permute-start | bytes 1572872 | tf_op jit(solution)/shard_map/ppermute | solution.py:531
  7.3 41.9 %collective-permute-start.3 = (bf16[512,512]{1,0:T(8,128)(2,1)}, bf16[512,512]{1,0:T(8,128)(2,1)S(1)}, u32[]{:S(2)}, u32[]{:S(2)}) collective-permute-start(bf16[512,512]{1,0:T(8,128)(2,1)} %wv0.3), channel_id=1, source_target_pairs={{0,16},{16,0},{1,17},{17,1},{2,18},{18,2},{3,19},{19,3},{4,20},{20... | collective-permute-start | bytes 1572872 | tf_op jit(solution)/shard_map/ppermute | solution.py:531
  59.6 16.1 %collective-permute-start.4 = (bf16[512,512]{1,0:T(8,128)(2,1)}, bf16[512,512]{1,0:T(8,128)(2,1)S(1)}, u32[]{:S(2)}, u32[]{:S(2)}) collective-permute-start(bf16[512,512]{1,0:T(8,128)(2,1)} %get-tuple-element.43.k0_ref), channel_id=1, source_target_pairs={{0,16},{1,17},{2,18},{3,19},{4,20},{5,21},{6,22},{7,23},{8,24},{9,... | collective-permute-start | bytes 1572872 | tf_op jit(solution)/shard_map/ppermute | solution.py:598
  63.0 23.9 %collective-permute-start.5 = (bf16[512,512]{1,0:T(8,128)(2,1)}, bf16[512,512]{1,0:T(8,128)(2,1)S(1)}, u32[]{:S(2)}, u32[]{:S(2)}) collective-permute-start(bf16[512,512]{1,0:T(8,128)(2,1)} %get-tuple-element.44.v0_ref), channel_id=1, source_target_pairs={{0,16},{1,17},{2,18},{3,19},{4,20},{5,21},{6,22},{7,23},{8,24},{9,... | collective-permute-start | bytes 1572872 | tf_op jit(solution)/shard_map/ppermute | solution.py:598
  64.6 44.6 %collective-permute-start.6 = (bf16[512,1024]{1,0:T(8,128)(2,1)S(1)}, bf16[512,1024]{1,0:T(8,128)(2,1)S(1)}, u32[]{:S(2)}, u32[]{:S(2)}) collective-permute-start(bf16[512,1024]{1,0:T(8,128)(2,1)S(1)} %copy-done), channel_id=1, source_target_pairs={{0,16},{16,0},{1,17},{17,1},{2,18},{18,2},{3,19},{19,3},{4,20},{20... | collective-permute-start | bytes 3145736 | tf_op jit(solution)/shard_map/ppermute | solution.py:531
  66.2 65.6 %collective-permute-start.8 = (bf16[512,1024]{1,0:T(8,128)(2,1)}, bf16[512,1024]{1,0:T(8,128)(2,1)}, u32[]{:S(2)}, u32[]{:S(2)}) collective-permute-start(bf16[512,1024]{1,0:T(8,128)(2,1)} %bitcast.6.c0.c_ref), channel_id=1, source_target_pairs={{0,16},{16,0},{1,17},{17,1},{2,18},{18,2},{3,19},{19,3},{4,20},{20... | collective-permute-start | bytes 3145736 | tf_op jit(solution)/shard_map/ppermute | solution.py:531
  112.0 40.3 %collective-permute-start.7 = (bf16[512,1024]{1,0:T(8,128)(2,1)}, bf16[512,1024]{1,0:T(8,128)(2,1)}, u32[]{:S(2)}, u32[]{:S(2)}) collective-permute-start(bf16[512,1024]{1,0:T(8,128)(2,1)} %get-tuple-element.48.x0), channel_id=1, source_target_pairs={{0,16},{16,0},{1,17},{17,1},{2,18},{18,2},{3,19},{19,3},{4,20},{20... | collective-permute-start | bytes 3145736 | tf_op jit(solution)/shard_map/ppermute | solution.py:531
  272.0 27.2 %collective-permute-start.10 = (bf16[512,1040]{0,1:T(8,128)(2,1)}, bf16[512,1040]{0,1:T(8,128)(2,1)}, u32[]{:S(2)}, u32[]{:S(2)}) collective-permute-start(bf16[512,1040]{0,1:T(8,128)(2,1)} %copy.270), channel_id=1, source_target_pairs={{0,16},{16,0},{1,17},{17,1},{2,18},{18,2},{3,19},{19,3},{4,20},{20... | collective-permute-start | bytes 3194888 | tf_op jit(solution)/shard_map/ppermute | solution.py:531
  278.2 76.6 %collective-permute-start.9 = (bf16[512,1024]{1,0:T(8,128)(2,1)}, bf16[512,1024]{1,0:T(8,128)(2,1)}, u32[]{:S(2)}, u32[]{:S(2)}) collective-permute-start(bf16[512,1024]{1,0:T(8,128)(2,1)} %get-tuple-element.51), channel_id=1, source_target_pairs={{0,16},{16,0},{1,17},{17,1},{2,18},{18,2},{3,19},{19,3},{4,20},{20... | collective-permute-start | bytes 3145736 | tf_op jit(solution)/shard_map/ppermute | solution.py:531
  278.2 211.1 %collective-permute-start.39 = (bf16[8,512,1536]{2,1,0:T(8,128)(2,1)}, bf16[8,512,1536]{2,1,0:T(8,128)(2,1)}, u32[]{:S(2)}, u32[]{:S(2)}) collective-permute-start(bf16[8,512,1536]{2,1,0:T(8,128)(2,1)} %get-tuple-element.72), channel_id=1, source_target_pairs={{0,1},{1,0},{2,3},{3,2},{4,5},{5,4},{6,7},{7,6},{8,9},{9,8},{10,11... | collective-permute-start | bytes 37748744 | tf_op jit(solution)/shard_map/ppermute | solution.py:533
  334.9 28.2 %collective-permute-start.11 = (bf16[512,512]{1,0:T(8,128)(2,1)}, bf16[512,512]{1,0:T(8,128)(2,1)}, u32[]{:S(2)}, u32[]{:S(2)}) collective-permute-start(bf16[512,512]{1,0:T(8,128)(2,1)} %get-tuple-element.61), channel_id=1, source_target_pairs={{16,0},{17,1},{18,2},{19,3},{20,4},{21,5},{22,6},{23,7},{24,8},{25... | collective-permute-start | bytes 1572872 | tf_op jit(solution)/shard_map/ppermute | solution.py:599
  336.3 32.4 %collective-permute-start.12 = (bf16[512,512]{1,0:T(8,128)(2,1)}, bf16[512,512]{1,0:T(8,128)(2,1)}, u32[]{:S(2)}, u32[]{:S(2)}) collective-permute-start(bf16[512,512]{1,0:T(8,128)(2,1)} %get-tuple-element.63), channel_id=1, source_target_pairs={{16,0},{17,1},{18,2},{19,3},{20,4},{21,5},{22,6},{23,7},{24,8},{25... | collective-permute-start | bytes 1572872 | tf_op jit(solution)/shard_map/ppermute | solution.py:599
  345.5 40.4 %collective-permute-start.26 = (bf16[512,1040]{0,1:T(8,128)(2,1)}, bf16[512,1040]{0,1:T(8,128)(2,1)S(1)}, u32[]{:S(2)}, u32[]{:S(2)}) collective-permute-start(bf16[512,1040]{0,1:T(8,128)(2,1)} %copy.279), channel_id=1, source_target_pairs={{0,1},{1,0},{2,3},{3,2},{4,5},{5,4},{6,7},{7,6},{8,9},{9,8},{10,11... | collective-permute-start | bytes 3194888 | tf_op jit(solution)/shard_map/ppermute | solution.py:533
  379.7 69.9 %collective-permute-start.13 = (bf16[512,2048]{1,0:T(8,128)(2,1)}, bf16[512,2048]{1,0:T(8,128)(2,1)}, u32[]{:S(2)}, u32[]{:S(2)}) collective-permute-start(bf16[512,2048]{1,0:T(8,128)(2,1)} %get-tuple-element.68), channel_id=1, source_target_pairs={{0,1},{1,0},{2,3},{3,2},{4,5},{5,4},{6,7},{7,6},{8,9},{9,8},{10,11... | collective-permute-start | bytes 6291464 | tf_op jit(solution)/shard_map/ppermute | solution.py:533
  389.9 38.3 %collective-permute-start.35 = (bf16[2,2,2,32,528]{4,3,2,1,0:T(8,128)(2,1)}, bf16[2,2,2,32,528]{4,3,2,1,0:T(8,128)(2,1)}, u32[]{:S(2)}, u32[]{:S(2)}) collective-permute-start(bf16[2,2,2,32,528]{4,3,2,1,0:T(8,128)(2,1)} %fusion.40), channel_id=1, source_target_pairs={{0,4},{1,5},{2,6},{3,7},{4,0},{5,1},{6,2},{7,3},{8,12},{9,13},{10,... | collective-permute-start | bytes 811016 | tf_op jit(solution)/shard_map/ppermute | solution.py:533
  399.3 16.6 %collective-permute-start.31 = (bf16[2,2,2,32,256]{4,3,2,1,0:T(8,128)(2,1)}, bf16[2,2,2,32,256]{4,3,2,1,0:T(8,128)(2,1)}, u32[]{:S(2)}, u32[]{:S(2)}) collective-permute-start(bf16[2,2,2,32,256]{4,3,2,1,0:T(8,128)(2,1)} %bitcast.70), channel_id=1, source_target_pairs={{0,2},{1,3},{2,0},{3,1},{4,6},{5,7},{6,4},{7,5},{8,10},{9,11},{10,... | collective-permute-start | bytes 393224 | tf_op jit(solution)/shard_map/ppermute | solution.py:533
  405.9 12.6 %collective-permute-start.27 = (bf16[2,2,2,32,256]{4,3,2,1,0:T(8,128)(2,1)S(1)}, bf16[2,2,2,32,256]{4,3,2,1,0:T(8,128)(2,1)S(1)}, u32[]{:S(2)}, u32[]{:S(2)}) collective-permute-start(bf16[2,2,2,32,256]{4,3,2,1,0:T(8,128)(2,1)S(1)} %fusion.49), channel_id=1, source_target_pairs={{0,16},{16,0},{1,17},{17,1},{2,18},{18,2},{3,19},{19,3},{4,20},{20... | collective-permute-start | bytes 393224 | tf_op jit(solution)/shard_map/ppermute | solution.py:531
  424.5 5.8 collective-permute-start.29
  427.6 15.7 %collective-permute-start.34 = (bf16[32,256]{1,0:T(8,128)(2,1)S(1)}, bf16[32,256]{1,0:T(8,128)(2,1)S(1)}, u32[]{:S(2)}, u32[]{:S(2)}) collective-permute-start(bf16[32,256]{1,0:T(8,128)(2,1)S(1)} %fusion.65), channel_id=1, source_target_pairs={{0,16},{16,0},{1,17},{17,1},{2,18},{18,2},{3,19},{19,3},{4,20},{20... | collective-permute-start | bytes 49160 | tf_op jit(solution)/shard_map/ppermute | solution.py:531
  429.2 5.4 collective-permute-start.36
  431.1 5.7 collective-permute-start.30
  435.5 5.4 collective-permute-start.37
  450.9 13.9 %collective-permute-start.22 = (bf16[2,2,2,32,768]{4,3,2,1,0:T(8,128)(2,1)S(1)}, bf16[2,2,2,32,768]{4,3,2,1,0:T(8,128)(2,1)S(1)}, u32[]{:S(2)}, u32[]{:S(2)}) collective-permute-start(bf16[2,2,2,32,768]{4,3,2,1,0:T(8,128)(2,1)S(1)} %fusion.33), channel_id=1, source_target_pairs={{0,4},{1,5},{2,6},{3,7},{4,0},{5,1},{6,2},{7,3},{8,12},{9,13},{10,... | collective-permute-start | bytes 1179656 | tf_op jit(solution)/shard_map/ppermute | solution.py:533
  453.7 9.7 %collective-permute-start.18 = (bf16[2,2,2,32,640]{4,3,2,1,0:T(8,128)(2,1)S(1)}, bf16[2,2,2,32,640]{4,3,2,1,0:T(8,128)(2,1)S(1)}, u32[]{:S(2)}, u32[]{:S(2)}) collective-permute-start(bf16[2,2,2,32,640]{4,3,2,1,0:T(8,128)(2,1)S(1)} %bitcast.585), channel_id=1, source_target_pairs={{0,2},{1,3},{2,0},{3,1},{4,6},{5,7},{6,4},{7,5},{8,10},{9,11},{10,... | collective-permute-start | bytes 983048 | tf_op jit(solution)/shard_map/ppermute | solution.py:533
  456.0 7.5 %collective-permute-start.14 = (bf16[2,2,2,32,640]{4,3,2,1,0:T(8,128)(2,1)S(1)}, bf16[2,2,2,32,640]{4,3,2,1,0:T(8,128)(2,1)S(1)}, u32[]{:S(2)}, u32[]{:S(2)}) collective-permute-start(bf16[2,2,2,32,640]{4,3,2,1,0:T(8,128)(2,1)S(1)} %fusion.39), channel_id=1, source_target_pairs={{0,16},{16,0},{1,17},{17,1},{2,18},{18,2},{3,19},{19,3},{4,20},{20... | collective-permute-start | bytes 983048 | tf_op jit(solution)/shard_map/ppermute | solution.py:531
  463.5 5.4 collective-permute-start.19
  463.6 6.1 collective-permute-start.15
  464.9 12.6 %collective-permute-start.23 = (bf16[2,2,32,768]{3,2,1,0:T(8,128)(2,1)S(1)}, bf16[2,2,32,768]{3,2,1,0:T(8,128)(2,1)S(1)}, u32[]{:S(2)}, u32[]{:S(2)}) collective-permute-start(bf16[2,2,32,768]{3,2,1,0:T(8,128)(2,1)S(1)} %fusion.38), channel_id=1, source_target_pairs={{0,2},{1,3},{2,0},{3,1},{4,6},{5,7},{6,4},{7,5},{8,10},{9,11},{10,... | collective-permute-start | bytes 589832 | tf_op jit(solution)/shard_map/ppermute | solution.py:533
  468.9 6.4 collective-permute-start.20
  469.8 7.4 %collective-permute-start.16 = (bf16[2,32,640]{2,1,0:T(8,128)(2,1)S(1)}, bf16[2,32,640]{2,1,0:T(8,128)(2,1)S(1)}, u32[]{:S(2)}, u32[]{:S(2)}) collective-permute-start(bf16[2,32,640]{2,1,0:T(8,128)(2,1)S(1)} %fusion.48), channel_id=1, source_target_pairs={{0,4},{1,5},{2,6},{3,7},{4,0},{5,1},{6,2},{7,3},{8,12},{9,13},{10,... | collective-permute-start | bytes 245768 | tf_op jit(solution)/shard_map/ppermute | solution.py:533
  477.2 7.2 %collective-permute-start.17 = (bf16[32,640]{1,0:T(8,128)(2,1)S(1)}, bf16[32,640]{1,0:T(8,128)(2,1)S(1)}, u32[]{:S(2)}, u32[]{:S(2)}) collective-permute-start(bf16[32,640]{1,0:T(8,128)(2,1)S(1)} %fusion.61), channel_id=1, source_target_pairs={{0,8},{1,9},{2,10},{3,11},{4,12},{5,13},{6,14},{7,15},{8,0},{9,1},... | collective-permute-start | bytes 122888 | tf_op jit(solution)/shard_map/ppermute | solution.py:533
  477.5 5.7 collective-permute-start.24
  497.2 31.1 %collective-permute-start.49 = (bf16[2,2,2,2,32,1536]{5,4,0,3,2,1:T(8,128)(2,1)}, bf16[2,2,2,2,32,1536]{5,4,0,3,2,1:T(8,128)(2,1)S(1)}, u32[]{:S(2)}, u32[]{:S(2)}) collective-permute-start(bf16[2,2,2,2,32,1536]{5,4,0,3,2,1:T(8,128)(2,1)} %fusion.15), channel_id=1, source_target_pairs={{0,4},{1,5},{2,6},{3,7},{4,0},{5,1},{6,2},{7,3},{8,12},{9,13},{10,... | collective-permute-start | bytes 4718600 | tf_op jit(solution)/shard_map/ppermute | solution.py:533
  503.7 37.5 %collective-permute-start.46 = (bf16[2,2,2,2,32,1536]{5,4,0,3,2,1:T(8,128)(2,1)}, bf16[2,2,2,2,32,1536]{5,4,0,3,2,1:T(8,128)(2,1)S(1)}, u32[]{:S(2)}, u32[]{:S(2)}) collective-permute-start(bf16[2,2,2,2,32,1536]{5,4,0,3,2,1:T(8,128)(2,1)} %fusion.14), channel_id=1, source_target_pairs={{0,2},{1,3},{2,0},{3,1},{4,6},{5,7},{6,4},{7,5},{8,10},{9,11},{10,... | collective-permute-start | bytes 4718600 | tf_op jit(solution)/shard_map/ppermute | solution.py:533
  509.4 65.7 %collective-permute-start.43 = (bf16[2,2,2,2,32,1536]{5,4,0,3,2,1:T(8,128)(2,1)}, bf16[2,2,2,2,32,1536]{5,4,0,3,2,1:T(8,128)(2,1)}, u32[]{:S(2)}, u32[]{:S(2)}) collective-permute-start(bf16[2,2,2,2,32,1536]{5,4,0,3,2,1:T(8,128)(2,1)} %fusion.13), channel_id=1, source_target_pairs={{0,2},{1,3},{2,0},{3,1},{4,6},{5,7},{6,4},{7,5},{8,10},{9,11},{10,... | collective-permute-start | bytes 4718600 | tf_op jit(solution)/shard_map/ppermute | solution.py:533
  513.7 91.1 %collective-permute-start.40 = (bf16[2,2,2,2,32,1536]{5,4,0,3,2,1:T(8,128)(2,1)S(1)}, bf16[2,2,2,2,32,1536]{5,4,0,3,2,1:T(8,128)(2,1)S(1)}, u32[]{:S(2)}, u32[]{:S(2)}) collective-permute-start(bf16[2,2,2,2,32,1536]{5,4,0,3,2,1:T(8,128)(2,1)S(1)} %fusion.12), channel_id=1, source_target_pairs={{0,2},{1,3},{2,0},{3,1},{4,6},{5,7},{6,4},{7,5},{8,10},{9,11},{10,... | collective-permute-start | bytes 4718600 | tf_op jit(solution)/shard_map/ppermute | solution.py:533
  528.7 84.5 %collective-permute-start.50 = (bf16[2,2,2,32,1536]{4,3,0,2,1:T(8,128)(2,1)S(1)}, bf16[2,2,2,32,1536]{4,3,0,2,1:T(8,128)(2,1)S(1)}, u32[]{:S(2)}, u32[]{:S(2)}) collective-permute-start(bf16[2,2,2,32,1536]{4,3,0,2,1:T(8,128)(2,1)S(1)} %fusion.31), channel_id=1, source_target_pairs={{0,2},{1,3},{2,0},{3,1},{4,6},{5,7},{6,4},{7,5},{8,10},{9,11},{10,... | collective-permute-start | bytes 2359304 | tf_op jit(solution)/shard_map/ppermute | solution.py:533
  541.5 74.4 %collective-permute-start.47 = (bf16[2,2,2,32,1536]{4,3,0,2,1:T(8,128)(2,1)S(1)}, bf16[2,2,2,32,1536]{4,3,0,2,1:T(8,128)(2,1)S(1)}, u32[]{:S(2)}, u32[]{:S(2)}) collective-permute-start(bf16[2,2,2,32,1536]{4,3,0,2,1:T(8,128)(2,1)S(1)} %fusion.30), channel_id=1, source_target_pairs={{0,4},{1,5},{2,6},{3,7},{4,0},{5,1},{6,2},{7,3},{8,12},{9,13},{10,... | collective-permute-start | bytes 2359304 | tf_op jit(solution)/shard_map/ppermute | solution.py:533
  576.5 40.1 %collective-permute-start.44 = (bf16[2,2,2,32,1536]{4,3,0,2,1:T(8,128)(2,1)S(1)}, bf16[2,2,2,32,1536]{4,3,0,2,1:T(8,128)(2,1)S(1)}, u32[]{:S(2)}, u32[]{:S(2)}) collective-permute-start(bf16[2,2,2,32,1536]{4,3,0,2,1:T(8,128)(2,1)S(1)} %fusion.29), channel_id=1, source_target_pairs={{0,4},{1,5},{2,6},{3,7},{4,0},{5,1},{6,2},{7,3},{8,12},{9,13},{10,... | collective-permute-start | bytes 2359304 | tf_op jit(solution)/shard_map/ppermute | solution.py:533
  605.1 19.8 %collective-permute-start.41 = (bf16[2,2,2,32,1536]{4,3,0,2,1:T(8,128)(2,1)S(1)}, bf16[2,2,2,32,1536]{4,3,0,2,1:T(8,128)(2,1)S(1)}, u32[]{:S(2)}, u32[]{:S(2)}) collective-permute-start(bf16[2,2,2,32,1536]{4,3,0,2,1:T(8,128)(2,1)S(1)} %fusion.28), channel_id=1, source_target_pairs={{0,4},{1,5},{2,6},{3,7},{4,0},{5,1},{6,2},{7,3},{8,12},{9,13},{10,... | collective-permute-start | bytes 2359304 | tf_op jit(solution)/shard_map/ppermute | solution.py:533
  613.4 39.0 %collective-permute-start.51 = (bf16[2,2,32,1536]{3,2,0,1:T(8,128)(2,1)S(1)}, bf16[2,2,32,1536]{3,2,0,1:T(8,128)(2,1)S(1)}, u32[]{:S(2)}, u32[]{:S(2)}) collective-permute-start(bf16[2,2,32,1536]{3,2,0,1:T(8,128)(2,1)S(1)} %fusion.37), channel_id=1, source_target_pairs={{0,8},{1,9},{2,10},{3,11},{4,12},{5,13},{6,14},{7,15},{8,0},{9,1},... | collective-permute-start | bytes 1179656 | tf_op jit(solution)/shard_map/ppermute | solution.py:533
  616.1 44.6 %collective-permute-start.48 = (bf16[2,2,32,1536]{3,2,0,1:T(8,128)(2,1)S(1)}, bf16[2,2,32,1536]{3,2,0,1:T(8,128)(2,1)S(1)}, u32[]{:S(2)}, u32[]{:S(2)}) collective-permute-start(bf16[2,2,32,1536]{3,2,0,1:T(8,128)(2,1)S(1)} %fusion.36), channel_id=1, source_target_pairs={{0,8},{1,9},{2,10},{3,11},{4,12},{5,13},{6,14},{7,15},{8,0},{9,1},... | collective-permute-start | bytes 1179656 | tf_op jit(solution)/shard_map/ppermute | solution.py:533
  616.9 52.4 %collective-permute-start.45 = (bf16[2,2,32,1536]{3,2,0,1:T(8,128)(2,1)S(1)}, bf16[2,2,32,1536]{3,2,0,1:T(8,128)(2,1)S(1)}, u32[]{:S(2)}, u32[]{:S(2)}) collective-permute-start(bf16[2,2,32,1536]{3,2,0,1:T(8,128)(2,1)S(1)} %fusion.35), channel_id=1, source_target_pairs={{0,8},{1,9},{2,10},{3,11},{4,12},{5,13},{6,14},{7,15},{8,0},{9,1},... | collective-permute-start | bytes 1179656 | tf_op jit(solution)/shard_map/ppermute | solution.py:533
  625.1 48.7 %collective-permute-start.42 = (bf16[2,2,32,1536]{3,2,0,1:T(8,128)(2,1)S(1)}, bf16[2,2,32,1536]{3,2,0,1:T(8,128)(2,1)S(1)}, u32[]{:S(2)}, u32[]{:S(2)}) collective-permute-start(bf16[2,2,32,1536]{3,2,0,1:T(8,128)(2,1)S(1)} %fusion.34), channel_id=1, source_target_pairs={{0,8},{1,9},{2,10},{3,11},{4,12},{5,13},{6,14},{7,15},{8,0},{9,1},... | collective-permute-start | bytes 1179656 | tf_op jit(solution)/shard_map/ppermute | solution.py:533
  674.4 17.8 %collective-permute-start.53 = (bf16[8,32,1536]{2,1,0:T(8,128)(2,1)S(1)}, bf16[8,32,1536]{2,1,0:T(8,128)(2,1)S(1)}, u32[]{:S(2)}, u32[]{:S(2)}) collective-permute-start(bf16[8,32,1536]{2,1,0:T(8,128)(2,1)S(1)} %fusion.32), channel_id=1, source_target_pairs={{0,16},{16,0},{1,17},{17,1},{2,18},{18,2},{3,19},{19,3},{4,20},{20... | collective-permute-start | bytes 2359304 | tf_op jit(solution)/shard_map/ppermute | solution.py:531
  676.1 15.4 %collective-permute-start.52 = (f32[32,128]{0,1:T(8,128)S(1)}, f32[32,128]{0,1:T(8,128)S(1)}, u32[]{:S(2)}, u32[]{:S(2)}) collective-permute-start(f32[32,128]{0,1:T(8,128)S(1)} %broadcast_in_dim.27), channel_id=1, source_target_pairs={{0,16},{16,0},{1,17},{17,1},{2,18},{18,2},{3,19},{19,3},{4,20},{20... | collective-permute-start | bytes 49160 | tf_op jit(solution)/shard_map/ppermute | solution.py:531
  (66 other events, 696.1 us)

commit v2 on v1

v2 whole, which is shorter than its diff:
```python
import functools
import math

import jax
import jax.numpy as jnp
import numpy as np
from jax import lax
from jax.experimental import pallas as pl
from jax.experimental.pallas import tpu as pltpu
from jax.sharding import PartitionSpec as P

HEADS = 16
KV_HEADS = 8
HEAD = 64
FF = 512
TOP = 8
EXPERTS = 16

EPSILON = 1e-06
THETA_BASE = 10000.0
MASKED = -1e30
HIGHEST = lax.Precision.HIGHEST
F32 = jnp.float32
BF16 = jnp.bfloat16
MIB = 1 << 20


def nn(left, right):
    return lax.dot_general(left, right, (((1,), (0,)), ((), ())), preferred_element_type=F32)


def nt(left, right):
    return lax.dot_general(left, right, (((1,), (1,)), ((), ())), preferred_element_type=F32)


def params(limit=24):
    return pltpu.CompilerParams(vmem_limit_bytes=limit * MIB)


def cost(microseconds):
    return pl.CostEstimate(flops=int(microseconds * 0.9e9), bytes_accessed=int(microseconds * 1e5), transcendentals=0)


def whole(shape):
    return pl.BlockSpec(shape, lambda *_: (0,) * len(shape), pipeline_mode=pl.Buffered(1))


SCALAR = pl.BlockSpec(memory_space=pltpu.SMEM)

FOLLOWED = []


def pallas(kernel, *, in_specs, out_shape, **more):
    def call(*args):
        tokens, count = list(FOLLOWED), len(in_specs)

        def body(*refs):
            kernel(*refs[:count], *refs[count + len(tokens) :])

        out = pl.pallas_call(
            body,
            in_specs=[*in_specs, *[pl.BlockSpec(memory_space=pl.ANY)] * len(tokens)],
            out_shape=out_shape,
            **more,
        )(*args, *tokens)
        FOLLOWED[:] = [min(jax.tree.leaves(out), key=lambda a: a.size)]
        return out

    return call
LANES = 128


def pieces(where_ref, width):
    g, core = where_ref[0], where_ref[1]
    half, quarter = width // 2, width // 4
    other = (1 - g) * half
    at = lambda start, size: pl.ds(pl.multiple_of(start, size), size)
    return (at(g * half, half), at(other + core * quarter, quarter), at(other + (1 - core) * quarter, quarter))


def project_rows(ref, where_ref, weights):
    cols = pieces(where_ref, ref.shape[1])
    return sum(nn(ref[:, c], w[...]) for c, w in zip(cols, weights))


def swap_halves(tile):
    lane = lax.broadcasted_iota(jnp.int32, tile.shape, 1) % HEAD
    return jnp.where(
        lane < HEAD // 2, pltpu.roll(tile, 128 - HEAD // 2, 1), pltpu.roll(tile, HEAD // 2, 1)
    )


def rotated(values, cosine, sine, sign):
    tiles = []
    for start in range(0, values.shape[1], 128):
        tile = values[:, start : start + 128]
        tiles.append(tile * cosine + swap_halves(tile) * (sine * sign))
    return tiles[0] if len(tiles) == 1 else jnp.concatenate(tiles, 1)


def project_kernel(where_ref, x_ref, gain_ref, wq0, wq1, wq2, wk0, wk1, wk2, wv0, wv1, wv2, cos_ref, sin_ref,
                   n_ref, q_ref, k_ref, v_ref):
    @pl.when(pl.program_id(0) == 0)
    def _():
        x = x_ref[...].astype(F32)
        scale = lax.rsqrt(jnp.mean(x * x, -1, keepdims=True) + EPSILON)
        n_ref[...] = (x * scale * gain_ref[...]).astype(BF16)

    cosine, sine = cos_ref[...], sin_ref[...]
    q = rotated(project_rows(n_ref, where_ref, (wq0, wq1, wq2)), cosine, sine, 1.0)
    q_ref[...] = q.astype(BF16) * jnp.asarray(1.0 / math.sqrt(HEAD), BF16)
    k = rotated(project_rows(n_ref, where_ref, (wk0, wk1, wk2)), cosine, sine, 1.0)
    k_ref[...] = k.astype(BF16)
    v_ref[...] = project_rows(n_ref, where_ref, (wv0, wv1, wv2)).astype(BF16)


def project_earlier_kernel(where_ref, x_ref, gain_ref, wk0, wk1, wk2, wv0, wv1, wv2, cos_ref, sin_ref,
                           k_ref, v_ref, n_ref):
    @pl.when(where_ref[0] != 0)
    def _():
        @pl.when(pl.program_id(0) == 0)
        def _():
            x = x_ref[...].astype(F32)
            scale = lax.rsqrt(jnp.mean(x * x, -1, keepdims=True) + EPSILON)
            n_ref[...] = (x * scale * gain_ref[...]).astype(BF16)

        k = rotated(project_rows(n_ref, where_ref, (wk0, wk1, wk2)), cos_ref[...], sin_ref[...], 1.0)
        k_ref[...] = k.astype(BF16)
        v_ref[...] = project_rows(n_ref, where_ref, (wv0, wv1, wv2)).astype(BF16)

    @pl.when(where_ref[0] == 0)
    def _():
        k_ref[...] = jnp.zeros_like(k_ref)
        v_ref[...] = jnp.zeros_like(v_ref)


def weight_specs(rows, n, first):
    packed = pl.BlockSpec((rows // 2, n), lambda i: (0, first // n + i))
    return [pl.BlockSpec((rows, n), lambda i: (0, i)), packed, packed]


def project(where, x, gain, wq, wk, wv, pack, cosine, sine):
    tokens, width = x.shape
    steps = 4
    half = width // 2
    nq, nk = wq.shape[1], wk.shape[1]
    qb, kb = nq // steps, nk // steps
    o_spec = lambda n: pl.BlockSpec((tokens, n), lambda i: (0, i))
    shape = jax.ShapeDtypeStruct
    return pallas(
        project_kernel,
        grid=(steps,),
        in_specs=[SCALAR, whole((tokens, width)), whole((1, width)),
                  *weight_specs(half, qb, 0), *weight_specs(half, kb, nq), *weight_specs(half, kb, nq + nk),
                  whole((tokens, LANES)), whole((tokens, LANES))],
        out_specs=[pl.BlockSpec((tokens, width), lambda i: (0, 0)), o_spec(qb), o_spec(kb), o_spec(kb)],
        out_shape=[shape((tokens, width), BF16), shape((tokens, nq), BF16), shape((tokens, nk), BF16),
                   shape((tokens, nk), BF16)],
        compiler_params=params(),
        cost_estimate=cost(0.1),
        name="project",
    )(where, x, gain, wq, *pack, wk, *pack, wv, *pack, cosine, sine)


def project_earlier(where, x, gain, wk, wv, pack, cosine, sine):
    tokens, width = x.shape
    steps = 2
    half = width // 2
    nk = wk.shape[1]
    kb = nk // steps
    o_spec = pl.BlockSpec((tokens, kb), lambda i: (0, i))
    shape = jax.ShapeDtypeStruct
    return pallas(
        project_earlier_kernel,
        grid=(steps,),
        in_specs=[SCALAR, whole((tokens, width)), whole((1, width)),
                  *weight_specs(half, kb, 2 * nk), *weight_specs(half, kb, 3 * nk),
                  whole((tokens, LANES)), whole((tokens, LANES))],
        out_specs=[o_spec, o_spec],
        out_shape=[shape((tokens, nk), BF16), shape((tokens, nk), BF16)],
        scratch_shapes=[pltpu.VMEM((tokens, width), BF16)],
        compiler_params=params(),
        cost_estimate=cost(0.1),
        name="project_earlier",
    )(where, x, gain, wk, *pack, wv, *pack, cosine, sine)


def lane_half(shape, which):
    lane = lax.broadcasted_iota(jnp.int32, shape, 1)
    return ((lane // HEAD) % 2 == which).astype(F32)


def doubled(tile, which):
    kept = tile.astype(F32) * lane_half(tile.shape, which)
    return kept + pltpu.roll(kept, HEAD, 1)


def fill_bias(bias, prefix_ref, g):
    shape = bias.shape
    key = lax.broadcasted_iota(jnp.int32, shape, 0)
    query = lax.broadcasted_iota(jnp.int32, shape, 1)
    seen = (key <= query) | (key + g * shape[0] < prefix_ref[0])
    bias[...] = jnp.where(seen, 0.0, MASKED)


def attend_kernel(g_ref, prefix_ref, q_ref, k0_ref, v0_ref, k1_ref, v1_ref, o_ref, lse_ref, bias):
    g = g_ref[0]
    which = pl.program_id(0) % 2

    @pl.when(pl.program_id(0) == 0)
    def _():
        fill_bias(bias, prefix_ref, g)

    def run(blocks):
        q = q_ref[...].astype(F32)
        keys = [doubled(k[...], which).astype(BF16) for k, _ in blocks]
        values = [doubled(v[...], which).T[:HEAD].astype(BF16) for _, v in blocks]
        outs = []
        for a in range(2):
            qa = (q * lane_half(q.shape, a)).astype(BF16)
            scores = [nt(k, qa) for k in keys]
            scores[0] = scores[0] + bias[...]
            peak = functools.reduce(jnp.maximum, [jnp.max(s, 0, keepdims=True) for s in scores])
            weights = [jnp.exp(s - peak) for s in scores]
            total = sum(jnp.sum(w, 0, keepdims=True) for w in weights)
            out = sum(nn(v, w.astype(BF16)) for v, w in zip(values, weights))
            outs.append(out * (1.0 / total))
            lse_ref[0, a : a + 1, :] = peak + jnp.log(total)
        o_ref[...] = jnp.concatenate(outs, 0).T.astype(BF16)

    @pl.when(g == 0)
    def _():
        run([(k0_ref, v0_ref)])

    @pl.when(g != 0)
    def _():
        run([(k0_ref, v0_ref), (k1_ref, v1_ref)])


def attend(g, prefix, q, k0, v0, k1, v1):
    tokens = q.shape[0]
    kv = pl.BlockSpec((tokens, 128), lambda i: (0, i // 2))
    qs = pl.BlockSpec((tokens, 128), lambda i: (0, i))
    return pallas(
        attend_kernel,
        grid=(KV_HEADS,),
        in_specs=[SCALAR, SCALAR, qs, kv, kv, kv, kv],
        out_specs=[qs, pl.BlockSpec((1, 8, tokens), lambda i: (i, 0, 0))],
        out_shape=[jax.ShapeDtypeStruct(q.shape, BF16), jax.ShapeDtypeStruct((KV_HEADS, 8, tokens), F32)],
        scratch_shapes=[pltpu.VMEM((tokens, tokens), F32)],
        compiler_params=params(),
        cost_estimate=cost(0.1),
        name="attend",
    )(g, prefix, q, k0, v0, k1, v1)


def attend_back_kernel(g_ref, prefix_ref, q_ref, k0_ref, v0_ref, k1_ref, v1_ref, do_ref, lse_ref,
                       cos_ref, sin_ref, dq_ref, own_ref, early_ref, bias):
    g = g_ref[0]
    which = pl.program_id(0) % 2

    @pl.when(pl.program_id(0) == 0)
    def _():
        fill_bias(bias, prefix_ref, g)

    def run(blocks):
        q = q_ref[...].astype(F32)
        do = do_ref[...].astype(F32)
        keys = [doubled(b[0][...], which) for b in blocks]
        keys_t = [k.T[:HEAD].astype(BF16) for k in keys]
        keys = [k.astype(BF16) for k in keys]
        values = [doubled(b[1][...], which).astype(BF16) for b in blocks]
        dks = [0.0 for _ in blocks]
        dvs = [0.0 for _ in blocks]
        dqs = []
        for a in range(2):
            half = lane_half(q.shape, a)
            qa = (q * half).astype(BF16)
            doa = (do * half).astype(BF16)
            lse = lse_ref[0, a : a + 1, :]
            scores = [nt(k, qa) for k in keys]
            scores[0] = scores[0] + bias[...]
            probs = [jnp.exp(s - lse) for s in scores]
            dps = [nt(v, doa) for v in values]
            delta = sum(jnp.sum(p * dp, 0, keepdims=True) for p, dp in zip(probs, dps))
            dq = 0.0
            for n in range(len(blocks)):
                ds = (probs[n] * (dps[n] - delta)).astype(BF16)
                dvs[n] = dvs[n] + nn(probs[n].astype(BF16), doa)
                dks[n] = dks[n] + nn(ds, qa)
                dq = dq + nn(keys_t[n], ds)
            dqs.append(dq)
        dq = jnp.concatenate(dqs, 0).T * (1.0 / math.sqrt(HEAD))
        dq_ref[...] = rotated(dq, cos_ref[...], sin_ref[...], -1.0).astype(BF16)
        for n, (_, _, outs) in enumerate(blocks):
            for ref, grad in zip(outs, (dks[n], dvs[n])):
                both = grad + pltpu.roll(grad, HEAD, 1)
                part = both * lane_half(both.shape, which)

                @pl.when(which == 0)
                def _():
                    ref[...] = part.astype(ref.dtype)

                @pl.when(which != 0)
                def _():
                    ref[...] = (ref[...].astype(F32) + part).astype(ref.dtype)

    own = (k0_ref, v0_ref, (own_ref.at[0], own_ref.at[1]))
    earlier = (k1_ref, v1_ref, (early_ref.at[0], early_ref.at[1]))

    @pl.when(g == 0)
    def _():
        run([own])
        early_ref[...] = jnp.zeros_like(early_ref)

    @pl.when(g != 0)
    def _():
        run([own, earlier])


def attend_back(g, prefix, q, k0, v0, k1, v1, do, lse, cosine, sine, first, count):
    tokens = q.shape[0]
    kv = pl.BlockSpec((tokens, LANES), lambda i: (0, first // 2 + i // 2))
    qs = pl.BlockSpec((tokens, LANES), lambda i: (0, first + i))
    both = pl.BlockSpec((2, tokens, LANES), lambda i: (0, 0, i // 2))
    shape = jax.ShapeDtypeStruct
    kv_shape = (2, tokens, count * HEAD)
    return pallas(
        attend_back_kernel,
        grid=(count,),
        in_specs=[SCALAR, SCALAR, qs, kv, kv, kv, kv, qs,
                  pl.BlockSpec((1, 8, tokens), lambda i: (first + i, 0, 0)),
                  whole((tokens, LANES)), whole((tokens, LANES))],
        out_specs=[pl.BlockSpec((tokens, LANES), lambda i: (0, i)), both, both],
        out_shape=[shape((tokens, count * LANES), BF16), shape(kv_shape, F32), shape(kv_shape, BF16)],
        scratch_shapes=[pltpu.VMEM((tokens, tokens), F32)],
        compiler_params=params(),
        cost_estimate=cost(0.1),
        name="attend_back",
    )(g, prefix, q, k0, v0, k1, v1, do, lse, cosine, sine)


def output_kernel(where_ref, a_ref, wo0, wo1, wo2, x_ref, gain_ref, res_ref, n_ref):
    res = x_ref[...].astype(F32) + project_rows(a_ref, where_ref, (wo0, wo1, wo2))
    res_ref[...] = res
    scale = lax.rsqrt(jnp.mean(res * res, -1, keepdims=True) + EPSILON)
    n_ref[...] = (res * scale * gain_ref[...]).astype(BF16)


def output(where, attended, wo, x, gain):
    tokens, width = x.shape
    rows = 256
    row = pl.BlockSpec((rows, width), lambda i: (i, 0))
    return pallas(
        output_kernel,
        grid=(tokens // rows,),
        in_specs=[SCALAR, row, *(whole(w.shape) for w in wo), row, whole((1, width))],
        out_specs=[row, row],
        out_shape=[jax.ShapeDtypeStruct((tokens, width), F32), jax.ShapeDtypeStruct((tokens, width), BF16)],
        compiler_params=params(),
        cost_estimate=cost(0.1),
        name="output",
    )(where, attended, *wo, x, gain)


def gates_of(rows, router_t, member):
    logits = jnp.where(member > 0.0, nt(rows, router_t), MASKED)
    peak = jnp.max(logits, -1, keepdims=True)
    weights = jnp.where(member > 0.0, jnp.exp(logits - peak), 0.0)
    return weights / jnp.sum(weights, -1, keepdims=True)


def experts_kernel(*refs, first, start, adding, carrying, final):
    refs = list(refs)
    take = lambda n: [refs.pop(0) for _ in range(n)]
    g_ref, x, c = take(3)
    if first:
        member, router, order = take(3)
    else:
        gates, xt, ct = take(3)
    win, wout = take(2)
    keep_in, send_in = take(2) if adding else (None, None)
    grad_in, sum_in, gg_in = take(3) if carrying else (None, None, None)
    keep, send, grad, total = take(4)
    gg_out = None if final else take(1)[0]
    if first:
        gates, xt, ct = take(3)
    hid_scr, dgu_scr, grad_scr, sum_scr, gg_scr = take(5)
    step = pl.program_id(0)
    width = x.shape[1]
    column = g_ref[0] * (EXPERTS // 2) + start + step

    @pl.when(step == 0)
    def _():
        if first:
            gates[...] = gates_of(x[...], router[...], member[...])
            xt[...] = nt(order[...], x[...]).astype(BF16)
            ct[...] = nt(order[...], c[...]).astype(BF16)
        gg_scr[...] = gg_in[...] if carrying else jnp.zeros_like(gg_scr)

    probs = gates[...]
    mine = lax.broadcasted_iota(jnp.int32, probs.shape, 1) == column
    p = jnp.sum(jnp.where(mine, probs, 0.0), 1, keepdims=True)
    gate_up = nn(x[...], win[0])
    back = nn(c[...], wout[0])
    gate, up = gate_up[:, :FF], gate_up[:, FF:]
    sig = 1.0 / (1.0 + jnp.exp(-gate))
    act = gate * sig
    hid = act * up
    gg_scr[...] = jnp.where(mine, jnp.sum(hid * back, 1, keepdims=True), gg_scr[...])
    back = back * p
    dgate = back * up * (sig * (1.0 + gate * (1.0 - sig)))
    hid_scr[...] = (hid * p).astype(BF16)
    dgu_scr[:, :FF] = dgate.astype(BF16)
    dgu_scr[:, FF:] = (back * act).astype(BF16)
    for scr, old, value in ((sum_scr, sum_in, nt(hid_scr[...], wout[0])), (grad_scr, grad_in, nt(dgu_scr[...], win[0]))):

        @pl.when(step == 0)
        def _():
            scr[...] = value + old[...] if carrying else value

        @pl.when(step != 0)
        def _():
            scr[...] += value

    for out, old, base in ((keep, keep_in, 0), (send, send_in, width // 2)):
        rows = pl.ds(base, width // 2)
        for cols, left, right in ((slice(0, 2 * FF), xt, dgu_scr), (slice(2 * FF, 3 * FF), ct, hid_scr)):
            value = nn(left[rows], right[...])
            if adding:
                value = value + old[0, :, cols].astype(F32)
            out[0, :, cols] = value.astype(BF16)

    @pl.when(step == pl.num_programs(0) - 1)
    def _():
        total[...] = sum_scr[...].astype(total.dtype)
        if final:
            grad[:, :width] = grad_scr[...].astype(BF16)
            grad[:, width:] = gg_scr[...].astype(BF16)
        else:
            grad[...] = grad_scr[...]
            gg_out[...] = gg_scr[...]


def experts(g, x, c, win, wout, start, count, fresh=None, known=None, adding=None, carrying=None, final=False):
    tokens, width = x.shape
    cols = 3 * FF
    shape = jax.ShapeDtypeStruct
    half = pl.BlockSpec((1, width // 2, cols), lambda i: (i, 0, 0))
    wide, narrow = (tokens, width), (tokens, LANES)
    args = [g, x, c]
    specs = [SCALAR, whole(wide), whole(wide)]
    for a in fresh or known:
        args.append(a)
        specs.append(whole(a.shape))
    args += [win, wout]
    specs += [pl.BlockSpec((1, width, 2 * FF), lambda i: (start + i, 0, 0)),
              pl.BlockSpec((1, width, FF), lambda i: (start + i, 0, 0))]
    if adding:
        args += adding
        specs += [half, half]
    if carrying:
        args += carrying
        specs += [whole(wide), whole(wide), whole(narrow)]
    outs = [half, half]
    shapes = [shape((count, width // 2, cols), BF16), shape((count, width // 2, cols), BF16)]
    ends = [((tokens, width + LANES), BF16), (wide, BF16)] if final else [(wide, F32), (wide, F32), (narrow, F32)]
    if fresh:
        ends += [(narrow, F32), ((width, tokens), BF16), ((width, tokens), BF16)]
    outs += [whole(size) for size, _ in ends]
    shapes += [shape(size, kind) for size, kind in ends]
    return pallas(
        functools.partial(experts_kernel, first=fresh is not None, start=start, adding=adding is not None,
                          carrying=carrying is not None, final=final),
        grid=(count,),
        in_specs=specs,
        out_specs=outs,
        out_shape=shapes,
        scratch_shapes=[pltpu.VMEM((tokens, FF), BF16), pltpu.VMEM((tokens, 2 * FF), BF16),
                        pltpu.VMEM(wide, F32), pltpu.VMEM(wide, F32), pltpu.VMEM(narrow, F32)],
        compiler_params=params(60),
        cost_estimate=cost(8 * count),
        name="experts",
    )(*args)


def middle_kernel(where_ref, c_ref, grad_ref, back_ref, gg_ref, p_ref, router_ref, res_ref, gain_ref,
                  wo0, wo1, wo2, dres_ref, low_ref, da_ref, dl_ref, dgain_ref):
    width = c_ref.shape[1]
    p = p_ref[...]
    gg = gg_ref[...] + back_ref[:, width:].astype(F32)
    dlogits = p * (gg - jnp.sum(p * gg, 1, keepdims=True))
    dl_ref[...] = dlogits.astype(BF16)
    high = dlogits.astype(BF16)
    rest = (dlogits - high.astype(F32)).astype(BF16)
    router = router_ref[...]
    grad = grad_ref[...] + back_ref[:, :width].astype(F32) + (nn(high, router) + nn(rest, router))
    res = res_ref[...]
    scale = lax.rsqrt(jnp.mean(res * res, -1, keepdims=True) + EPSILON)
    part = jnp.broadcast_to(jnp.sum(grad * (res * scale), 0, keepdims=True), dgain_ref.shape)

    @pl.when(pl.program_id(0) == 0)
    def _():
        dgain_ref[...] = part

    @pl.when(pl.program_id(0) != 0)
    def _():
        dgain_ref[...] += part

    w = grad * gain_ref[...]
    dres = c_ref[...].astype(F32) + (scale * w - res * (scale * scale * scale)
                                     * jnp.mean(w * res, -1, keepdims=True))
    dres_ref[...] = dres
    low = dres.astype(BF16)
    low_ref[...] = low
    for at, wo in zip(pieces(where_ref, width), (wo0, wo1, wo2)):
        da_ref[:, at] = nt(low, wo[...]).astype(BF16)


def middle(where, c, grad, back, gg, p, router_t, res, gain, wo):
    tokens, width = c.shape
    rows = 256
    row = lambda n: pl.BlockSpec((rows, n), lambda i: (i, 0))
    shape = jax.ShapeDtypeStruct
    return pallas(
        middle_kernel,
        grid=(tokens // rows,),
        in_specs=[SCALAR, row(width), row(width), row(width + LANES), row(LANES), row(LANES),
                  whole((LANES, width)), row(width), whole((1, width)), *(whole(w.shape) for w in wo)],
        out_specs=[row(width), row(width), row(width), row(LANES), pl.BlockSpec((8, width), lambda i: (0, 0))],
        out_shape=[shape((tokens, width), F32), shape((tokens, width), BF16), shape((tokens, width), BF16),
                   shape((tokens, LANES), BF16), shape((8, width), F32)],
        compiler_params=params(),
        cost_estimate=cost(100),
        name="middle",
    )(where, c, grad, back, gg, p, router_t, res, gain, *wo)


def weight_kernel(*refs, joined, pieces_sent):
    refs = list(refs)
    take = lambda n: [refs.pop(0) for _ in range(n)]
    xt, dq, own, early, cos, sin = take(6)
    order, low, att, xt_ffn, dlogits, dgain = take(6) if joined else [None] * 6
    keep, dkv = take(2)
    sends = take(pieces_sent)
    half = keep.shape[0]
    dk = rotated(own[0] + early[0].astype(F32), cos[...], sin[...], -1.0).astype(BF16)
    dv = (own[1] + early[1].astype(F32)).astype(BF16)
    nq, nk = dq.shape[1], dk.shape[1]
    dkv[:, :nk] = dk
    dkv[:, nk:] = dv
    if joined:
        low_t, gain_rows = take(2)
        low_t[...] = nt(order[...], low[...]).astype(BF16)
        row = lax.broadcasted_iota(jnp.int32, gain_rows.shape, 0)
        gain_rows[...] = jnp.where(row == EXPERTS, dgain[0:1, :], 0.0).astype(BF16)
    def put(cols, rows, value):
        value = value.astype(BF16)
        if rows.start == 0:
            keep[:, cols] = value
        else:
            size = half // pieces_sent
            for n, send in enumerate(sends):
                send[:, cols] = value[n * size : (n + 1) * size]

    for base in (0, half):
        rows = pl.ds(base, half)
        put(slice(0, nq), rows, nn(xt[rows], dq[...]))
        first = nq + 2 * nk
        put(slice(nq, first), rows, nn(xt[rows], dkv[...]))
        if joined:
            wide = att.shape[1]
            put(slice(first, first + wide), rows, nn(low_t[rows], att[...]))
            put(slice(first + wide, first + wide + LANES), rows,
                nn(xt_ffn[rows], dlogits[...]) + nt(order[rows], gain_rows[...]))


def weight_grads(xt, dq, own, early, cosine, sine, pieces_sent, joined=None):
    width, tokens = xt.shape
    nq, nk = dq.shape[1], own.shape[2]
    shape = jax.ShapeDtypeStruct
    cols = nq + 2 * nk + (joined[2].shape[1] + LANES if joined else 0)
    out = shape((width // 2, cols), BF16)
    vmem = pl.BlockSpec(memory_space=pltpu.VMEM)
    args = (xt, dq, own, early, cosine, sine, *(joined or ()))
    sent = shape((width // 2 // pieces_sent, cols), BF16)
    return pallas(
        functools.partial(weight_kernel, joined=bool(joined), pieces_sent=pieces_sent),
        in_specs=[vmem] * len(args),
        out_specs=[vmem] * (2 + pieces_sent),
        out_shape=[out, shape((tokens, 2 * nk), BF16)] + [sent] * pieces_sent,
        scratch_shapes=[pltpu.VMEM((width, tokens), BF16), pltpu.VMEM((LANES, width), BF16)] if joined else [],
        compiler_params=params(),
        cost_estimate=cost(0.1),
        name="weight_grads",
    )(*args)


def input_kernel(where_ref, *refs, parts):
    refs = list(refs)
    take = lambda n: [refs.pop(0) for _ in range(n)]
    dqs, dkvs, wq, wk, wv = take(parts), take(parts), take(1), take(1), take(1)
    packs = take(2)
    x_ref, gain_ref, dres_ref, out_ref, grad = refs
    nq, nk = wq[0].shape[1], wk[0].shape[1]
    columns = []
    for n in range(parts):
        q0, k0 = n * nq // parts, n * nk // parts
        q1, k1 = q0 + nq // parts, k0 + nk // parts
        dkv = dkvs[n][...]
        half = dkv.shape[1] // 2
        for left, own, first, (lo, hi) in (
                (dqs[n][...], wq[0], 0, (q0, q1)),
                (dkv[:, :half], wk[0], nq, (k0, k1)),
                (dkv[:, half:], wv[0], nq + nk, (k0, k1))):
            columns.append((left, own, slice(lo, hi), slice(first + lo, first + hi)))
    at = pieces(where_ref, x_ref.shape[1])
    grad[:, at[0]] = sum(nt(left, own[:, mine]) for left, own, mine, _ in columns)
    for place, pack in zip(at[1:], packs):
        grad[:, place] = sum(nt(left, pack[:, packed]) for left, _, _, packed in columns)
    x = x_ref[...].astype(F32)
    scale = lax.rsqrt(jnp.mean(x * x, -1, keepdims=True) + EPSILON)
    w = grad[...] * gain_ref[...]
    out_ref[...] = dres_ref[...] + (scale * w - x * (scale * scale * scale) * jnp.mean(w * x, -1, keepdims=True))


def input_grads(where, dqs, dkvs, wq, wk, wv, pack, x, gain, dres):
    tokens, width = x.shape
    rows = 256
    row = lambda a: pl.BlockSpec((rows, a.shape[1]), lambda i: (i, 0))
    weights = (wq, wk, wv, *pack)
    return pallas(
        functools.partial(input_kernel, parts=len(dqs)),
        grid=(tokens // rows,),
        in_specs=[SCALAR, *map(row, dqs), *map(row, dkvs), *(whole(w.shape) for w in weights), row(x),
                  whole((1, width)), row(dres)],
        out_specs=row(dres),
        out_shape=jax.ShapeDtypeStruct((tokens, width), F32),
        scratch_shapes=[pltpu.VMEM((rows, width), F32)],
        compiler_params=params(),
        cost_estimate=cost(0.1),
        name="input_grads",
    )(where, *dqs, *dkvs, *weights, x, gain, dres)


def exchange(value, *bits):
    count = lax.axis_size("replica")
    flip = sum(count if b == "group" else 1 << b for b in bits)
    return lax.ppermute(value, ("group", "replica"), [(i, i ^ flip) for i in range(2 * count)])


def after(value, *others):
    out = lax.optimization_barrier((value, *others))
    return out[0], list(out[1:])


def deal(out, to, entries, rows):
    at = 0
    finest = min(p.shape[1] for part, _ in entries for p in part)
    for start, total in rows:
        for first in range(start, start + total, min(finest, total)):
            size = min(finest - first % finest, start + total - first)
            value = 0.0
            for part, e in entries:
                height = part[0].shape[1]
                inner = first % height
                value = value + part[first // height][e, inner : inner + size, :].astype(F32)
            out[to, at : at + size, :] = value.astype(BF16)
            at += size


def split_kernel(*refs, groups, ranges):
    refs = list(refs)
    parts = [[[refs.pop(0) for _ in range(n)] for n in counts] for counts, _, _ in groups]
    to = 0
    for group, (_, first, count) in zip(parts, groups):
        for n in range(count):
            entries = [(p, n + (first if p[0].shape[0] > count else 0)) for p in group]
            for out, rows in zip(refs, ranges):
                deal(out, to, entries, rows)
            to += 1


def stream_kernel(*refs, count, pieces):
    parts, outs = [[r] for r in refs[:count]], list(refs[count:])
    for first, size, ranges in pieces:
        mine = [outs.pop(0) for _ in ranges]

        @pl.when((pl.program_id(0) >= first) & (pl.program_id(0) < first + size))
        def _():
            for out, rows in zip(mine, ranges):
                deal(out, 0, [(p, 0) for p in parts], rows)


def ranges_of(axes, chunk, bits):
    spots = np.stack(np.unravel_index(np.arange(2 ** len(axes)), (2,) * len(axes)), 1)
    at = [axes.index(b) for b in bits]
    ranges = []
    for combo in np.ndindex(*(2,) * len(bits)):
        rows = []
        for n in np.nonzero((spots[:, at] == combo).all(1))[0]:
            if rows and rows[-1][0] + rows[-1][1] == n * chunk:
                rows[-1] = (rows[-1][0], rows[-1][1] + chunk)
            else:
                rows.append((int(n) * chunk, chunk))
        ranges.append(tuple(rows))
    return tuple(ranges)


def flips_of(bits):
    return [[b for b, on in zip(bits, combo) if on] for combo in list(np.ndindex(*(2,) * len(bits)))[1:]]


class Run:
    def __init__(self, parts, axes, chunk, first=0, count=1):
        self.parts, self.axes, self.chunk, self.first, self.count = list(parts), list(axes), chunk, first, count


def split(runs, *bits):
    axes, chunk = runs[0].axes, runs[0].chunk
    ranges = ranges_of(axes, chunk, bits)
    cols = runs[0].parts[0].shape[2]
    total = sum(r.count for r in runs)
    flat = lambda part: list(part) if isinstance(part, (list, tuple)) else [part]
    args = [a for r in runs for p in r.parts for a in flat(p)]
    vmem = pl.BlockSpec(memory_space=pltpu.VMEM)
    kept, *sends = pallas(
        functools.partial(
            split_kernel, ranges=ranges,
            groups=tuple((tuple(len(flat(p)) for p in r.parts), r.first, r.count) for r in runs)),
        in_specs=[vmem] * len(args),
        out_specs=[vmem] * len(ranges),
        out_shape=[jax.ShapeDtypeStruct((total, sum(n for _, n in rows), cols), BF16) for rows in ranges],
        compiler_params=params(),
        cost_estimate=cost(0.1),
        name="split",
    )(*args)
    return Run([kept, *(exchange(s, *flip) for s, flip in zip(sends, flips_of(bits)))],
               [b for b in axes if b not in bits], chunk, 0, total)


def split_apart(run, *pieces):
    rows, cols = run.parts[0].shape[1:]
    shapes, specs, plan, first = [], [], [], 0
    for bits, count in pieces:
        ranges = ranges_of(run.axes, run.chunk, bits)
        plan.append((first, count, ranges))
        for chosen in ranges:
            size = sum(n for _, n in chosen)
            shapes.append(jax.ShapeDtypeStruct((count, size, cols), BF16))
            specs.append(pl.BlockSpec(
                (1, size, cols), lambda i, first=first, count=count: (jnp.clip(i - first, 0, count - 1), 0, 0)))
        first += count
    outs = list(pallas(
        functools.partial(stream_kernel, count=len(run.parts), pieces=tuple(plan)),
        grid=(first,),
        in_specs=[pl.BlockSpec((1, rows, cols), lambda i: (i, 0, 0))] * len(run.parts),
        out_specs=specs,
        out_shape=shapes,
        compiler_params=params(),
        cost_estimate=cost(0.1),
        name="split_apart",
    )(*run.parts))
    runs = []
    for bits, count in pieces:
        kept = outs.pop(0)
        received = [exchange(outs.pop(0), *flip) for flip in flips_of(bits)]
        runs.append(Run([kept, *received], [b for b in run.axes if b not in bits], run.chunk, 0, count))
    return runs


def finish_attention_kernel(*refs, counts):
    refs = list(refs)
    take = lambda n: [refs.pop(0) for _ in range(n)]
    joined, alone = take(counts[0]), take(counts[1])
    wq, wk, wv, gain = take(4)
    dq, dk, dv, do, drouter, dgain_attn, dgain_ffn = refs
    a = sum(p[0].astype(F32) for p in joined)
    b = sum(p[0].astype(F32) for p in alone)
    nq, nk = wq.shape[1] // 2, wk.shape[1] // 2
    dgain = 0.0
    for n, part in enumerate((a, b)):
        for ref, w, size, first in ((dq, wq, nq, 0), (dk, wk, nk, nq), (dv, wv, nk, nq + nk)):
            grad = part[:, first : first + size]
            ref[:, n * size : (n + 1) * size] = grad
            dgain = dgain + jnp.sum(grad * w[:, n * size : (n + 1) * size].astype(F32), 1, keepdims=True)
    dgain_attn[...] = dgain / gain[...]
    first = nq + 2 * nk
    width = do.shape[0]
    do[...] = a[:, first : first + width].T
    last = a[:, first + width :]
    drouter[...] = last[:, :EXPERTS]
    lane = lax.broadcasted_iota(jnp.int32, last.shape, 1)
    dgain_ffn[...] = jnp.sum(jnp.where(lane == EXPERTS, last, 0.0), 1, keepdims=True)


def finish_attention(joined, alone, wq, wk, wv, gain, width):
    chunk = wq.shape[0]
    shape = lambda *s: jax.ShapeDtypeStruct(s, F32)
    args = (*joined, *alone, wq, wk, wv, gain)
    vmem = pl.BlockSpec(memory_space=pltpu.VMEM)
    return pallas(
        functools.partial(finish_attention_kernel, counts=(len(joined), len(alone))),
        in_specs=[vmem] * len(args),
        out_specs=[vmem] * 7,
        out_shape=[shape(chunk, wq.shape[1]), shape(chunk, wk.shape[1]), shape(chunk, wv.shape[1]),
                   shape(width, chunk), shape(chunk, EXPERTS), shape(chunk, 1), shape(chunk, 1)],
        compiler_params=params(),
        cost_estimate=cost(0.1),
        name="finish_attention",
    )(*args)


def finish_experts_kernel(g_ref, *refs):
    own, other, (win, wout) = refs[: len(refs) // 2 - 1], refs[len(refs) // 2 - 1 : -2], refs[-2:]
    count = win.shape[0] // 2
    g = g_ref[0]
    for parts, side in ((own, g), (other, 1 - g)):
        e = 0
        for p in parts:
            for n in range(p.shape[0]):
                win[side * count + e] = p[n, :, : 2 * FF].astype(F32)
                wout[side * count + e] = p[n, :, 2 * FF :].astype(F32)
                e += 1


def finish_experts(g, own, other):
    chunk = own[0].shape[1]
    shape = lambda *s: jax.ShapeDtypeStruct(s, F32)
    vmem = pl.BlockSpec(memory_space=pltpu.VMEM)
    return pallas(
        finish_experts_kernel,
        in_specs=[SCALAR] + [vmem] * (2 * len(own)),
        out_specs=[vmem] * 2,
        out_shape=[shape(EXPERTS, chunk, 2 * FF), shape(EXPERTS, chunk, FF)],
        compiler_params=params(),
        cost_estimate=cost(0.1),
        name="finish_experts",
    )(g, *own, *other)


def on_device(
    block_in, attn_gain, query_weight, key_weight, value_weight, out_weight, ffn_gain, router_weight,
    expert_in, expert_out, routes, prefix, cotangent,
):
    FOLLOWED.clear()
    replicas = lax.axis_size("replica")
    bits = replicas.bit_length() - 1
    tokens, width = block_in.shape[1:]
    half = width // 2
    chunk = half // replicas
    group, replica = lax.axis_index("group"), lax.axis_index("replica")
    core = replica % 2
    g = group.astype(jnp.int32).reshape(1)
    where = jnp.stack([group, core]).astype(jnp.int32)
    x, cot = block_in[0], cotangent[0]
    swap = lambda v: exchange(v, "group")

    def ordered(own, other, axis):
        return jnp.where(group == 0, jnp.concatenate([own, other], axis), jnp.concatenate([other, own], axis))

    quarter = lambda w: lax.dynamic_slice_in_dim(w, core * (w.shape[0] // 2), w.shape[0] // 2, 0)
    pack_send = jnp.concatenate([quarter(query_weight), quarter(key_weight), quarter(value_weight)], 1)
    pack = swap(pack_send)
    small = jnp.concatenate([attn_gain[None], ffn_gain[None], router_weight.T], 0)
    vectors = ordered(small, swap(small), 1)
    gain_attn, gain_ffn = vectors[0:1].astype(F32), vectors[1:2].astype(F32)
    router_t = jnp.concatenate([vectors[2:], jnp.zeros((LANES - EXPERTS, width), BF16)], 0)
    lanes = jnp.arange(LANES, dtype=jnp.int32)
    member = (routes[0][:, :, None] == lanes[None, None, :]).any(1).astype(F32)

    frequency = THETA_BASE ** (-jnp.arange(HEAD // 2, dtype=F32) * 2.0 / HEAD)

    def tables(first):
        angles = (first + jnp.arange(tokens, dtype=jnp.int32)).astype(F32)[:, None] * frequency[None, :]
        cosine, sine = jnp.cos(angles), jnp.sin(angles)
        return jnp.tile(cosine, (1, 4)), jnp.concatenate([-sine, sine, -sine, sine], 1)

    cosine, sine = tables(group * tokens)
    early_tables = tables(0)
    place = np.arange(width)
    blocks, inner = place // chunk, place % chunk
    reverse = np.zeros_like(blocks)
    for b in range(bits):
        reverse |= ((blocks >> 1 >> (bits - 1 - b)) & 1) << b
    feature = ((jnp.asarray(blocks & 1, jnp.int32) ^ group) * half
               + (jnp.asarray(reverse, jnp.int32) ^ replica) * chunk + jnp.asarray(inner, jnp.int32))
    order = (feature[:, None] == jnp.arange(width, dtype=jnp.int32)[None, :]).astype(BF16)

    mine = lambda a: lax.dynamic_slice_in_dim(a, replica * chunk, chunk, 0)
    rows = (mine(query_weight), mine(key_weight), mine(value_weight), mine(attn_gain).astype(F32)[:, None])
    pack, (cosine, sine, member, order, x_send, gain_attn, wo_send, cot_send, *more) = after(
        pack, cosine, sine, member, order, x, gain_attn, quarter(out_weight), cot, *early_tables, *rows)
    early_tables, rows = more[:2], more[2:]
    x_early = lax.ppermute(x_send, "group", [(0, 1)])
    pack = (pack, exchange(pack, 0))

    normed_attn, q, k, v = project(where, x, gain_attn, query_weight, key_weight, value_weight, pack, cosine, sine)
    normed_t = nt(order, normed_attn).astype(BF16)
    x_early, (q, normed_t) = after(x_early, q, normed_t)
    wo = swap(wo_send)
    cot_other = swap(cot_send)
    k1, v1 = project_earlier(where, x_early, gain_attn, key_weight, value_weight, pack, *early_tables)
    attended, lse = attend(g, prefix, q, k, v, k1, v1)
    wo, (attended,) = after(wo, attended)
    wo = (out_weight, wo, exchange(wo, 0))
    residual, normed = output(where, attended, wo, x, gain_ffn)
    member_other = swap(member.astype(BF16)).astype(F32)
    normed, (cot_other, member_other) = after(normed, cot_other, member_other)
    normed_other = swap(normed)
    count = expert_in.shape[0] // 2
    near = lambda *a, **k: experts(g, normed, cot, expert_in, expert_out, *a, **k)
    far = lambda *a, **k: experts(g, *a[0], expert_in, expert_out, *a[1:], **k)
    keep, send, grad_own, sum_own, gg_own, *known = near(0, count, fresh=(member, router_t, order))
    gates, xt_own, _ = known
    normed_other, (keep,) = after(normed_other, keep)
    keep_a, send_a, *sums, gates_o, xt_o, ct_o = far(
        (normed_other, cot_other), 0, count, fresh=(member_other, router_t, order), adding=(keep, send))
    received_a = exchange(send_a, 0)
    keep, send, back, sum_other = far(
        (normed_other, cot_other), count, count, known=(gates_o, xt_o, ct_o), carrying=sums, final=True)
    back = swap(back)
    dims = [*range(1, bits), "group"]
    two = count // 2
    first, second, *rest = [*range(1, bits)]
    run_a = Run((keep_a, received_a), dims, chunk, 0, count)
    run0, run1 = split_apart(run_a, ((first,), two), ((second,), two))
    keep_b, send_b, grad_own, sum_own, gg_own = near(
        count, count, known=known, adding=(keep, send), carrying=(grad_own, sum_own, gg_own))
    back, (keep_b, sum_send) = after(back, keep_b, sum_other)
    run_b = Run((keep_b, exchange(send_b, 0)), dims, chunk, 0, count)
    sum_other = swap(sum_send)
    run0, run1 = split([run0], second), split([run1], first)

    grad_res, grad_low, grad_att, grad_logits, grad_gain = middle(
        where, cot, grad_own, back, gg_own, gates, router_t, residual, gain_ffn, wo)
    run2, run3 = split_apart(run_b, ((first,), two), ((second,), two))
    heads = KV_HEADS // 2
    attn = lambda first: attend_back(g, prefix, q, k, v, k1, v1, grad_att, lse, cosine, sine, first, heads)
    to_earlier = lambda a: lax.ppermute(a, "group", [(1, 0)])
    dq0, own0, early0 = attn(0)
    early0 = to_earlier(early0)
    FOLLOWED.append(sum_other)
    for bit in rest:
        run0, run1 = split([run0], bit), split([run1], bit)
    dq1, own1, early1 = attn(heads)
    early1 = to_earlier(early1)
    run2, run3 = split([run2], second), split([run3], first)
    one = lambda keep, sends: Run((keep[None], [exchange(s, 0)[None] for s in sends]), dims, chunk)
    keep0, dkv0, *sends = weight_grads(
        normed_t, dq0, own0, early0, cosine, sine, 1,
        joined=(order, grad_low, attended, xt_own, grad_logits, grad_gain))
    attn0 = one(keep0, sends)
    pairs = lambda *bits: [bits[i : i + 2] for i in range(0, len(bits), 2)]
    pairs0, pairs1 = pairs(second, first, "group", *rest), pairs("group", second, first, *rest)
    attn0 = split([attn0], *pairs0[0])
    keep1, dkv1, *sends = weight_grads(normed_t, dq1, own1, early1, cosine, sine, 1)
    attn1 = one(keep1, sends)
    swap_a = split([run0, run1], "group")
    input_grad = input_grads(where, (dq0, dq1), (dkv0, dkv1), query_weight, key_weight, value_weight, pack,
                             x, gain_attn, grad_res)
    attn1 = split([attn1], *pairs1[0])
    for bit in rest:
        run2, run3 = split([run2], bit), split([run3], bit)
    for pair0, pair1 in zip(pairs0[1:], pairs1[1:]):
        attn0 = split([attn0], *pair0)
        attn1 = split([attn1], *pair1)
    swap_b = split([run2, run3], "group")
    block_out = (residual + sum_own + sum_other.astype(F32)).astype(BF16)

    query_grad, key_grad, value_grad, out_grad, router_grad, attn_gain_grad, ffn_gain_grad = finish_attention(
        attn0.parts, attn1.parts, *rows, width)
    expert_in_grad, expert_out_grad = finish_experts(
        g, (swap_a.parts[0], swap_b.parts[0]), (swap_a.parts[1], swap_b.parts[1]))
    return (
        block_out[None], input_grad[None], attn_gain_grad[:, 0], query_grad, key_grad, value_grad, out_grad,
        ffn_gain_grad[:, 0], router_grad, expert_in_grad, expert_out_grad,
    )


def solution(mesh):
    placed = (
        P("replica", "group", None),
        P("group"),
        P("group", None),
        P("group", None),
        P("group", None),
        P("group", None),
        P("group"),
        P("group", None),
        P("group", None, None),
        P("group", None, None),
        P("replica", "group", None),
        P("replica"),
        P("replica", "group", None),
    )
    both = ("group", "replica")
    return jax.shard_map(
        on_device,
        mesh=mesh,
        in_specs=placed,
        out_specs=(
            P("replica", "group", None),
            P("replica", "group", None),
            P(both),
            P(both, None),
            P(both, None),
            P(both, None),
            P(None, both),
            P(both),
            P(both, None),
            P(None, both, None),
            P(None, both, None),
        ),
        check_vma=False,
    )
```

time: 701 us -> 491 us (0.70)
  waiting for transfers between devices: 295 us -> 159 us
  local copies, waits for them, and re-layouts: 77.5 us -> 30.3 us
  Pallas kernels: 180 us -> 218 us
  other arithmetic: 45.5 us -> 15.5 us
  starting transfers between devices: 74.5 us -> 54 us
  matrix products: 20.4 us -> 2.3 us
    ppermute x52 -> x41, waiting for transfers between devices: 286 us -> 142 us  [the longest x40 136 us: exchange(): lax.ppermute(value, ('group', 'replica'), [(i, i ^ flip) for i in range(2...]
    pallas_call x8 -> x32, Pallas kernels: 180 us -> 218 us  [call(): pl.pallas_call(body, in_specs=[*in_specs, *[pl.BlockSpec(memory_space=pl....]
    slice x24 -> x1, local copies, waits for them, and re-layouts: 37.2 us -> 0.01 us  [on_device(): vectors[2:]]
    ppermute x52 -> x41, starting transfers between devices: 71.8 us -> 51.2 us  [the longest x40 46.3 us: exchange(): lax.ppermute(value, ('group', 'replica'), [(i, i ^ flip) for i in range(2...]
    convert_element_type x36 -> x6, other arithmetic: 21.6 us -> 3.19 us  [the longest x1 1.73 us: on_device(): (feature[:, None] == jnp.arange(width, dtype=jnp.int32)[None, :]).astype(...]
    dot_general x5 -> x1, matrix products: 16.3 us -> 2.3 us  [nt(): lax.dot_general(left, right, (((1,), (1,)), ((), ())), preferred_element_...]
    add x18 -> x0, other arithmetic: 9.97 us -> none  [the longest x10 5.52 us: halving(): return sum((p.astype(F32) for p in parts))]
    ppermute x2, waiting for transfers between devices: 9.26 us -> 16.7 us  [on_device(): to_earlier = lambda a: lax.ppermute(a, 'group', [(1, 0)])]
  transfers between devices with their start and end apart: 54 -> 43, of which waited for: 34 -> 17; matrix products, arithmetic and copies ran while one was open for 16% -> 5% of each run, Pallas kernels for 8% -> 36%
where the time goes in v2:
time: 491 us; the launch traced here: 482 us
  Pallas kernels  218 us (44%)
  waiting for transfers between devices  159 us (32%)
  starting transfers between devices  54 us (11%)
  local copies, waits for them, and re-layouts  30.3 us (6%)
  other arithmetic  15.5 us (3%)
    pallas_call x32, Pallas kernels, call(): pl.pallas_call(body, in_specs=[*in_specs, *[pl.BlockSpec(memory_space=pl....  218 us
    ppermute x40, waiting for transfers between devices, exchange(): lax.ppermute(value, ('group', 'replica'), [(i, i ^ flip) for i in range(2...  136 us
    ppermute x40, starting transfers between devices, exchange(): lax.ppermute(value, ('group', 'replica'), [(i, i ^ flip) for i in range(2...  46.3 us
    unnamed x162, local copies, waits for them, and re-layouts  20.5 us
    ppermute x2, waiting for transfers between devices, on_device(): to_earlier = lambda a: lax.ppermute(a, 'group', [(1, 0)])  16.7 us
  transfers between devices with their start and end apart: 43, of which 17 were waited for; matrix products, arithmetic and copies ran while one was open for 5% of the time, Pallas kernels for 36%

profile of v2, /device:TPU:28, one launch (start us, length us, event | category | flops | bytes accessed | tf_op | source)
XLA Modules:
  0.0 482.0 jit_solution(8107615345437716566)
XLA Ops:
  6.4 2.9 fusion.1
  11.7 1.9 fusion.4
  16.2 1.7 fusion.refs_5_.refs_6_
  19.4 10.3 %collective-permute-done.1 = bf16[18,512]{1,0:T(8,128)(2,1)S(1)} collective-permute-done((bf16[18,512]{1,0:T(8,128)(2,1)S(1)}, bf16[18,512]{1,0:T(8,128)(2,1)S(1)}, u32[]{:S(2)}, u32[]{:S(2)}) %collective-permute-start.1) | collective-permute-done | bytes 18464 | tf_op jit(solution)/shard_map/ppermute | solution.py:649
  30.5 4.9 %collective-permute-start.3 = (bf16[512,1024]{1,0:T(8,128)(2,1)}, bf16[512,1024]{1,0:T(8,128)(2,1)}, u32[]{:S(2)}, u32[]{:S(2)}) collective-permute-start(bf16[512,1024]{1,0:T(8,128)(2,1)} %bitcast.4.refs_1_.refs_5_.refs_10_), channel_id=1, source_target_pairs={{0,16},{1,17},{2,18},{3,19},{4,20},{5,21},{6,22},{7,23},{8,24},{9,... | collective-permute-start | bytes 3145736 | tf_op jit(solution)/shard_map/ppermute | solution.py:895
  35.5 2.0 collective-permute-start.6
  41.9 7.0 %project.1 = (bf16[512,1024]{1,0:T(8,128)(2,1)S(1)}, bf16[512,1024]{1,0:T(8,128)(2,1)S(1)}, bf16[512,512]{1,0:T(8,128)(2,1)S(1)}, bf16[512,512]{1,0:T(8,128)(2,1)S(1)}) custom-call(s32[2]{0:T(128)S(1)} %pad_add_fusion.refs_0_, bf16[512,1024]{1,0:T(8,128)(2,1)} %bitcast.4.refs_1_.refs_5_.refs_10_, f32[1,1024]{1,0:T(1,128)S(1)} %get-tuple-element.146.refs_2_.refs_11_, ...), custom_call_target="tpu_custom_call" | custom-call | flops 90000000 | bytes 10000 | tf_op jit(solution)/shard_map/project/pallas_call | solution.py:60
  48.9 2.3 convolution_convert_fusion.refs_0_
  51.2 6.5 %collective-permute-done.3.refs_1_ = bf16[512,1024]{1,0:T(8,128)(2,1)} collective-permute-done((bf16[512,1024]{1,0:T(8,128)(2,1)}, bf16[512,1024]{1,0:T(8,128)(2,1)}, u32[]{:S(2)}, u32[]{:S(2)}) %collective-permute-start.3) | collective-permute-done | bytes 1048608 | tf_op jit(solution)/shard_map/ppermute | solution.py:895
  59.4 11.8 %attend.1 = (bf16[512,1024]{1,0:T(8,128)(2,1)S(1)}, f32[8,8,512]{2,1,0:T(8,128)S(1)}) custom-call(s32[1]{0:T(128)} %bitcast.refs_0_, s32[1]{0:T(128)S(6)} %copy.69.refs_1_, bf16[512,1024]{1,0:T(8,128)(2,1)S(1)} %get-tuple-element.153.refs_2_, bf16[512,512]{1,0:T(8,128)(2,1)S(1)} %get-tuple-element.154.refs_11_.refs_3_, ...), custom_call_target="tpu_custom_call" | custom-call | flops 90000000 | bytes 10000 | tf_op jit(solution)/shard_map/attend/pallas_call | solution.py:60
  71.4 11.2 %collective-permute-start.7 = (bf16[512,128]{1,0:T(8,128)(2,1)S(1)}, bf16[512,128]{1,0:T(8,128)(2,1)S(1)}, u32[]{:S(2)}, u32[]{:S(2)}) collective-permute-start(bf16[512,128]{1,0:T(8,128)(2,1)S(1)} %convert_element_type.57), channel_id=1, source_target_pairs={{0,16},{1,17},{2,18},{3,19},{4,20},{5,21},{6,22},{7,23},{8,24},{9,... | collective-permute-start | bytes 393224 | tf_op jit(solution)/shard_map/ppermute | solution.py:649
  83.3 10.4 %collective-permute-done.7 = bf16[512,128]{1,0:T(8,128)(2,1)S(1)} collective-permute-done((bf16[512,128]{1,0:T(8,128)(2,1)S(1)}, bf16[512,128]{1,0:T(8,128)(2,1)S(1)}, u32[]{:S(2)}, u32[]{:S(2)}) %collective-permute-start.7) | collective-permute-done | bytes 131104 | tf_op jit(solution)/shard_map/ppermute | solution.py:649
  94.4 3.9 output.1
  99.7 2.5 collective-permute-start.8
  102.2 33.8 %experts.4 = (bf16[4,512,1536]{2,1,0:T(8,128)(2,1)}, bf16[4,512,1536]{2,1,0:T(8,128)(2,1)}, f32[512,1024]{1,0:T(8,128)}, f32[512,1024]{1,0:T(8,128)}, f32[512,12...) custom-call(s32[1]{0:T(128)} %bitcast.refs_0_, ...), custom_call_target="tpu_custom_call" | custom-call | flops 28800000000 | bytes 3200000 | tf_op jit(solution)/shard_map/experts/pallas_call | solution.py:60
  136.1 35.2 %experts.5 = (bf16[4,512,1536]{2,1,0:T(8,128)(2,1)}, bf16[4,512,1536]{2,1,0:T(8,128)(2,1)}, f32[512,1024]{1,0:T(8,128)}, f32[512,1024]{1,0:T(8,128)}, f32[512,12...) custom-call(s32[1]{0:T(128)} %bitcast.refs_0_, ...), custom_call_target="tpu_custom_call" | custom-call | flops 28800000000 | bytes 3200000 | tf_op jit(solution)/shard_map/experts/pallas_call | solution.py:60
  171.3 31.3 %experts.6 = (bf16[4,512,1536]{2,1,0:T(8,128)(2,1)}, bf16[4,512,1536]{2,1,0:T(8,128)(2,1)}, bf16[512,1152]{1,0:T(8,128)(2,1)}, bf16[512,1024]{1,0:T(8,128)(2,1)}) custom-call(s32[1]{0:T(128)} %bitcast.refs_0_, bf16[512,1024]{1,0:T(8,128)(2,1)} %collective-permute-done.8.refs_1_, bf16[512,1024]{1,0:T(8,128)(2,1)} %collective-permute-done.6.refs_2_, ...), custom_call_target="tpu_custom_call" | custom-call | flops 28800000000 | bytes 3200000 | tf_op jit(solution)/shard_map/experts/pallas_call | solution.py:60
  202.7 2.8 copy-done.15
  206.7 5.7 %split_apart.2 = (bf16[2,256,1536]{2,1,0:T(8,128)(2,1)S(1)}, bf16[2,256,1536]{2,1,0:T(8,128)(2,1)}, bf16[2,256,1536]{2,1,0:T(8,128)(2,1)S(1)}, bf16[2,256,1536]{2,1,0:T(8,128)(2,1)}) custom-call(bf16[4,512,1536]{2,1,0:T(8,128)(2,1)S(1)} %copy-done.15, bf16[4,512,1536]{2,1,0:T(8,128)(2,1)} %collective-permute-done.9.refs_1_, bf16[512,1024]{1,0:T(8,128)(2,1)S(1)} %copy-done.46), custom_call_target="tpu_custom_call" | custom-call | flops 90000000 | bytes 10000 | tf_op jit(solution)/shard_map/split_apart/pallas_call | solution.py:60
  215.7 33.0 %experts.7 = (bf16[4,512,1536]{2,1,0:T(8,128)(2,1)}, bf16[4,512,1536]{2,1,0:T(8,128)(2,1)}, f32[512,1024]{1,0:T(8,128)}, f32[512,1024]{1,0:T(8,128)}, f32[512,128]{1,0:T(8,128)}) custom-call(s32[1]{0:T(128)} %bitcast.refs_0_, bf16[512,1024]{1,0:T(8,128)(2,1)} %get-tuple-element.169.refs_1_, bf16[512,1024]{1,0:T(8,128)(2,1)} %bitcast.29, ...), custom_call_target="tpu_custom_call" | custom-call | flops 28800000000 | bytes 3200000 | tf_op jit(solution)/shard_map/experts/pallas_call | solution.py:60
  248.8 3.2 collective-permute-done.13.refs_1_
  254.4 1.9 split.14
  256.4 2.6 split.15
  259.1 1.9 copy-done.68
  261.0 4.5 middle.1
  265.6 2.5 split_apart.3
  273.9 11.2 %attend_back.2 = (bf16[512,512]{1,0:T(8,128)(2,1)S(1)}, f32[2,512,256]{2,1,0:T(8,128)S(1)}, bf16[2,512,256]{2,1,0:T(8,128)(2,1)S(1)}) custom-call(s32[1]{0:T(128)} %bitcast.refs_0_, s32[1]{0:T(128)S(6)} %copy.69.refs_1_, bf16[512,1024]{1,0:T(8,128)(2,1)S(1)} %copy-done.1, bf16[512,512]{1,0:T(8,128)(2,1)S(1)} %copy-done.6, bf16[512,512]{1,0:T(8,128)(2,1)S(1)} %copy-done.17, ...), custom_call_target="tpu_custom_call" | custom-call | flops 90000000 | bytes 10000 | tf_op jit(solution)/shard_map/attend_back/pallas_call | solution.py:60
  285.1 8.9 %collective-permute-done.11.refs_3_ = bf16[512,1024]{1,0:T(8,128)(2,1)S(1)} collective-permute-done((bf16[512,1024]{1,0:T(8,128)(2,1)S(1)}, bf16[512,1024]{1,0:T(8,128)(2,1)S(1)}, u32[]{:S(2)}, u32[]{:S(2)}) %collective-permute-start.11) | collective-permute-done | bytes 1048608 | tf_op jit(solution)/shard_map/ppermute | solution.py:649
  295.3 25.7 %collective-permute-done.16.refs_1_ = bf16[2,128,1536]{2,1,0:T(8,128)(2,1)S(1)} collective-permute-done((bf16[2,128,1536]{2,1,0:T(8,128)(2,1)S(1)}, bf16[2,128,1536]{2,1,0:T(8,128)(2,1)S(1)}, u32[]{:S(2)}, u32[]{:S(2)}) %collective-permute-start.16) | collective-permute-done | bytes 786464 | tf_op jit(solution)/shard_map/ppermute | solution.py:649
  321.4 11.5 %attend_back.3 = (bf16[512,512]{1,0:T(8,128)(2,1)S(1)}, f32[2,512,256]{2,1,0:T(8,128)S(1)}, bf16[2,512,256]{2,1,0:T(8,128)(2,1)S(1)}) custom-call(s32[1]{0:T(128)} %bitcast.refs_0_, s32[1]{0:T(128)S(6)} %copy.69.refs_1_, bf16[512,1024]{1,0:T(8,128)(2,1)S(1)} %copy-done.1, bf16[512,512]{1,0:T(8,128)(2,1)S(1)} %copy-done.6, bf16[512,512]{1,0:T(8,128)(2,1)S(1)} %copy-done.17, ...), custom_call_target="tpu_custom_call" | custom-call | flops 90000000 | bytes 10000 | tf_op jit(solution)/shard_map/attend_back/pallas_call | solution.py:60
  335.8 4.3 weight_grads.2
  341.7 2.8 collective-permute-done.21
  345.0 16.7 %collective-permute-done.20.refs_3_ = bf16[2,512,256]{2,1,0:T(8,128)(2,1)S(1)} collective-permute-done((bf16[2,512,256]{2,1,0:T(8,128)(2,1)S(1)}, bf16[2,512,256]{2,1,0:T(8,128)(2,1)S(1)}, u32[]{:S(2)}, u32[]{:S(2)}) %collective-permute-start.20) | collective-permute-done | bytes 524320 | tf_op jit(solution)/shard_map/ppermute | solution.py:940
  363.5 2.6 collective-permute-start.23
  369.2 23.7 %collective-permute-done.22.refs_1_ = bf16[2,64,1536]{2,1,0:T(8,128)(2,1)S(1)} collective-permute-done((bf16[2,64,1536]{2,1,0:T(8,128)(2,1)S(1)}, bf16[2,64,1536]{2,1,0:T(8,128)(2,1)S(1)}, u32[]{:S(2)}, u32[]{:S(2)}) %collective-permute-start.22) | collective-permute-done | bytes 393248 | tf_op jit(solution)/shard_map/ppermute | solution.py:649
  394.5 6.5 %collective-permute-done.23.refs_3_ = bf16[2,64,1536]{2,1,0:T(8,128)(2,1)S(1)} collective-permute-done((bf16[2,64,1536]{2,1,0:T(8,128)(2,1)S(1)}, bf16[2,64,1536]{2,1,0:T(8,128)(2,1)S(1)}, u32[]{:S(2)}, u32[]{:S(2)}) %collective-permute-start.23) | collective-permute-done | bytes 393248 | tf_op jit(solution)/shard_map/ppermute | solution.py:649
  401.0 3.0 collective-permute-start.26
  404.8 5.3 %input_grads.1.refs_2_ = f32[512,1024]{1,0:T(8,128)} custom-call(s32[2]{0:T(128)S(1)} %pad_add_fusion.refs_0_, bf16[512,512]{1,0:T(8,128)(2,1)S(1)} %get-tuple-element.211.refs_2_.refs_1_, bf16[512,512]{1,0:T(8,128)(2,1)S(1)} %get-tuple-element.216.refs_2_.refs_1_, bf16[512,512]{1,0:T(8,128)(2,1)S(1)} %get-tuple-element.227.refs_2_.refs_3_, ...), custom_call_target="tpu_custom_call" | custom-call | flops 90000000 | bytes 10000 | tf_op jit(solution)/shard_map/input_grads/pallas_call | solution.py:60
  412.4 3.0 collective-permute-start.40
  415.4 13.3 %collective-permute-done.25.refs_2_ = bf16[1,128,2176]{2,1,0:T(8,128)(2,1)S(1)} collective-permute-done((bf16[1,128,2176]{2,1,0:T(8,128)(2,1)S(1)}, bf16[1,128,2176]{2,1,0:T(8,128)(2,1)S(1)}, u32[]{:S(2)}, u32[]{:S(2)}) %collective-permute-start.25) | collective-permute-done | bytes 557088 | tf_op jit(solution)/shard_map/ppermute | solution.py:649
  428.7 13.9 %collective-permute-done.26.refs_3_ = bf16[1,128,2176]{2,1,0:T(8,128)(2,1)S(1)} collective-permute-done((bf16[1,128,2176]{2,1,0:T(8,128)(2,1)S(1)}, bf16[1,128,2176]{2,1,0:T(8,128)(2,1)S(1)}, u32[]{:S(2)}, u32[]{:S(2)}) %collective-permute-start.26) | collective-permute-done | bytes 557088 | tf_op jit(solution)/shard_map/ppermute | solution.py:649
  443.5 8.9 %collective-permute-done.33.refs_1_ = bf16[1,128,1024]{2,1,0:T(8,128)(2,1)S(1)} collective-permute-done((bf16[1,128,1024]{2,1,0:T(8,128)(2,1)S(1)}, bf16[1,128,1024]{2,1,0:T(8,128)(2,1)S(1)}, u32[]{:S(2)}, u32[]{:S(2)}) %collective-permute-start.33) | collective-permute-done | bytes 262176 | tf_op jit(solution)/shard_map/ppermute | solution.py:649
  452.4 3.7 collective-permute-done.35.refs_3_
  463.4 1.8 collective-permute-start.36
  467.8 3.2 fusion.2
  471.1 2.3 collective-permute-done.38.refs_7_
  473.5 1.9 finish_attention.1
  478.7 3.0 finish_experts.1
  (271 shorter events, 64.4 us)
Async XLA Ops:
  4.1 25.7 %collective-permute-start = (bf16[256,2048]{1,0:T(8,128)(2,1)}, bf16[256,2048]{1,0:T(8,128)(2,1)S(1)}, u32[]{:S(2)}, u32[]{:S(2)}) collective-permute-start(bf16[256,2048]{1,0:T(8,128)(2,1)} %pad_maximum_fusion), channel_id=1, source_target_pairs={{0,16},{1,17},{2,18},{3,19},{4,20},{5,21},{6,22},{7,23},{8,24},{9,... | collective-permute-start | bytes 3145736 | tf_op jit(solution)/shard_map/ppermute | solution.py:649
  5.6 24.1 %collective-permute-start.1 = (bf16[18,512]{1,0:T(8,128)(2,1)S(1)}, bf16[18,512]{1,0:T(8,128)(2,1)S(1)}, u32[]{:S(2)}, u32[]{:S(2)}) collective-permute-start(bf16[18,512]{1,0:T(8,128)(2,1)S(1)} %pad_maximum_fusion.3), channel_id=1, source_target_pairs={{0,16},{1,17},{2,18},{3,19},{4,20},{5,21},{6,22},{7,23},{8,24},{9,... | collective-permute-start | bytes 55304 | tf_op jit(solution)/shard_map/ppermute | solution.py:649
  30.5 8.9 %collective-permute-start.4 = (bf16[256,2048]{1,0:T(8,128)(2,1)S(1)}, bf16[256,2048]{1,0:T(8,128)(2,1)S(1)}, u32[]{:S(2)}, u32[]{:S(2)}) collective-permute-start(bf16[256,2048]{1,0:T(8,128)(2,1)S(1)} %collective-permute-done.refs_4_.refs_7_.refs_10_.refs_8_), channel_id=1, source_target_pairs={{0,1},{1,0},{2,3},{3,2},{4,5},{5,4},{6,7},{7,6},{8,9},{9,8},{10,11... | collective-permute-start | bytes 3145736 | tf_op jit(solution)/shard_map/ppermute | solution.py:649
  30.5 27.2 %collective-permute-start.3 = (bf16[512,1024]{1,0:T(8,128)(2,1)}, bf16[512,1024]{1,0:T(8,128)(2,1)}, u32[]{:S(2)}, u32[]{:S(2)}) collective-permute-start(bf16[512,1024]{1,0:T(8,128)(2,1)} %bitcast.4.refs_1_.refs_5_.refs_10_), channel_id=1, source_target_pairs={{0,16},{1,17},{2,18},{3,19},{4,20},{5,21},{6,22},{7,23},{8,24},{9,... | collective-permute-start | bytes 3145736 | tf_op jit(solution)/shard_map/ppermute | solution.py:895
  35.4 35.8 %collective-permute-start.2 = (bf16[256,1024]{1,0:T(8,128)(2,1)}, bf16[256,1024]{1,0:T(8,128)(2,1)}, u32[]{:S(2)}, u32[]{:S(2)}) collective-permute-start(bf16[256,1024]{1,0:T(8,128)(2,1)} %constant_dynamic-slice_fusion.3), channel_id=1, source_target_pairs={{0,16},{1,17},{2,18},{3,19},{4,20},{5,21},{6,22},{7,23},{8,24},{9,... | collective-permute-start | bytes 1572872 | tf_op jit(solution)/shard_map/ppermute | solution.py:649
  35.5 64.2 %collective-permute-start.6 = (bf16[512,1024]{1,0:T(8,128)(2,1)}, bf16[512,1024]{1,0:T(8,128)(2,1)}, u32[]{:S(2)}, u32[]{:S(2)}) collective-permute-start(bf16[512,1024]{1,0:T(8,128)(2,1)} %bitcast.27), channel_id=1, source_target_pairs={{0,16},{1,17},{2,18},{3,19},{4,20},{5,21},{6,22},{7,23},{8,24},{9,... | collective-permute-start | bytes 3145736 | tf_op jit(solution)/shard_map/ppermute | solution.py:649
  71.3 23.2 %collective-permute-start.5 = (bf16[256,1024]{1,0:T(8,128)(2,1)}, bf16[256,1024]{1,0:T(8,128)(2,1)S(1)}, u32[]{:S(2)}, u32[]{:S(2)}) collective-permute-start(bf16[256,1024]{1,0:T(8,128)(2,1)} %collective-permute-done.2.refs_3_.refs_10_), channel_id=1, source_target_pairs={{0,1},{1,0},{2,3},{3,2},{4,5},{5,4},{6,7},{7,6},{8,9},{9,8},{10,11... | collective-permute-start | bytes 1572872 | tf_op jit(solution)/shard_map/ppermute | solution.py:649
  71.4 22.3 %collective-permute-start.7 = (bf16[512,128]{1,0:T(8,128)(2,1)S(1)}, bf16[512,128]{1,0:T(8,128)(2,1)S(1)}, u32[]{:S(2)}, u32[]{:S(2)}) collective-permute-start(bf16[512,128]{1,0:T(8,128)(2,1)S(1)} %convert_element_type.57), channel_id=1, source_target_pairs={{0,16},{1,17},{2,18},{3,19},{4,20},{5,21},{6,22},{7,23},{8,24},{9,... | collective-permute-start | bytes 393224 | tf_op jit(solution)/shard_map/ppermute | solution.py:649
  99.7 36.3 %collective-permute-start.8 = (bf16[512,1024]{1,0:T(8,128)(2,1)}, bf16[512,1024]{1,0:T(8,128)(2,1)}, u32[]{:S(2)}, u32[]{:S(2)}) collective-permute-start(bf16[512,1024]{1,0:T(8,128)(2,1)} %get-tuple-element.169.refs_1_), channel_id=1, source_target_pairs={{0,16},{1,17},{2,18},{3,19},{4,20},{5,21},{6,22},{7,23},{8,24},{9,... | collective-permute-start | bytes 3145736 | tf_op jit(solution)/shard_map/ppermute | solution.py:649
  171.2 31.5 %collective-permute-start.9 = (bf16[4,512,1536]{2,1,0:T(8,128)(2,1)}, bf16[4,512,1536]{2,1,0:T(8,128)(2,1)}, u32[]{:S(2)}, u32[]{:S(2)}) collective-permute-start(bf16[4,512,1536]{2,1,0:T(8,128)(2,1)} %get-tuple-element.191), channel_id=1, source_target_pairs={{0,1},{1,0},{2,3},{3,2},{4,5},{5,4},{6,7},{7,6},{8,9},{9,8},{10,11... | collective-permute-start | bytes 18874376 | tf_op jit(solution)/shard_map/ppermute | solution.py:649
  202.6 46.1 %collective-permute-start.10 = (bf16[512,1152]{1,0:T(8,128)(2,1)}, bf16[512,1152]{1,0:T(8,128)(2,1)}, u32[]{:S(2)}, u32[]{:S(2)}) collective-permute-start(bf16[512,1152]{1,0:T(8,128)(2,1)} %get-tuple-element.195), channel_id=1, source_target_pairs={{0,16},{1,17},{2,18},{3,19},{4,20},{5,21},{6,22},{7,23},{8,24},{9,... | collective-permute-start | bytes 3538952 | tf_op jit(solution)/shard_map/ppermute | solution.py:649
  214.8 41.6 %collective-permute-start.12 = (bf16[2,256,1536]{2,1,0:T(8,128)(2,1)}, bf16[2,256,1536]{2,1,0:T(8,128)(2,1)}, u32[]{:S(2)}, u32[]{:S(2)}) collective-permute-start(bf16[2,256,1536]{2,1,0:T(8,128)(2,1)} %get-tuple-element.202), channel_id=1, source_target_pairs={{0,4},{1,5},{2,6},{3,7},{4,0},{5,1},{6,2},{7,3},{8,12},{9,13},{10,... | collective-permute-start | bytes 4718600 | tf_op jit(solution)/shard_map/ppermute | solution.py:649
  215.2 36.8 %collective-permute-start.13 = (bf16[2,256,1536]{2,1,0:T(8,128)(2,1)}, bf16[2,256,1536]{2,1,0:T(8,128)(2,1)}, u32[]{:S(2)}, u32[]{:S(2)}) collective-permute-start(bf16[2,256,1536]{2,1,0:T(8,128)(2,1)} %get-tuple-element.203), channel_id=1, source_target_pairs={{0,2},{1,3},{2,0},{3,1},{4,6},{5,7},{6,4},{7,5},{8,10},{9,11},{10,... | collective-permute-start | bytes 4718600 | tf_op jit(solution)/shard_map/ppermute | solution.py:649
  248.7 16.8 %collective-permute-start.14 = (bf16[4,512,1536]{2,1,0:T(8,128)(2,1)}, bf16[4,512,1536]{2,1,0:T(8,128)(2,1)S(1)}, u32[]{:S(2)}, u32[]{:S(2)}) collective-permute-start(bf16[4,512,1536]{2,1,0:T(8,128)(2,1)} %get-tuple-element.208), channel_id=1, source_target_pairs={{0,1},{1,0},{2,3},{3,2},{4,5},{5,4},{6,7},{7,6},{8,9},{9,8},{10,11... | collective-permute-start | bytes 18874376 | tf_op jit(solution)/shard_map/ppermute | solution.py:649
  268.1 64.8 %collective-permute-start.19 = (bf16[2,256,1536]{2,1,0:T(8,128)(2,1)S(1)}, bf16[2,256,1536]{2,1,0:T(8,128)(2,1)S(1)}, u32[]{:S(2)}, u32[]{:S(2)}) collective-permute-start(bf16[2,256,1536]{2,1,0:T(8,128)(2,1)S(1)} %get-tuple-element.224), channel_id=1, source_target_pairs={{0,2},{1,3},{2,0},{3,1},{4,6},{5,7},{6,4},{7,5},{8,10},{9,11},{10,... | collective-permute-start | bytes 4718600 | tf_op jit(solution)/shard_map/ppermute | solution.py:649
  268.6 64.8 %collective-permute-start.18 = (bf16[2,256,1536]{2,1,0:T(8,128)(2,1)}, bf16[2,256,1536]{2,1,0:T(8,128)(2,1)S(1)}, u32[]{:S(2)}, u32[]{:S(2)}) collective-permute-start(bf16[2,256,1536]{2,1,0:T(8,128)(2,1)} %get-tuple-element.223), channel_id=1, source_target_pairs={{0,4},{1,5},{2,6},{3,7},{4,0},{5,1},{6,2},{7,3},{8,12},{9,13},{10,... | collective-permute-start | bytes 4718600 | tf_op jit(solution)/shard_map/ppermute | solution.py:649
  270.2 23.8 %collective-permute-start.11 = (bf16[512,1024]{1,0:T(8,128)(2,1)S(1)}, bf16[512,1024]{1,0:T(8,128)(2,1)S(1)}, u32[]{:S(2)}, u32[]{:S(2)}) collective-permute-start(bf16[512,1024]{1,0:T(8,128)(2,1)S(1)} %copy-done.47), channel_id=1, source_target_pairs={{0,16},{1,17},{2,18},{3,19},{4,20},{5,21},{6,22},{7,23},{8,24},{9,... | collective-permute-start | bytes 3145736 | tf_op jit(solution)/shard_map/ppermute | solution.py:649
  271.9 49.1 %collective-permute-start.16 = (bf16[2,128,1536]{2,1,0:T(8,128)(2,1)S(1)}, bf16[2,128,1536]{2,1,0:T(8,128)(2,1)S(1)}, u32[]{:S(2)}, u32[]{:S(2)}) collective-permute-start(bf16[2,128,1536]{2,1,0:T(8,128)(2,1)S(1)} %get-tuple-element.213), channel_id=1, source_target_pairs={{0,4},{1,5},{2,6},{3,7},{4,0},{5,1},{6,2},{7,3},{8,12},{9,13},{10,... | collective-permute-start | bytes 2359304 | tf_op jit(solution)/shard_map/ppermute | solution.py:649
  272.3 48.9 %collective-permute-start.15 = (bf16[2,128,1536]{2,1,0:T(8,128)(2,1)}, bf16[2,128,1536]{2,1,0:T(8,128)(2,1)S(1)}, u32[]{:S(2)}, u32[]{:S(2)}) collective-permute-start(bf16[2,128,1536]{2,1,0:T(8,128)(2,1)} %get-tuple-element.212), channel_id=1, source_target_pairs={{0,2},{1,3},{2,0},{3,1},{4,6},{5,7},{6,4},{7,5},{8,10},{9,11},{10,... | collective-permute-start | bytes 2359304 | tf_op jit(solution)/shard_map/ppermute | solution.py:649
  285.1 36.1 %copy-start.49 = (bf16[2,128,1536]{2,1,0:T(8,128)(2,1)S(1)}, bf16[2,128,1536]{2,1,0:T(8,128)(2,1)}, u32[]{:S(2)}) copy-start(bf16[2,128,1536]{2,1,0:T(8,128)(2,1)} %copy-done.48) | copy-start | bytes 2359300
  294.0 39.7 %collective-permute-start.17 = (bf16[2,512,256]{2,1,0:T(8,128)(2,1)S(1)}, bf16[2,512,256]{2,1,0:T(8,128)(2,1)S(1)}, u32[]{:S(2)}, u32[]{:S(2)}) collective-permute-start(bf16[2,512,256]{2,1,0:T(8,128)(2,1)S(1)} %get-tuple-element.219), channel_id=1, source_target_pairs={{16,0},{17,1},{18,2},{19,3},{20,4},{21,5},{22,6},{23,7},{24,8},{25... | collective-permute-start | bytes 1572872 | tf_op jit(solution)/shard_map/ppermute | solution.py:940
  340.1 4.4 collective-permute-start.21
  340.2 21.6 %collective-permute-start.20 = (bf16[2,512,256]{2,1,0:T(8,128)(2,1)S(1)}, bf16[2,512,256]{2,1,0:T(8,128)(2,1)S(1)}, u32[]{:S(2)}, u32[]{:S(2)}) collective-permute-start(bf16[2,512,256]{2,1,0:T(8,128)(2,1)S(1)} %get-tuple-element.229), channel_id=1, source_target_pairs={{16,0},{17,1},{18,2},{19,3},{20,4},{21,5},{22,6},{23,7},{24,8},{25... | collective-permute-start | bytes 1572872 | tf_op jit(solution)/shard_map/ppermute | solution.py:940
  361.7 43.1 %copy-start.32 = (f32[512,1024]{1,0:T(8,128)S(1)}, f32[512,1024]{1,0:T(8,128)}, u32[]{:S(2)}) copy-start(f32[512,1024]{1,0:T(8,128)} %copy-done.31) | copy-start | bytes 6291460
  363.0 41.8 %copy-start.10 = (bf16[512,1024]{1,0:T(8,128)(2,1)S(1)}, bf16[512,1024]{1,0:T(8,128)(2,1)}, u32[]{:S(2)}) copy-start(bf16[512,1024]{1,0:T(8,128)(2,1)} %refs_5_.1) | copy-start | bytes 3145732
  363.0 41.8 %copy-start.14 = (bf16[512,512]{1,0:T(8,128)(2,1)S(1)}, bf16[512,512]{1,0:T(8,128)(2,1)}, u32[]{:S(2)}) copy-start(bf16[512,512]{1,0:T(8,128)(2,1)} %refs_6_.13) | copy-start | bytes 1572868
  363.0 41.8 %copy-start.63 = (f32[1,1024]{1,0:T(1,128)S(1)}, f32[1,1024]{1,0:T(1,128)}, u32[]{:S(2)}) copy-start(f32[1,1024]{1,0:T(1,128)} %copy-done.62) | copy-start | bytes 12292
  363.1 37.9 %collective-permute-start.29 = (bf16[512,1024]{1,0:T(8,128)(2,1)S(1)}, bf16[512,1024]{1,0:T(8,128)(2,1)S(1)}, u32[]{:S(2)}, u32[]{:S(2)}) collective-permute-start(bf16[512,1024]{1,0:T(8,128)(2,1)S(1)} %get-tuple-element.244), channel_id=1, source_target_pairs={{0,1},{1,0},{2,3},{3,2},{4,5},{5,4},{6,7},{7,6},{8,9},{9,8},{10,11... | collective-permute-start | bytes 3145736 | tf_op jit(solution)/shard_map/ppermute | solution.py:649
  363.1 29.8 %collective-permute-start.22 = (bf16[2,64,1536]{2,1,0:T(8,128)(2,1)S(1)}, bf16[2,64,1536]{2,1,0:T(8,128)(2,1)S(1)}, u32[]{:S(2)}, u32[]{:S(2)}) collective-permute-start(bf16[2,64,1536]{2,1,0:T(8,128)(2,1)S(1)} %get-tuple-element.235), channel_id=1, source_target_pairs={{0,8},{1,9},{2,10},{3,11},{4,12},{5,13},{6,14},{7,15},{8,0},{9,1},... | collective-permute-start | bytes 1179656 | tf_op jit(solution)/shard_map/ppermute | solution.py:649
  363.5 37.4 %collective-permute-start.23 = (bf16[2,64,1536]{2,1,0:T(8,128)(2,1)S(1)}, bf16[2,64,1536]{2,1,0:T(8,128)(2,1)S(1)}, u32[]{:S(2)}, u32[]{:S(2)}) collective-permute-start(bf16[2,64,1536]{2,1,0:T(8,128)(2,1)S(1)} %get-tuple-element.236), channel_id=1, source_target_pairs={{0,8},{1,9},{2,10},{3,11},{4,12},{5,13},{6,14},{7,15},{8,0},{9,1},... | collective-permute-start | bytes 1179656 | tf_op jit(solution)/shard_map/ppermute | solution.py:649
  366.1 45.8 %collective-permute-start.28 = (bf16[2,128,1536]{2,1,0:T(8,128)(2,1)S(1)}, bf16[2,128,1536]{2,1,0:T(8,128)(2,1)S(1)}, u32[]{:S(2)}, u32[]{:S(2)}) collective-permute-start(bf16[2,128,1536]{2,1,0:T(8,128)(2,1)S(1)} %get-tuple-element.242), channel_id=1, source_target_pairs={{0,4},{1,5},{2,6},{3,7},{4,0},{5,1},{6,2},{7,3},{8,12},{9,13},{10,... | collective-permute-start | bytes 2359304 | tf_op jit(solution)/shard_map/ppermute | solution.py:649
  367.7 44.5 %collective-permute-start.27 = (bf16[2,128,1536]{2,1,0:T(8,128)(2,1)S(1)}, bf16[2,128,1536]{2,1,0:T(8,128)(2,1)S(1)}, u32[]{:S(2)}, u32[]{:S(2)}) collective-permute-start(bf16[2,128,1536]{2,1,0:T(8,128)(2,1)S(1)} %get-tuple-element.241), channel_id=1, source_target_pairs={{0,2},{1,3},{2,0},{3,1},{4,6},{5,7},{6,4},{7,5},{8,10},{9,11},{10,... | collective-permute-start | bytes 2359304 | tf_op jit(solution)/shard_map/ppermute | solution.py:649
  393.0 22.4 %collective-permute-start.24 = (bf16[1,128,2176]{2,1,0:T(8,128)(2,1)S(1)}, bf16[1,128,2176]{2,1,0:T(8,128)(2,1)S(1)}, u32[]{:S(2)}, u32[]{:S(2)}) collective-permute-start(bf16[1,128,2176]{2,1,0:T(8,128)(2,1)S(1)} %get-tuple-element.238), channel_id=1, source_target_pairs={{0,2},{1,3},{2,0},{3,1},{4,6},{5,7},{6,4},{7,5},{8,10},{9,11},{10,... | collective-permute-start | bytes 1671176 | tf_op jit(solution)/shard_map/ppermute | solution.py:649
  400.9 27.8 %collective-permute-start.25 = (bf16[1,128,2176]{2,1,0:T(8,128)(2,1)S(1)}, bf16[1,128,2176]{2,1,0:T(8,128)(2,1)S(1)}, u32[]{:S(2)}, u32[]{:S(2)}) collective-permute-start(bf16[1,128,2176]{2,1,0:T(8,128)(2,1)S(1)} %get-tuple-element.239), channel_id=1, source_target_pairs={{0,4},{1,5},{2,6},{3,7},{4,0},{5,1},{6,2},{7,3},{8,12},{9,13},{10,... | collective-permute-start | bytes 1671176 | tf_op jit(solution)/shard_map/ppermute | solution.py:649
  401.0 41.7 %collective-permute-start.26 = (bf16[1,128,2176]{2,1,0:T(8,128)(2,1)S(1)}, bf16[1,128,2176]{2,1,0:T(8,128)(2,1)S(1)}, u32[]{:S(2)}, u32[]{:S(2)}) collective-permute-start(bf16[1,128,2176]{2,1,0:T(8,128)(2,1)S(1)} %get-tuple-element.240), channel_id=1, source_target_pairs={{0,6},{1,7},{2,4},{3,5},{4,2},{5,3},{6,0},{7,1},{8,14},{9,15},{10,... | collective-permute-start | bytes 1671176 | tf_op jit(solution)/shard_map/ppermute | solution.py:649
  412.1 45.2 %collective-permute-start.39 = (bf16[2,64,1536]{2,1,0:T(8,128)(2,1)S(1)}, bf16[2,64,1536]{2,1,0:T(8,128)(2,1)S(1)}, u32[]{:S(2)}, u32[]{:S(2)}) collective-permute-start(bf16[2,64,1536]{2,1,0:T(8,128)(2,1)S(1)} %get-tuple-element.263), channel_id=1, source_target_pairs={{0,8},{1,9},{2,10},{3,11},{4,12},{5,13},{6,14},{7,15},{8,0},{9,1},... | collective-permute-start | bytes 1179656 | tf_op jit(solution)/shard_map/ppermute | solution.py:649
  412.4 46.6 %collective-permute-start.40 = (bf16[2,64,1536]{2,1,0:T(8,128)(2,1)S(1)}, bf16[2,64,1536]{2,1,0:T(8,128)(2,1)S(1)}, u32[]{:S(2)}, u32[]{:S(2)}) collective-permute-start(bf16[2,64,1536]{2,1,0:T(8,128)(2,1)S(1)} %get-tuple-element.264), channel_id=1, source_target_pairs={{0,8},{1,9},{2,10},{3,11},{4,12},{5,13},{6,14},{7,15},{8,0},{9,1},... | collective-permute-start | bytes 1179656 | tf_op jit(solution)/shard_map/ppermute | solution.py:649
  415.4 37.0 %collective-permute-start.33 = (bf16[1,128,1024]{2,1,0:T(8,128)(2,1)S(1)}, bf16[1,128,1024]{2,1,0:T(8,128)(2,1)S(1)}, u32[]{:S(2)}, u32[]{:S(2)}) collective-permute-start(bf16[1,128,1024]{2,1,0:T(8,128)(2,1)S(1)} %get-tuple-element.252), channel_id=1, source_target_pairs={{0,4},{1,5},{2,6},{3,7},{4,0},{5,1},{6,2},{7,3},{8,12},{9,13},{10,... | collective-permute-start | bytes 786440 | tf_op jit(solution)/shard_map/ppermute | solution.py:649
  428.7 23.7 %collective-permute-start.34 = (bf16[1,128,1024]{2,1,0:T(8,128)(2,1)S(1)}, bf16[1,128,1024]{2,1,0:T(8,128)(2,1)S(1)}, u32[]{:S(2)}, u32[]{:S(2)}) collective-permute-start(bf16[1,128,1024]{2,1,0:T(8,128)(2,1)S(1)} %get-tuple-element.253), channel_id=1, source_target_pairs={{0,16},{1,17},{2,18},{3,19},{4,20},{5,21},{6,22},{7,23},{8,24},{9,... | collective-permute-start | bytes 786440 | tf_op jit(solution)/shard_map/ppermute | solution.py:649
  442.6 13.4 %collective-permute-start.35 = (bf16[1,128,1024]{2,1,0:T(8,128)(2,1)S(1)}, bf16[1,128,1024]{2,1,0:T(8,128)(2,1)S(1)}, u32[]{:S(2)}, u32[]{:S(2)}) collective-permute-start(bf16[1,128,1024]{2,1,0:T(8,128)(2,1)S(1)} %get-tuple-element.254), channel_id=1, source_target_pairs={{0,20},{1,21},{2,22},{3,23},{4,16},{5,17},{6,18},{7,19},{8,28},{9,... | collective-permute-start | bytes 786440 | tf_op jit(solution)/shard_map/ppermute | solution.py:649
  452.4 11.0 %collective-permute-start.30 = (bf16[1,32,2176]{2,1,0:T(8,128)(2,1)}, bf16[1,32,2176]{2,1,0:T(8,128)(2,1)}, u32[]{:S(2)}, u32[]{:S(2)}) collective-permute-start(bf16[1,32,2176]{2,1,0:T(8,128)(2,1)} %get-tuple-element.249), channel_id=1, source_target_pairs={{0,8},{1,9},{2,10},{3,11},{4,12},{5,13},{6,14},{7,15},{8,0},{9,1},... | collective-permute-start | bytes 417800 | tf_op jit(solution)/shard_map/ppermute | solution.py:649
  452.4 12.8 %collective-permute-start.31 = (bf16[1,32,2176]{2,1,0:T(8,128)(2,1)}, bf16[1,32,2176]{2,1,0:T(8,128)(2,1)}, u32[]{:S(2)}, u32[]{:S(2)}) collective-permute-start(bf16[1,32,2176]{2,1,0:T(8,128)(2,1)} %get-tuple-element.250), channel_id=1, source_target_pairs={{0,16},{1,17},{2,18},{3,19},{4,20},{5,21},{6,22},{7,23},{8,24},{9,... | collective-permute-start | bytes 417800 | tf_op jit(solution)/shard_map/ppermute | solution.py:649
  456.1 10.9 %collective-permute-start.32 = (bf16[1,32,2176]{2,1,0:T(8,128)(2,1)}, bf16[1,32,2176]{2,1,0:T(8,128)(2,1)}, u32[]{:S(2)}, u32[]{:S(2)}) collective-permute-start(bf16[1,32,2176]{2,1,0:T(8,128)(2,1)} %get-tuple-element.251), channel_id=1, source_target_pairs={{0,24},{1,25},{2,26},{3,27},{4,28},{5,29},{6,30},{7,31},{8,16},{9,... | collective-permute-start | bytes 417800 | tf_op jit(solution)/shard_map/ppermute | solution.py:649
  457.4 20.7 %collective-permute-start.41 = (bf16[4,32,1536]{2,1,0:T(8,128)(2,1)}, bf16[4,32,1536]{2,1,0:T(8,128)(2,1)}, u32[]{:S(2)}, u32[]{:S(2)}) collective-permute-start(bf16[4,32,1536]{2,1,0:T(8,128)(2,1)} %get-tuple-element.273), channel_id=1, source_target_pairs={{0,16},{1,17},{2,18},{3,19},{4,20},{5,21},{6,22},{7,23},{8,24},{9,... | collective-permute-start | bytes 1179656 | tf_op jit(solution)/shard_map/ppermute | solution.py:649
  460.7 18.1 %collective-permute-start.42 = (bf16[4,32,1536]{2,1,0:T(8,128)(2,1)}, bf16[4,32,1536]{2,1,0:T(8,128)(2,1)}, u32[]{:S(2)}, u32[]{:S(2)}) collective-permute-start(bf16[4,32,1536]{2,1,0:T(8,128)(2,1)} %get-tuple-element.274), channel_id=1, source_target_pairs={{0,16},{1,17},{2,18},{3,19},{4,20},{5,21},{6,22},{7,23},{8,24},{9,... | collective-permute-start | bytes 1179656 | tf_op jit(solution)/shard_map/ppermute | solution.py:649
  463.4 7.7 %collective-permute-start.36 = (bf16[1,32,1024]{2,1,0:T(8,128)(2,1)}, bf16[1,32,1024]{2,1,0:T(8,128)(2,1)S(1)}, u32[]{:S(2)}, u32[]{:S(2)}) collective-permute-start(bf16[1,32,1024]{2,1,0:T(8,128)(2,1)} %copy-done.67), channel_id=1, source_target_pairs={{0,8},{1,9},{2,10},{3,11},{4,12},{5,13},{6,14},{7,15},{8,0},{9,1},... | collective-permute-start | bytes 196616 | tf_op jit(solution)/shard_map/ppermute | solution.py:649
  465.2 5.8 %collective-permute-start.37 = (bf16[1,32,1024]{2,1,0:T(8,128)(2,1)}, bf16[1,32,1024]{2,1,0:T(8,128)(2,1)S(1)}, u32[]{:S(2)}, u32[]{:S(2)}) collective-permute-start(bf16[1,32,1024]{2,1,0:T(8,128)(2,1)} %copy-done.66), channel_id=1, source_target_pairs={{0,2},{1,3},{2,0},{3,1},{4,6},{5,7},{6,4},{7,5},{8,10},{9,11},{10,... | collective-permute-start | bytes 196616 | tf_op jit(solution)/shard_map/ppermute | solution.py:649
  467.0 6.5 %collective-permute-start.38 = (bf16[1,32,1024]{2,1,0:T(8,128)(2,1)}, bf16[1,32,1024]{2,1,0:T(8,128)(2,1)S(1)}, u32[]{:S(2)}, u32[]{:S(2)}) collective-permute-start(bf16[1,32,1024]{2,1,0:T(8,128)(2,1)} %copy-done.65), channel_id=1, source_target_pairs={{0,10},{1,11},{2,8},{3,9},{4,14},{5,15},{6,12},{7,13},{8,2},{9,3},... | collective-permute-start | bytes 196616 | tf_op jit(solution)/shard_map/ppermute | solution.py:649
  (75 other events, 576.0 us)
